TPU v7x, 32 devices: a whole 2x2x4 slice. The times are simulated.
32 devices in a mesh: groups: 2 (over x), tm: 8 (over z, y), rows: 2 (over core).
Axes of the slice: x: 2, y: 2, z: 4, core: 2. Of those that a mesh axis runs over, the one named last changes fastest.
Arguments:
- frames_in: bfloat16 [4, 8, 16, 256, 128], P('groups', 'tm', 'rows'), parts along dimension 0, may hold values from -12 to 12
- gain_one: float32 [128], replicated, may hold values from 0.25 to 1.75
- norm_bias_one: float32 [128], replicated, may hold values from -3 to 3
- kernel_one: bfloat16 [3, 3, 3, 128, 128], replicated, may hold values from -0.109375 to 0.109375
- bias_one: float32 [128], replicated, may hold values from -2 to 2
- gain_two: float32 [128], replicated, may hold values from 0.25 to 1.75
- norm_bias_two: float32 [128], replicated, may hold values from -3 to 3
- kernel_two: bfloat16 [3, 3, 3, 128, 128], replicated, may hold values from -0.109375 to 0.109375
- bias_two: float32 [128], replicated, may hold values from -2 to 2
- kernel_down: bfloat16 [3, 3, 128, 128], replicated, may hold values from -0.1875 to 0.1875
- bias_down: float32 [128], replicated, may hold values from -2 to 2
Outputs:
- features_down: bfloat16 [4, 8, 8, 128, 128], P('groups', 'tm', 'rows'), parts along dimension 0
There are 2 independent parts, one for each index of `groups`. A program takes and returns all parts, laid end to end along the dimension named above; an argument that names none is the same for every part. Nothing has to cross between parts.
All inputs are finite; a program needn't handle non-finite values.
Results may differ from a plain program's by a relative error of at most 0.0095.
Values may be sent and summed in bfloat16 or wider, within the bound.
No kernel may reach another device: no remote copies, remote signals or barrier semaphores. Data moves between devices by JAX's collectives and lax.ppermute only.
A program may use at most 128 MiB of HBM per device.

v0:
```python
import functools

import jax
import jax.numpy as jnp
from jax import lax
from jax.experimental import pallas as pl
from jax.experimental.pallas import tpu as pltpu
from jax.sharding import PartitionSpec as P


G = 32
EPSILON = 1e-06
F32 = jnp.float32
VMEM_LIMIT = 16 << 20
BF16 = jnp.bfloat16


def norm_params(totals, gain, bias, cells):
    channels = totals.shape[1]
    size = channels // G
    left = lax.broadcasted_iota(jnp.int32, (channels, channels), 0) // size
    right = lax.broadcasted_iota(jnp.int32, (channels, channels), 1) // size
    same = (left == right).astype(F32)
    grouped = jnp.dot(totals, same, precision=lax.Precision.HIGHEST, preferred_element_type=F32)
    grouped = grouped / (cells * size)
    mean = grouped[0:1]
    inverse = lax.rsqrt(grouped[1:2] - mean * mean + EPSILON)
    return mean, inverse * gain, bias


def keep_params(ref, params):
    for k, value in enumerate(params):
        ref[k : k + 1] = value


def kept_params(ref):
    return ref[0:1], ref[1:2], ref[2:3]


def fill_row(stack, r, values, params):
    mean, scale, bias = params
    width, channels = values.shape
    half = 0.5 * ((values.astype(F32) - mean) * scale + bias)
    normed = half + half * jnp.tanh(half)
    column = lax.broadcasted_iota(jnp.int32, (width, channels), 0)
    before = jnp.where(column == 0, 0.0, pltpu.roll(normed, 1, 0))
    after = jnp.where(column == width - 1, 0.0, pltpu.roll(normed, width - 1, 0))
    stack[r, :, 0:channels] = before.astype(BF16)
    stack[r, :, channels : 2 * channels] = normed.astype(BF16)
    stack[r, :, 2 * channels :] = after.astype(BF16)


def fill_frame(stack, values, params):
    for r, value in enumerate(values):
        fill_row(stack, r, value(), params)


def close_stack(stack):
    last = stack.shape[0] - 1
    stack[last] = jnp.zeros(stack.shape[1:], BF16)


def taps(stack, weights, start, count):
    rows = [
        jnp.concatenate([stack[r], stack[r + 1], stack[r + 2]], axis=1)
        for r in range(start, start + count)
    ]
    return jnp.dot(jnp.concatenate(rows, axis=0), weights, preferred_element_type=F32)


def steps(first, last):
    total = last - first
    size = 3 if total % 3 == 0 else 2
    return [(r, min(size, last - r)) for r in range(first, last, size)]


def reader(ref, r):
    return lambda: ref[r]


def rows_of(*refs):
    return [reader(ref, r) for ref in refs for r in range(ref.shape[0])]


def choose(flags, part, own, mate):
    def read():
        return jnp.where(flags[1] == 1, jnp.where(flags[0] == 0, own(), mate()), part())

    return read


def chosen(flags, parts, owns, mates):
    return [choose(flags, p, o, m) for p, o, m in zip(parts, owns, mates)]


def place_kernel(flags, x_ref, *parts):
    height = x_ref.shape[1]
    side, band = flags[0], flags[2]
    clips = [side] * height + [1 - side] * height
    rows = list(range(height)) * 2
    for part in parts:
        for k in range(part.shape[0]):
            r = rows.pop(0)
            part[k] = x_ref[clips.pop(0), jnp.where(band == 0, height - 1 - r, r)]


def lay_weights(out, k_ref, slot, band):
    channels = k_ref.shape[-1]
    for f in range(out.shape[1] // channels):
        frame = slot - f
        known = jnp.logical_and(frame >= 0, frame <= 2)
        frame = jnp.clip(frame, 0, 2)
        for a in range(3):
            tap = jnp.where(band == 0, 2 - a, a)
            for b in range(3):
                k = (3 * a + b) * channels
                block = jnp.where(known, k_ref[tap, b, frame], jnp.zeros((), BF16))
                out[k : k + channels, f * channels : (f + 1) * channels] = block


def sums_kernel(flags, own, other, out_ref):
    width, channels = own[0].shape[1:]
    for c, rows in enumerate((rows_of(*own), rows_of(*other))):
        total = jnp.zeros((8, channels), F32)
        square = jnp.zeros((8, channels), F32)
        for read in rows:
            v = read().astype(F32).reshape(width // 8, 8, channels)
            total += jnp.sum(v, axis=0)
            square += jnp.sum(v * v, axis=0)
        out_ref[c, 0:1] = jnp.sum(total, axis=0, keepdims=True)
        out_ref[c, 1:2] = jnp.sum(square, axis=0, keepdims=True)
        out_ref[c, 2:8] = jnp.zeros((6, channels), F32)


def own_kernel(cells, flags, own, t_ref, g_ref, c_ref, k_ref, acc_ref, stack, w_ref):
    height, width, _ = acc_ref.shape
    lay_weights(w_ref, k_ref, 2 + flags[0], flags[2])
    params = norm_params(t_ref[0], g_ref[...], c_ref[...], cells)
    fill_frame(stack, rows_of(*own), params)
    close_stack(stack)
    for start, count in steps(0, height):
        part = taps(stack, w_ref[...], start, count)
        acc_ref[start : start + count] = part.reshape(count, width, -1)


def mates_kernel(cells, flags, own, mate, past, to_ref, tm_ref, tp_ref, tq_ref, g_ref, c_ref, k_ref, in_ref, acc_ref, last_ref, edge_ref, xm, xp, wm, wp):
    height, width, _ = acc_ref.shape
    side = flags[0]
    first, even = flags[1] == 1, side == 0
    lay_weights(wm, k_ref, 3 - side, flags[2])
    lay_weights(wp, k_ref, side, flags[2])
    params = norm_params(tm_ref[1], g_ref[...], c_ref[...], cells)
    fill_frame(xm, rows_of(*mate), params)
    close_stack(xm)
    start_totals = jnp.where(even, to_ref[0], tm_ref[1])
    totals = jnp.where(first, start_totals, tp_ref[0])
    params = norm_params(totals, g_ref[...], c_ref[...], cells)
    fill_frame(xp, chosen(flags, rows_of(*past), rows_of(*own), rows_of(*mate)), params)
    close_stack(xp)
    for start, count in steps(0, height):
        part = taps(xm, wm[...], start, count) + taps(xp, wp[...], start, count)
        acc_ref[start : start + count] = in_ref[start : start + count] + part.reshape(count, width, -1)
    totals = jnp.where(first, start_totals, tq_ref[1])
    keep_params(last_ref, norm_params(totals, g_ref[...], c_ref[...], cells))
    edge_ref[0] = own[0][0]
    edge_ref[1] = mate[0][0]


def hidden_rows(stack, w_ref, in_ref, bias_ref, first, a_ref, b_ref, sum_ref):
    rows, width, channels = a_ref.shape
    both = 2 * channels
    bias = jnp.concatenate([bias_ref[...], bias_ref[...]], axis=1)
    total = jnp.zeros((8, both), F32)
    square = jnp.zeros((8, both), F32)
    for start, count in steps(0, rows):
        part = taps(stack, w_ref[...], start, count).reshape(count, width, both)
        begin = first + start
        hidden = (in_ref[begin : begin + count] + part + bias).astype(BF16)
        a_ref[start : start + count] = hidden[:, :, :channels]
        b_ref[start : start + count] = hidden[:, :, channels:]
        wide = hidden.astype(F32).reshape(count * width // 8, 8, both)
        total += jnp.sum(wide, axis=0)
        square += jnp.sum(wide * wide, axis=0)
    total = jnp.sum(total, axis=0, keepdims=True)
    square = jnp.sum(square, axis=0, keepdims=True)
    for k in range(2):
        sum_ref[k, 0:1] = total[:, k * channels : (k + 1) * channels]
        sum_ref[k, 1:2] = square[:, k * channels : (k + 1) * channels]
        sum_ref[k, 2:8] = jnp.zeros((6, channels), F32)


def near_kernel(cells, flags, own, mate, past, n_ref, k_ref, in_ref, bias_ref, a_ref, b_ref, edge_ref, sum_ref, stack, w_ref):
    lay_weights(w_ref, k_ref, 1 - flags[0], flags[2])
    edges = own[0]
    owns = [reader(edges, 0)] + rows_of(*own[1:])
    mates = [reader(edges, 1)] + rows_of(*mate)
    fill_frame(stack, chosen(flags, rows_of(*past), owns, mates), kept_params(n_ref))
    hidden_rows(stack, w_ref, in_ref, bias_ref, 0, a_ref, b_ref, sum_ref)
    edge_ref[0] = a_ref[0:2]
    edge_ref[1] = b_ref[0:2]


def far_kernel(cells, flags, own, mate, past, n_ref, k_ref, in_ref, bias_ref, near_ref, part_ref, a_ref, b_ref, c_ref, sum_ref, stack, held, w_ref):
    lay_weights(w_ref, k_ref, 1 - flags[0], flags[2])
    height = in_ref.shape[0]
    rows, early = b_ref.shape[0], near_ref.shape[0]
    values = chosen(flags, rows_of(*past), rows_of(*own), rows_of(*mate))
    fill_frame(stack, values[height - rows - 1 :], kept_params(n_ref))
    close_stack(stack)
    hidden_rows(stack, w_ref, in_ref, bias_ref, height - rows, held, b_ref, sum_ref)
    sum_ref[...] += part_ref[...]
    whole = a_ref.shape[0]
    a_ref[0:early] = near_ref[...]
    a_ref[early:] = held[0 : whole - early]
    c_ref[...] = held[whole - early :]


def halves(edge, k, near, far):
    return [lambda: edge[k, 1], lambda: edge[k, 0]] + rows_of(near, far)


def local_kernel(cells, flags, a1, a2, b1, b2, e_ref, t_ref, g_ref, c_ref, k_ref, acc_ref, xa, xb, wa, wb):
    out_rows, width, _ = acc_ref.shape
    lay_weights(wa, k_ref, 2, flags[2])
    lay_weights(wb, k_ref, 3, flags[2])
    for k, (stack, near, far) in enumerate(((xa, a1, a2), (xb, b1, b2))):
        params = norm_params(t_ref[k], g_ref[...], c_ref[...], cells)
        fill_frame(stack, halves(e_ref, k, near, far), params)
        close_stack(stack)
    for start, count in steps(0, out_rows):
        part = taps(xa, wa[...], start, count) + taps(xb, wb[...], start, count)
        acc_ref[start : start + count] = part.reshape(count, width, -1)


def either(flags, first, other):
    return lambda: jnp.where(flags[1] == 1, first(), other())


def residual_row(raw, branch):
    return (raw.astype(F32) + branch).astype(BF16)


def put_row(res, r, value):
    res[r, 0 : value.shape[0], :] = value.astype(F32)


def down_rows(flags, res, wd_ref, bd_ref, first, last):
    half = (res.shape[1] - 8) // 2
    band = flags[2]
    rows = []
    for i in range(first, last):
        cols = [
            res[2 * i + a + band, pl.ds(b, half, stride=2), :].astype(BF16)
            for a in range(3)
            for b in range(3)
        ]
        rows.append(jnp.concatenate(cols, axis=1))
    out = jnp.dot(jnp.concatenate(rows, axis=0), wd_ref[...], preferred_element_type=F32)
    out = (out + bd_ref[...]).astype(BF16)
    return out.reshape(last - first, half, -1)


def raw_rows(even, first, second):
    return [lambda f=f, s=s: jnp.where(even, f(), s()) for f, s in zip(first, second)]


def second_kernel(cells, flags, b1, b2, eb_ref, tp_ref, a1, a2, e_ref, t_ref, g_ref, c_ref, k_ref, in_ref, bias_ref, own, mate, wd_ref, bd_ref, acc_ref, out_ref, last_ref, wl_ref, stack, res, w_ref):
    out_rows, width, channels = acc_ref.shape
    height = out_rows - 1
    lay_weights(w_ref, k_ref, 1, flags[2])
    lay_weights(wl_ref, k_ref, 0, flags[2])
    params = norm_params(jnp.where(flags[1] == 1, t_ref[0], tp_ref[1]), g_ref[...], c_ref[...], cells)
    values = [
        either(flags, f, o) for f, o in zip(halves(e_ref, 0, a1, a2), halves(eb_ref, 0, b1, b2))
    ]
    fill_frame(stack, values, params)
    close_stack(stack)
    raw = raw_rows(flags[0] == 0, rows_of(*mate), rows_of(*own))
    bias = jnp.concatenate([bias_ref[...], bias_ref[...]], axis=1)
    res[:, width:, :] = jnp.zeros((res.shape[0], res.shape[1] - width, channels), F32)
    res[out_rows] = jnp.zeros(res.shape[1:], F32)
    for start, count in steps(0, out_rows):
        part = taps(stack, w_ref[...], start, count).reshape(count, width, 2 * channels)
        branch = in_ref[start : start + count] + part + bias
        acc_ref[start : start + count] = branch[:, :, :channels]
        for k in range(count):
            put_row(res, start + k, residual_row(raw[start + k](), branch[k, :, channels:]))
    out_ref[...] = down_rows(flags, res, wd_ref, bd_ref, 0, height // 2)
    params = norm_params(jnp.where(flags[1] == 1, t_ref[0], tp_ref[0]), g_ref[...], c_ref[...], cells)
    keep_params(last_ref, params)


def first_near_kernel(cells, flags, p1, ep_ref, n_ref, a1, e_ref, w_ref, in_ref, own, mate, out_ref, stack):
    rows, width, channels = out_ref.shape
    firsts = [lambda: e_ref[0, 1], lambda: e_ref[0, 0]] + rows_of(a1)
    others = [lambda: ep_ref[0, 1], lambda: ep_ref[0, 0]] + rows_of(p1)
    fill_frame(stack, [either(flags, f, o) for f, o in zip(firsts, others)], kept_params(n_ref))
    raw = raw_rows(flags[0] == 0, rows_of(*own), rows_of(*mate))
    for start, count in steps(0, rows):
        part = taps(stack, w_ref[...], start, count).reshape(count, width, channels)
        branch = in_ref[start : start + count] + part
        for k in range(count):
            out_ref[start + k] = residual_row(raw[start + k](), branch[k])


def first_far_kernel(cells, flags, p1, p2, n_ref, a1, a2, w_ref, in_ref, near_ref, other_ref, own, mate, wd_ref, bd_ref, send_ref, keep_ref, stack, res):
    out_rows, width, channels = in_ref.shape
    height = out_rows - 1
    done = near_ref.shape[0]
    even = flags[0] == 0
    values = [either(flags, f, o) for f, o in zip(rows_of(a1, a2), rows_of(p1, p2))]
    fill_frame(stack, values[done - 2 :], kept_params(n_ref))
    close_stack(stack)
    raw = raw_rows(even, rows_of(*own), rows_of(*mate))
    res[:, width:, :] = jnp.zeros((res.shape[0], res.shape[1] - width, channels), F32)
    res[out_rows] = jnp.zeros(res.shape[1:], F32)
    for r in range(done):
        put_row(res, r, near_ref[r])
    for start, count in steps(0, out_rows - done):
        part = taps(stack, w_ref[...], start, count).reshape(count, width, channels)
        branch = in_ref[done + start : done + start + count] + part
        for k in range(count):
            r = done + start + k
            put_row(res, r, residual_row(raw[r - 1](), branch[k]))
    out = down_rows(flags, res, wd_ref, bd_ref, 0, height // 2)
    rows = height // 2
    for i in range(rows):
        row = jnp.where(flags[2] == 0, rows - 1 - i, i)
        send_ref[row] = jnp.where(even, other_ref[i], out[i])
        keep_ref[row] = jnp.where(even, out[i], other_ref[i])


def call(body, out_shape, scratch, flags, *groups, flops=0):
    vmem = pl.BlockSpec(memory_space=pltpu.VMEM)
    several = isinstance(out_shape, (list, tuple))
    args = [a for g in groups for a in (g if isinstance(g, tuple) else (g,))]
    moved = sum(a.size * a.dtype.itemsize for a in args)

    def kernel(flags_ref, *refs):
        rest = list(refs)
        given = [
            tuple(rest.pop(0) for _ in g) if isinstance(g, tuple) else rest.pop(0) for g in groups
        ]
        body(flags_ref, *given, *rest)

    return pl.pallas_call(
        kernel,
        out_shape=out_shape,
        in_specs=[pl.BlockSpec(memory_space=pltpu.SMEM)] + [vmem] * len(args),
        out_specs=[vmem] * len(out_shape) if several else vmem,
        scratch_shapes=scratch,
        cost_estimate=pl.CostEstimate(flops=flops, bytes_accessed=moved, transcendentals=0),
        compiler_params=pltpu.CompilerParams(vmem_limit_bytes=VMEM_LIMIT),
    )(flags, *args)


def turned(value, band):
    return jnp.where(band == 0, value[::-1], value)


def local(
    frames_in,
    gain_one,
    norm_bias_one,
    kernel_one,
    bias_one,
    gain_two,
    norm_bias_two,
    kernel_two,
    bias_two,
    kernel_down,
    bias_down,
):
    x = frames_in[:, 0]
    clips, height, width, channels = x.shape
    count = lax.axis_size("tm")
    bands = lax.axis_size("rows")
    assert clips == 2 and bands == 2 and count % 2 == 0 and height % 8 == 0
    cells = height * bands * width
    near = 3 * height // 8
    tail = height // TAIL
    position = lax.axis_index("tm")
    band = lax.axis_index("rows")
    side = position % 2
    flags = jnp.stack([side, (position < 2).astype(jnp.int32), band]).astype(jnp.int32)
    swap = [(i, i ^ 1) for i in range(count)]
    across = [(0, 1), (1, 0)]

    def onward(name, turn):
        wrap = name not in OPEN
        pairs = [(i, (i ^ turn) + 2) for i in range(count)]
        return [(i, j % count) for i, j in pairs if wrap or j < count]

    def swapped(v):
        return lax.ppermute(v, "tm", swap)

    def later(v, name):
        return lax.ppermute(v, "tm", onward(name, 0))

    def crossed(v, name):
        return lax.ppermute(v, "tm", onward(name, 1))

    def beside(v):
        return lax.ppermute(v, "rows", across)

    def row(v):
        return v.reshape(1, -1)

    def stack(rows):
        return [pltpu.VMEM((rows, width, 3 * channels), BF16)]

    def laid(n):
        return [pltpu.VMEM((9 * channels, n * channels), BF16)]

    def flops(rows, slots):
        return 2 * rows * width * 9 * channels * 2 * channels * slots

    def shape(*dims, dtype=BF16):
        return jax.ShapeDtypeStruct(dims, dtype)

    def kernel(body, *rest, **options):
        return call(functools.partial(body, cells), *rest, **options)

    split = near + 1
    sizes = (1, height - 1, 1, split - 1, height - split)
    parts = call(place_kernel, [shape(n, width, channels) for n in sizes], [], flags, x)
    own, other = tuple(parts[:2]), tuple(parts[2:])
    past = later(own[0], "own_on0"), later(own[1], "own_on1")
    mate = tuple(swapped(v) for v in other)
    partial = call(sums_kernel, shape(2, 8, channels, dtype=F32), [], flags, own, other)
    totals = partial + beside(partial)
    own_on_total = later(totals, "own_sums")
    cross_total = crossed(totals, "cross_sums")
    mate_total = swapped(totals)
    own = (beside(own[0]), *own)
    mate_on = tuple(later(v, f"mate_on{k}") for k, v in enumerate(mate))
    mate = (beside(mate[0]), *mate)
    past = (beside(past[0]), *past)

    norm_one = (row(gain_one), row(norm_bias_one))
    sums = shape(2, 8, channels, dtype=F32)
    params = shape(8, channels, dtype=F32)
    acc_shape = shape(height, width, 2 * channels, dtype=F32)
    acc = kernel(
        own_kernel,
        acc_shape,
        stack(height + 2) + laid(2),
        flags,
        own,
        totals,
        *norm_one,
        kernel_one,
        flops=flops(height, 1),
    )
    acc, cross_params, fall_edges = kernel(
        mates_kernel,
        [acc_shape, params, shape(2, width, channels)],
        stack(height + 2) + stack(height + 2) + laid(2) + laid(2),
        flags,
        own,
        mate,
        past,
        totals,
        mate_total,
        own_on_total,
        cross_total,
        *norm_one,
        kernel_one,
        acc,
        flops=flops(height, 2),
    )
    cross_edge = beside(mate_on[0])
    bias = row(bias_one)
    part = shape(near, width, channels)
    rest = shape(height - near, width, channels)
    early = shape(height - tail, width, channels)
    a_near, b1, edges, sums_near = kernel(
        near_kernel,
        [part, part, shape(2, 2, width, channels), sums],
        stack(near + 2) + laid(2),
        flags,
        (fall_edges, *own[1:]),
        mate[1:3],
        (cross_edge, *mate_on[:2]),
        cross_params,
        kernel_one,
        acc,
        bias,
        flops=flops(near, 1),
    )
    b1_on = later(b1, "b_on1")
    a1, b2, a2, partial = kernel(
        far_kernel,
        [early, rest, shape(tail, width, channels), sums],
        stack(height - near + 2) + [pltpu.VMEM(rest.shape, BF16)] + laid(2),
        flags,
        own[1:],
        mate[1:],
        mate_on,
        cross_params,
        kernel_one,
        acc,
        bias,
        a_near,
        sums_near,
        flops=flops(height - near, 1),
    )
    b2_on = later(b2, "b_on2")
    totals = partial + beside(partial)
    totals_on = later(totals, "hsums_on")
    a1_on = later(a1, "a_on1")
    a2_on = later(a2, "a_on2")
    edges = beside(edges)

    norm_two = (row(gain_two), row(norm_bias_two))
    acc = kernel(
        local_kernel,
        shape(height + 1, width, 2 * channels, dtype=F32),
        stack(height + 3) + stack(height + 3) + laid(2) + laid(2),
        flags,
        a1,
        a2,
        b1,
        b2,
        edges,
        totals,
        *norm_two,
        kernel_two,
        flops=flops(height + 1, 2),
    )
    down = turned(kernel_down, band).reshape(-1, channels)
    residual = [pltpu.VMEM((height + 2, width + 8, channels), F32)]
    b_edge = beside(b1_on[None, :2])
    out_shape = shape(height // 2, width // 2, channels)
    acc, out_b, a_params, w_a_on = kernel(
        second_kernel,
        [shape(height + 1, width, channels, dtype=F32), out_shape, params, shape(9 * channels, channels)],
        stack(height + 3) + residual + laid(2),
        flags,
        b1_on,
        b2_on,
        b_edge,
        totals_on,
        a1,
        a2,
        edges,
        totals,
        *norm_two,
        kernel_two,
        acc,
        row(bias_two),
        own,
        mate,
        down,
        row(bias_down),
        flops=flops(height + 1, 1),
    )
    a_edge = beside(a1_on[None, :2])
    ready = height - tail
    first_near = kernel(
        first_near_kernel,
        shape(ready, width, channels),
        stack(ready + 2),
        flags,
        a1_on,
        a_edge,
        a_params,
        a1,
        edges,
        w_a_on,
        acc,
        own,
        mate[:3],
        flops=flops(ready, 1),
    )
    sent, kept = kernel(
        first_far_kernel,
        [out_shape, out_shape],
        stack(tail + 3) + residual,
        flags,
        a1_on,
        a2_on,
        a_params,
        a1,
        a2,
        w_a_on,
        acc,
        first_near,
        out_b,
        own[1:],
        mate[1:],
        down,
        row(bias_down),
        flops=flops(tail + 1, 1),
    )
    received = swapped(sent)
    even = side == 0
    result = jnp.where(even, jnp.stack([kept, received]), jnp.stack([received, kept]))
    return result[:, None]


OPEN = ('b_on1', 'b_on2', 'a_on1', 'a_on2', 'hsums_on')
TAIL = 2


def solution(mesh):
    placed = (P("groups", "tm", "rows", None, None),) + (P(),) * 10
    return jax.shard_map(
        local,
        mesh=mesh,
        in_specs=placed,
        out_specs=P("groups", "tm", "rows", None, None),
        check_vma=False,
    )
```

profile of v0, /device:TPU:0, one launch (start us, length us, event | category | flops | bytes accessed | tf_op | source)
XLA Modules:
  0.0 92.0 jit_solution(13509080162968377159)
XLA Ops:
  0.0 0.1 pad_add_fusion.flags_ref
  0.1 1.3 %copy-done.1 = bf16[2,1,8,256,128]{4,3,2,1,0:T(8,128)(2,1)S(1)} copy-done((bf16[2,1,8,256,128]{4,3,2,1,0:T(8,128)(2,1)S(1)}, bf16[2,1,8,256,128]{4,3,2,1,0:T(8,128)(2,1)}, u32[]{:S(2)}) %copy-start.1) | copy-done | bytes 1048600
  1.4 0.6 shard_map.109
  2.0 3.1 %collective-permute-start.10 = (bf16[7,256,128]{2,1,0:T(8,128)(2,1)S(1)}, bf16[7,256,128]{2,1,0:T(8,128)(2,1)S(1)}, u32[]{:S(2)}, u32[]{:S(2)}) collective-permute-start(bf16[7,256,128]{2,1,0:T(8,128)(2,1)S(1)} %get-tuple-element.28.refs_1_.refs_2_.refs_15_.refs_9_.refs_10_), channel_id=1, source_target_pairs={{0,4},{2,6},{4,8},{6,10},{8,12},{10,14},{12,0},{14,2},{1,5},{3,7},... | collective-permute-start | bytes 1376264 | tf_op jit(solution)/shard_map/ppermute | solution.py:398
  5.1 1.5 %collective-permute-start.2 = (bf16[4,256,128]{2,1,0:T(8,128)(2,1)S(1)}, bf16[4,256,128]{2,1,0:T(8,128)(2,1)S(1)}, u32[]{:S(2)}, u32[]{:S(2)}) collective-permute-start(bf16[4,256,128]{2,1,0:T(8,128)(2,1)S(1)} %get-tuple-element.31.refs_4_), channel_id=1, source_target_pairs={{0,2},{2,0},{4,6},{6,4},{8,10},{10,8},{12,14},{14,12},{1,3},{3,1},... | collective-permute-start | bytes 786440 | tf_op jit(solution)/shard_map/ppermute | solution.py:395
  6.6 0.0 collective-permute-start.6
  6.6 0.5 collective-permute-start
  7.1 0.8 shard_map.110
  8.0 0.3 collective-permute-start.11
  8.3 0.9 %collective-permute-done.11 = f32[2,8,128]{2,1,0:T(8,128)S(1)} collective-permute-done((f32[2,8,128]{2,1,0:T(8,128)S(1)}, f32[2,8,128]{2,1,0:T(8,128)S(1)}, u32[]{:S(2)}, u32[]{:S(2)}) %collective-permute-start.11) | collective-permute-done | bytes 8224 | tf_op jit(solution)/shard_map/ppermute | solution.py:404
  9.2 1.5 %collective-permute-start.12 = (f32[2,8,128]{2,1,0:T(8,128)S(1)}, f32[2,8,128]{2,1,0:T(8,128)S(1)}, u32[]{:S(2)}, u32[]{:S(2)}) collective-permute-start(f32[2,8,128]{2,1,0:T(8,128)S(1)} %add.11.refs_3_.refs_10_), channel_id=1, source_target_pairs={{0,2},{2,0},{4,6},{6,4},{8,10},{10,8},{12,14},{14,12},{1,3},{3,1},... | collective-permute-start | bytes 24584 | tf_op jit(solution)/shard_map/ppermute | solution.py:395
  10.7 3.7 %collective-permute-done.12.refs_11_ = f32[2,8,128]{2,1,0:T(8,128)S(1)} collective-permute-done((f32[2,8,128]{2,1,0:T(8,128)S(1)}, f32[2,8,128]{2,1,0:T(8,128)S(1)}, u32[]{:S(2)}, u32[]{:S(2)}) %collective-permute-start.12) | collective-permute-done | bytes 8224 | tf_op jit(solution)/shard_map/ppermute | solution.py:395
  14.4 1.6 %collective-permute-start.13 = (f32[2,8,128]{2,1,0:T(8,128)S(1)}, f32[2,8,128]{2,1,0:T(8,128)S(1)}, u32[]{:S(2)}, u32[]{:S(2)}) collective-permute-start(f32[2,8,128]{2,1,0:T(8,128)S(1)} %add.11.refs_3_.refs_10_), channel_id=1, source_target_pairs={{0,4},{2,6},{4,8},{6,10},{8,12},{10,14},{12,0},{14,2},{1,5},{3,7},... | collective-permute-start | bytes 24584 | tf_op jit(solution)/shard_map/ppermute | solution.py:398
  16.0 3.9 %collective-permute-done.13.refs_12_ = f32[2,8,128]{2,1,0:T(8,128)S(1)} collective-permute-done((f32[2,8,128]{2,1,0:T(8,128)S(1)}, f32[2,8,128]{2,1,0:T(8,128)S(1)}, u32[]{:S(2)}, u32[]{:S(2)}) %collective-permute-start.13) | collective-permute-done | bytes 8224 | tf_op jit(solution)/shard_map/ppermute | solution.py:398
  19.9 0.7 collective-permute-start.14
  20.6 5.7 %collective-permute-done.14.refs_13_ = f32[2,8,128]{2,1,0:T(8,128)S(1)} collective-permute-done((f32[2,8,128]{2,1,0:T(8,128)S(1)}, f32[2,8,128]{2,1,0:T(8,128)S(1)}, u32[]{:S(2)}, u32[]{:S(2)}) %collective-permute-start.14) | collective-permute-done | bytes 8224 | tf_op jit(solution)/shard_map/ppermute | solution.py:401
  26.4 1.5 %collective-permute-start.1 = (bf16[3,256,128]{2,1,0:T(8,128)(2,1)S(1)}, bf16[3,256,128]{2,1,0:T(8,128)(2,1)S(1)}, u32[]{:S(2)}, u32[]{:S(2)}) collective-permute-start(bf16[3,256,128]{2,1,0:T(8,128)(2,1)S(1)} %get-tuple-element.30.refs_3_), channel_id=1, source_target_pairs={{0,2},{2,0},{4,6},{6,4},{8,10},{10,8},{12,14},{14,12},{1,3},{3,1},... | collective-permute-start | bytes 589832 | tf_op jit(solution)/shard_map/ppermute | solution.py:395
  27.9 0.0 collective-permute-done.6.refs_0_.refs_13_.refs_7_
  27.9 0.0 collective-permute-start.8
  27.9 0.0 collective-permute-done.refs_4_.refs_3_.refs_2_.refs_17_.refs_11_
  27.9 0.1 collective-permute-start.7
  28.0 6.3 %collective-permute-done.8.refs_8_ = bf16[1,256,128]{2,1,0:T(8,128)(2,1)S(1)} collective-permute-done((bf16[1,256,128]{2,1,0:T(8,128)(2,1)S(1)}, bf16[1,256,128]{2,1,0:T(8,128)(2,1)S(1)}, u32[]{:S(2)}, u32[]{:S(2)}) %collective-permute-start.8) | collective-permute-done | bytes 65568 | tf_op jit(solution)/shard_map/ppermute | solution.py:398
  34.3 0.0 collective-permute-start.3
  34.3 0.0 collective-permute-done.7.refs_3_.refs_16_.refs_10_
  34.3 0.0 collective-permute-start.9
  34.3 2.6 %shard_map.111.refs_17_ = f32[8,256,256]{2,1,0:T(8,128)S(1)} custom-call(s32[3]{0:T(128)S(1)} %pad_add_fusion.flags_ref, bf16[1,256,128]{2,1,0:T(8,128)(2,1)S(1)} %collective-permute-done.6.refs_0_.refs_13_.refs_7_, bf16[1,256,128]{2,1,0:T(8,128)(2,1)S(1)} %get-tuple-element.27.refs_0_.refs_1_.refs_14_.refs_8_.refs_9_, ...), custom_call_target="tpu_custom_call" | custom-call | flops 1207959552 | bytes 1483776 | tf_op jit(solution)/shard_map/pallas_call | solution.py:346
  36.9 0.0 copy-start.4
  37.0 3.4 %collective-permute-done.3.refs_6_.refs_5_ = bf16[1,256,128]{2,1,0:T(8,128)(2,1)S(1)} collective-permute-done((bf16[1,256,128]{2,1,0:T(8,128)(2,1)S(1)}, bf16[1,256,128]{2,1,0:T(8,128)(2,1)S(1)}, u32[]{:S(2)}, u32[]{:S(2)}) %collective-permute-start.3) | collective-permute-done | bytes 65568 | tf_op jit(solution)/shard_map/ppermute | solution.py:398
  40.4 0.0 collective-permute-start.15
  40.4 0.0 collective-permute-done.1.refs_5_.refs_4_.refs_3_.refs_18_.refs_12_
  40.4 0.0 collective-permute-start.4
  40.4 0.1 collective-permute-start.5
  40.5 0.0 collective-permute-done.9.refs_7_
  40.5 0.0 collective-permute-done.10.refs_9_
  40.5 4.2 %shard_map.112 = (f32[8,256,256]{2,1,0:T(8,128)S(1)}, f32[8,128]{1,0:T(8,128)S(1)}, bf16[2,256,128]{2,1,0:T(8,128)(2,1)S(1)}) custom-call(s32[3]{0:T(128)S(1)} %pad_add_fusion.flags_ref, bf16[1,256,128]{2,1,0:T(8,128)(2,1)S(1)} %collective-permute-done.6.refs_0_.refs_13_.refs_7_, ...), custom_call_target="tpu_custom_call" | custom-call | flops 2415919104 | bytes 4785152 | tf_op jit(solution)/shard_map/pallas_call | solution.py:346
  44.6 5.3 %collective-permute-done.4.refs_7_.refs_6_ = bf16[3,256,128]{2,1,0:T(8,128)(2,1)S(1)} collective-permute-done((bf16[3,256,128]{2,1,0:T(8,128)(2,1)S(1)}, bf16[3,256,128]{2,1,0:T(8,128)(2,1)S(1)}, u32[]{:S(2)}, u32[]{:S(2)}) %collective-permute-start.4) | collective-permute-done | bytes 196640 | tf_op jit(solution)/shard_map/ppermute | solution.py:398
  49.9 1.5 %shard_map.113 = (bf16[3,256,128]{2,1,0:T(8,128)(2,1)S(1)}, bf16[3,256,128]{2,1,0:T(8,128)(2,1)S(1)}, bf16[2,2,256,128]{3,2,1,0:T(8,128)(2,1)S(1)}, f32[2,8,128]{2,1,0:T(8,128)S(1)}) custom-call(s32[3]{0:T(128)S(1)} %pad_add_fusion.flags_ref, bf16[2,256,128]{2,1,0:T(8,128)(2,1)S(1)} %get-tuple-element.34.refs_0_, ...), custom_call_target="tpu_custom_call" | custom-call | flops 452984832 | bytes 4231680 | tf_op jit(solution)/shard_map/pallas_call | solution.py:346
  51.5 1.3 %collective-permute-start.18 = (bf16[3,256,128]{2,1,0:T(8,128)(2,1)S(1)}, bf16[3,256,128]{2,1,0:T(8,128)(2,1)S(1)}, u32[]{:S(2)}, u32[]{:S(2)}) collective-permute-start(bf16[3,256,128]{2,1,0:T(8,128)(2,1)S(1)} %get-tuple-element.39.refs_2_), channel_id=1, source_target_pairs={{0,4},{2,6},{4,8},{6,10},{8,12},{10,14},{1,5},{3,7},{5,9},{7,11},{... | collective-permute-start | bytes 589832 | tf_op jit(solution)/shard_map/ppermute | solution.py:398
  52.8 2.3 %collective-permute-done.5.refs_7_ = bf16[4,256,128]{2,1,0:T(8,128)(2,1)S(1)} collective-permute-done((bf16[4,256,128]{2,1,0:T(8,128)(2,1)S(1)}, bf16[4,256,128]{2,1,0:T(8,128)(2,1)S(1)}, u32[]{:S(2)}, u32[]{:S(2)}) %collective-permute-start.5) | collective-permute-done | bytes 262176 | tf_op jit(solution)/shard_map/ppermute | solution.py:398
  55.1 2.0 %shard_map.114 = (bf16[4,256,128]{2,1,0:T(8,128)(2,1)S(1)}, bf16[5,256,128]{2,1,0:T(8,128)(2,1)S(1)}, bf16[4,256,128]{2,1,0:T(8,128)(2,1)S(1)}, f32[2,8,128]{2,1,0:T(8,128)S(1)}) custom-call(s32[3]{0:T(128)S(1)} %pad_add_fusion.flags_ref, bf16[1,256,128]{2,1,0:T(8,128)(2,1)S(1)} %get-tuple-element.27.refs_0_.refs_1_.refs_14_.refs_8_.refs_9_, ...), custom_call_target="tpu_custom_call" | custom-call | flops 754974720 | bytes 4764160 | tf_op jit(solution)/shard_map/pallas_call | solution.py:346
  57.1 0.1 collective-permute-start.21
  57.2 1.3 %collective-permute-start.16 = (bf16[4,256,128]{2,1,0:T(8,128)(2,1)S(1)}, bf16[4,256,128]{2,1,0:T(8,128)(2,1)S(1)}, u32[]{:S(2)}, u32[]{:S(2)}) collective-permute-start(bf16[4,256,128]{2,1,0:T(8,128)(2,1)S(1)} %get-tuple-element.37.refs_0_.refs_4_.refs_3_), channel_id=1, source_target_pairs={{0,4},{2,6},{4,8},{6,10},{8,12},{10,14},{1,5},{3,7},{5,9},{7,11},{... | collective-permute-start | bytes 786440 | tf_op jit(solution)/shard_map/ppermute | solution.py:398
  58.5 0.1 reverse_select_fusion
  58.6 0.6 collective-permute-start.23
  59.1 1.3 %collective-permute-start.19 = (bf16[5,256,128]{2,1,0:T(8,128)(2,1)S(1)}, bf16[5,256,128]{2,1,0:T(8,128)(2,1)S(1)}, u32[]{:S(2)}, u32[]{:S(2)}) collective-permute-start(bf16[5,256,128]{2,1,0:T(8,128)(2,1)S(1)} %get-tuple-element.40.refs_3_), channel_id=1, source_target_pairs={{0,4},{2,6},{4,8},{6,10},{8,12},{10,14},{1,5},{3,7},{5,9},{7,11},{... | collective-permute-start | bytes 983048 | tf_op jit(solution)/shard_map/ppermute | solution.py:398
  60.5 0.0 collective-permute-done.21
  60.5 3.5 %collective-permute-start.17 = (bf16[4,256,128]{2,1,0:T(8,128)(2,1)S(1)}, bf16[4,256,128]{2,1,0:T(8,128)(2,1)S(1)}, u32[]{:S(2)}, u32[]{:S(2)}) collective-permute-start(bf16[4,256,128]{2,1,0:T(8,128)(2,1)S(1)} %get-tuple-element.38.refs_1_.refs_5_.refs_4_), channel_id=1, source_target_pairs={{0,4},{2,6},{4,8},{6,10},{8,12},{10,14},{1,5},{3,7},{5,9},{7,11},{... | collective-permute-start | bytes 786440 | tf_op jit(solution)/shard_map/ppermute | solution.py:398
  64.0 0.0 collective-permute-done.18.refs_0_
  64.0 2.1 %collective-permute-start.22 = (f32[2,8,128]{2,1,0:T(8,128)S(1)}, f32[2,8,128]{2,1,0:T(8,128)S(1)}, u32[]{:S(2)}, u32[]{:S(2)}) collective-permute-start(f32[2,8,128]{2,1,0:T(8,128)S(1)} %add.12.refs_5_.refs_7_), channel_id=1, source_target_pairs={{0,4},{2,6},{4,8},{6,10},{8,12},{10,14},{1,5},{3,7},{5,9},{7,11},{... | collective-permute-start | bytes 24584 | tf_op jit(solution)/shard_map/ppermute | solution.py:398
  66.1 0.0 collective-permute-done.16.refs_0_
  66.1 0.1 collective-permute-start.20
  66.2 0.0 collective-permute-done.23.refs_4_.refs_6_
  66.2 0.6 collective-permute-start.24
  66.8 0.0 copy-start.7
  66.8 4.4 %shard_map.115.refs_11_ = f32[9,256,256]{2,1,0:T(8,128)S(1)} custom-call(s32[3]{0:T(128)S(1)} %pad_add_fusion.flags_ref, bf16[4,256,128]{2,1,0:T(8,128)(2,1)S(1)} %get-tuple-element.37.refs_0_.refs_4_.refs_3_, bf16[4,256,128]{2,1,0:T(8,128)(2,1)S(1)} %get-tuple-element.38.refs_1_.refs_5_.refs_4_, bf16[3,256,128]{2,1,0:T(8,128)(2,1)S(1)} %get-tuple-element.39.refs_2_, ...), custom_call_target="tpu_custom_call" | custom-call | flops 2717908992 | bytes 2204672 | tf_op jit(solution)/shard_map/pallas_call | solution.py:346
  71.2 6.6 %collective-permute-done.22.refs_3_ = f32[2,8,128]{2,1,0:T(8,128)S(1)} collective-permute-done((f32[2,8,128]{2,1,0:T(8,128)S(1)}, f32[2,8,128]{2,1,0:T(8,128)S(1)}, u32[]{:S(2)}, u32[]{:S(2)}) %collective-permute-start.22) | collective-permute-done | bytes 8224 | tf_op jit(solution)/shard_map/ppermute | solution.py:398
  77.8 0.0 collective-permute-done.20.refs_2_
  77.8 4.0 %shard_map.116 = (f32[9,256,128]{2,1,0:T(8,128)S(1)}, bf16[4,128,128]{2,1,0:T(8,128)(2,1)S(1)}, f32[8,128]{1,0:T(8,128)S(1)}, bf16[1152,128]{1,0:T(8,128)(2,1)S(1)}) custom-call(s32[3]{0:T(128)S(1)} %pad_add_fusion.flags_ref, bf16[3,256,128]{2,1,0:T(8,128)(2,1)S(1)} %collective-permute-done.18.refs_0_, ...), custom_call_target="tpu_custom_call" | custom-call | flops 1358954496 | bytes 6178816 | tf_op jit(solution)/shard_map/pallas_call | solution.py:346
  81.8 0.0 collective-permute-done.24.refs_1_
  81.8 1.5 %shard_map.117.refs_7_ = bf16[4,256,128]{2,1,0:T(8,128)(2,1)S(1)} custom-call(s32[3]{0:T(128)S(1)} %pad_add_fusion.flags_ref, bf16[4,256,128]{2,1,0:T(8,128)(2,1)S(1)} %collective-permute-done.16.refs_0_, bf16[1,2,256,128]{3,2,1,0:T(8,128)(2,1)S(1)} %collective-permute-done.24.refs_1_, f32[8,128]{1,0:T(8,128)S(1)} %get-tuple-element.43.refs_2_, ...), custom_call_target="tpu_custom_call" | custom-call | flops 603979776 | bytes 3313664 | tf_op jit(solution)/shard_map/pallas_call | solution.py:346
  83.3 2.5 %shard_map.118 = (bf16[4,128,128]{2,1,0:T(8,128)(2,1)S(1)}, bf16[4,128,128]{2,1,0:T(8,128)(2,1)S(1)}) custom-call(s32[3]{0:T(128)S(1)} %pad_add_fusion.flags_ref, bf16[4,256,128]{2,1,0:T(8,128)(2,1)S(1)} %collective-permute-done.16.refs_0_, bf16[4,256,128]{2,1,0:T(8,128)(2,1)S(1)} %collective-permute-done.17.refs_1_, ...), custom_call_target="tpu_custom_call" | custom-call | flops 754974720 | bytes 4264448 | tf_op jit(solution)/shard_map/pallas_call | solution.py:346
  85.9 0.6 collective-permute-start.25
  86.5 4.8 %collective-permute-done.25 = bf16[4,128,128]{2,1,0:T(8,128)(2,1)S(1)} collective-permute-done((bf16[4,128,128]{2,1,0:T(8,128)(2,1)S(1)}, bf16[4,128,128]{2,1,0:T(8,128)(2,1)S(1)}, u32[]{:S(2)}, u32[]{:S(2)}) %collective-permute-start.25) | collective-permute-done | bytes 131104 | tf_op jit(solution)/shard_map/ppermute | solution.py:395
  91.3 0.7 maximum_select_fusion
  (27 shorter events, 0.1 us)
Async XLA Ops:
  0.0 34.3 %copy-start = (bf16[3,3,3,128,128]{4,3,2,1,0:T(8,128)(2,1)S(1)}, bf16[3,3,3,128,128]{4,3,2,1,0:T(8,128)(2,1)}, u32[]{:S(2)}) copy-start(bf16[3,3,3,128,128]{4,3,2,1,0:T(8,128)(2,1)} %refs_9_.3) | copy-start | bytes 2654212
  0.1 1.3 %copy-start.1 = (bf16[2,1,8,256,128]{4,3,2,1,0:T(8,128)(2,1)S(1)}, bf16[2,1,8,256,128]{4,3,2,1,0:T(8,128)(2,1)}, u32[]{:S(2)}) copy-start(bf16[2,1,8,256,128]{4,3,2,1,0:T(8,128)(2,1)} %param.11) | copy-start | bytes 3145732
  1.4 33.0 %copy-start.8 = (f32[128]{0:T(128)S(1)}, f32[128]{0:T(128)}, u32[]{:S(2)}) copy-start(f32[128]{0:T(128)} %param.12) | copy-start | bytes 1540
  1.4 33.0 %copy-start.9 = (f32[128]{0:T(128)S(1)}, f32[128]{0:T(128)}, u32[]{:S(2)}) copy-start(f32[128]{0:T(128)} %param.13) | copy-start | bytes 1540
  2.0 38.5 %collective-permute-start.10 = (bf16[7,256,128]{2,1,0:T(8,128)(2,1)S(1)}, bf16[7,256,128]{2,1,0:T(8,128)(2,1)S(1)}, u32[]{:S(2)}, u32[]{:S(2)}) collective-permute-start(bf16[7,256,128]{2,1,0:T(8,128)(2,1)S(1)} %get-tuple-element.28.refs_1_.refs_2_.refs_15_.refs_9_.refs_10_), channel_id=1, source_target_pairs={{0,4},{2,6},{4,8},{6,10},{8,12},{10,14},{12,0},{14,2},{1,5},{3,7},... | collective-permute-start | bytes 1376264 | tf_op jit(solution)/shard_map/ppermute | solution.py:398
  5.1 35.3 %collective-permute-start.2 = (bf16[4,256,128]{2,1,0:T(8,128)(2,1)S(1)}, bf16[4,256,128]{2,1,0:T(8,128)(2,1)S(1)}, u32[]{:S(2)}, u32[]{:S(2)}) collective-permute-start(bf16[4,256,128]{2,1,0:T(8,128)(2,1)S(1)} %get-tuple-element.31.refs_4_), channel_id=1, source_target_pairs={{0,2},{2,0},{4,6},{6,4},{8,10},{10,8},{12,14},{14,12},{1,3},{3,1},... | collective-permute-start | bytes 786440 | tf_op jit(solution)/shard_map/ppermute | solution.py:395
  6.6 21.3 %collective-permute-start.6 = (bf16[1,256,128]{2,1,0:T(8,128)(2,1)S(1)}, bf16[1,256,128]{2,1,0:T(8,128)(2,1)S(1)}, u32[]{:S(2)}, u32[]{:S(2)}) collective-permute-start(bf16[1,256,128]{2,1,0:T(8,128)(2,1)S(1)} %get-tuple-element.27.refs_0_.refs_1_.refs_14_.refs_8_.refs_9_), channel_id=1, source_target_pairs={{0,1},{1,0},{2,3},{3,2},{4,5},{5,4},{6,7},{7,6},{8,9},{9,8},{10,11... | collective-permute-start | bytes 196616 | tf_op jit(solution)/shard_map/ppermute | solution.py:404
  6.6 21.3 %collective-permute-start = (bf16[1,256,128]{2,1,0:T(8,128)(2,1)S(1)}, bf16[1,256,128]{2,1,0:T(8,128)(2,1)S(1)}, u32[]{:S(2)}, u32[]{:S(2)}) collective-permute-start(bf16[1,256,128]{2,1,0:T(8,128)(2,1)S(1)} %get-tuple-element.29.refs_2_), channel_id=1, source_target_pairs={{0,2},{2,0},{4,6},{6,4},{8,10},{10,8},{12,14},{14,12},{1,3},{3,1},... | collective-permute-start | bytes 196616 | tf_op jit(solution)/shard_map/ppermute | solution.py:395
  8.0 1.2 %collective-permute-start.11 = (f32[2,8,128]{2,1,0:T(8,128)S(1)}, f32[2,8,128]{2,1,0:T(8,128)S(1)}, u32[]{:S(2)}, u32[]{:S(2)}) collective-permute-start(f32[2,8,128]{2,1,0:T(8,128)S(1)} %shard_map.110), channel_id=1, source_target_pairs={{0,1},{1,0},{2,3},{3,2},{4,5},{5,4},{6,7},{7,6},{8,9},{9,8},{10,11... | collective-permute-start | bytes 24584 | tf_op jit(solution)/shard_map/ppermute | solution.py:404
  9.2 5.2 %collective-permute-start.12 = (f32[2,8,128]{2,1,0:T(8,128)S(1)}, f32[2,8,128]{2,1,0:T(8,128)S(1)}, u32[]{:S(2)}, u32[]{:S(2)}) collective-permute-start(f32[2,8,128]{2,1,0:T(8,128)S(1)} %add.11.refs_3_.refs_10_), channel_id=1, source_target_pairs={{0,2},{2,0},{4,6},{6,4},{8,10},{10,8},{12,14},{14,12},{1,3},{3,1},... | collective-permute-start | bytes 24584 | tf_op jit(solution)/shard_map/ppermute | solution.py:395
  14.4 5.4 %collective-permute-start.13 = (f32[2,8,128]{2,1,0:T(8,128)S(1)}, f32[2,8,128]{2,1,0:T(8,128)S(1)}, u32[]{:S(2)}, u32[]{:S(2)}) collective-permute-start(f32[2,8,128]{2,1,0:T(8,128)S(1)} %add.11.refs_3_.refs_10_), channel_id=1, source_target_pairs={{0,4},{2,6},{4,8},{6,10},{8,12},{10,14},{12,0},{14,2},{1,5},{3,7},... | collective-permute-start | bytes 24584 | tf_op jit(solution)/shard_map/ppermute | solution.py:398
  19.9 6.5 %collective-permute-start.14 = (f32[2,8,128]{2,1,0:T(8,128)S(1)}, f32[2,8,128]{2,1,0:T(8,128)S(1)}, u32[]{:S(2)}, u32[]{:S(2)}) collective-permute-start(f32[2,8,128]{2,1,0:T(8,128)S(1)} %add.11.refs_3_.refs_10_), channel_id=1, source_target_pairs={{0,6},{2,4},{4,10},{6,8},{8,14},{10,12},{12,2},{14,0},{1,7},{3,5},... | collective-permute-start | bytes 24584 | tf_op jit(solution)/shard_map/ppermute | solution.py:401
  26.4 14.0 %collective-permute-start.1 = (bf16[3,256,128]{2,1,0:T(8,128)(2,1)S(1)}, bf16[3,256,128]{2,1,0:T(8,128)(2,1)S(1)}, u32[]{:S(2)}, u32[]{:S(2)}) collective-permute-start(bf16[3,256,128]{2,1,0:T(8,128)(2,1)S(1)} %get-tuple-element.30.refs_3_), channel_id=1, source_target_pairs={{0,2},{2,0},{4,6},{6,4},{8,10},{10,8},{12,14},{14,12},{1,3},{3,1},... | collective-permute-start | bytes 589832 | tf_op jit(solution)/shard_map/ppermute | solution.py:395
  27.9 6.4 %collective-permute-start.8 = (bf16[1,256,128]{2,1,0:T(8,128)(2,1)S(1)}, bf16[1,256,128]{2,1,0:T(8,128)(2,1)S(1)}, u32[]{:S(2)}, u32[]{:S(2)}) collective-permute-start(bf16[1,256,128]{2,1,0:T(8,128)(2,1)S(1)} %get-tuple-element.27.refs_0_.refs_1_.refs_14_.refs_8_.refs_9_), channel_id=1, source_target_pairs={{0,4},{2,6},{4,8},{6,10},{8,12},{10,14},{12,0},{14,2},{1,5},{3,7},... | collective-permute-start | bytes 196616 | tf_op jit(solution)/shard_map/ppermute | solution.py:398
  27.9 6.4 %collective-permute-start.7 = (bf16[1,256,128]{2,1,0:T(8,128)(2,1)S(1)}, bf16[1,256,128]{2,1,0:T(8,128)(2,1)S(1)}, u32[]{:S(2)}, u32[]{:S(2)}) collective-permute-start(bf16[1,256,128]{2,1,0:T(8,128)(2,1)S(1)} %collective-permute-done.refs_4_.refs_3_.refs_2_.refs_17_.refs_11_), channel_id=1, source_target_pairs={{0,1},{1,0},{2,3},{3,2},{4,5},{5,4},{6,7},{7,6},{8,9},{9,8},{10,11... | collective-permute-start | bytes 196616 | tf_op jit(solution)/shard_map/ppermute | solution.py:404
  34.3 6.1 %collective-permute-start.3 = (bf16[1,256,128]{2,1,0:T(8,128)(2,1)S(1)}, bf16[1,256,128]{2,1,0:T(8,128)(2,1)S(1)}, u32[]{:S(2)}, u32[]{:S(2)}) collective-permute-start(bf16[1,256,128]{2,1,0:T(8,128)(2,1)S(1)} %collective-permute-done.refs_4_.refs_3_.refs_2_.refs_17_.refs_11_), channel_id=1, source_target_pairs={{0,4},{2,6},{4,8},{6,10},{8,12},{10,14},{12,0},{14,2},{1,5},{3,7},... | collective-permute-start | bytes 196616 | tf_op jit(solution)/shard_map/ppermute | solution.py:398
  34.3 6.2 %collective-permute-start.9 = (bf16[1,256,128]{2,1,0:T(8,128)(2,1)S(1)}, bf16[1,256,128]{2,1,0:T(8,128)(2,1)S(1)}, u32[]{:S(2)}, u32[]{:S(2)}) collective-permute-start(bf16[1,256,128]{2,1,0:T(8,128)(2,1)S(1)} %collective-permute-done.8.refs_8_), channel_id=1, source_target_pairs={{0,1},{1,0},{2,3},{3,2},{4,5},{5,4},{6,7},{7,6},{8,9},{9,8},{10,11... | collective-permute-start | bytes 196616 | tf_op jit(solution)/shard_map/ppermute | solution.py:404
  36.9 13.0 %copy-start.4 = (f32[128]{0:T(128)S(1)}, f32[128]{0:T(128)}, u32[]{:S(2)}) copy-start(f32[128]{0:T(128)} %param.15) | copy-start | bytes 1540
  40.4 4.3 %collective-permute-start.15 = (bf16[1,256,128]{2,1,0:T(8,128)(2,1)S(1)}, bf16[1,256,128]{2,1,0:T(8,128)(2,1)S(1)}, u32[]{:S(2)}, u32[]{:S(2)}) collective-permute-start(bf16[1,256,128]{2,1,0:T(8,128)(2,1)S(1)} %collective-permute-done.3.refs_6_.refs_5_), channel_id=1, source_target_pairs={{0,1},{1,0},{2,3},{3,2},{4,5},{5,4},{6,7},{7,6},{8,9},{9,8},{10,11... | collective-permute-start | bytes 196616 | tf_op jit(solution)/shard_map/ppermute | solution.py:404
  40.4 9.6 %collective-permute-start.4 = (bf16[3,256,128]{2,1,0:T(8,128)(2,1)S(1)}, bf16[3,256,128]{2,1,0:T(8,128)(2,1)S(1)}, u32[]{:S(2)}, u32[]{:S(2)}) collective-permute-start(bf16[3,256,128]{2,1,0:T(8,128)(2,1)S(1)} %collective-permute-done.1.refs_5_.refs_4_.refs_3_.refs_18_.refs_12_), channel_id=1, source_target_pairs={{0,4},{2,6},{4,8},{6,10},{8,12},{10,14},{12,0},{14,2},{1,5},{3,7},... | collective-permute-start | bytes 589832 | tf_op jit(solution)/shard_map/ppermute | solution.py:398
  40.4 14.7 %collective-permute-start.5 = (bf16[4,256,128]{2,1,0:T(8,128)(2,1)S(1)}, bf16[4,256,128]{2,1,0:T(8,128)(2,1)S(1)}, u32[]{:S(2)}, u32[]{:S(2)}) collective-permute-start(bf16[4,256,128]{2,1,0:T(8,128)(2,1)S(1)} %collective-permute-done.2.refs_6_.refs_4_.refs_19_.refs_13_), channel_id=1, source_target_pairs={{0,4},{2,6},{4,8},{6,10},{8,12},{10,14},{12,0},{14,2},{1,5},{3,7},... | collective-permute-start | bytes 786440 | tf_op jit(solution)/shard_map/ppermute | solution.py:398
  51.5 12.5 %collective-permute-start.18 = (bf16[3,256,128]{2,1,0:T(8,128)(2,1)S(1)}, bf16[3,256,128]{2,1,0:T(8,128)(2,1)S(1)}, u32[]{:S(2)}, u32[]{:S(2)}) collective-permute-start(bf16[3,256,128]{2,1,0:T(8,128)(2,1)S(1)} %get-tuple-element.39.refs_2_), channel_id=1, source_target_pairs={{0,4},{2,6},{4,8},{6,10},{8,12},{10,14},{1,5},{3,7},{5,9},{7,11},{... | collective-permute-start | bytes 589832 | tf_op jit(solution)/shard_map/ppermute | solution.py:398
  55.1 3.4 %copy-start.10 = (bf16[3,3,128,128]{3,2,1,0:T(8,128)(2,1)S(1)}, bf16[3,3,128,128]{3,2,1,0:T(8,128)(2,1)}, u32[]{:S(2)}) copy-start(bf16[3,3,128,128]{3,2,1,0:T(8,128)(2,1)} %param.20) | copy-start | bytes 884740
  55.1 11.7 %copy-start.2 = (bf16[3,3,3,128,128]{4,3,2,1,0:T(8,128)(2,1)S(1)}, bf16[3,3,3,128,128]{4,3,2,1,0:T(8,128)(2,1)}, u32[]{:S(2)}) copy-start(bf16[3,3,3,128,128]{4,3,2,1,0:T(8,128)(2,1)} %refs_10_.1) | copy-start | bytes 2654212
  55.1 11.7 %copy-start.5 = (f32[128]{0:T(128)S(1)}, f32[128]{0:T(128)}, u32[]{:S(2)}) copy-start(f32[128]{0:T(128)} %param.16) | copy-start | bytes 1540
  55.1 11.7 %copy-start.6 = (f32[128]{0:T(128)S(1)}, f32[128]{0:T(128)}, u32[]{:S(2)}) copy-start(f32[128]{0:T(128)} %param.17) | copy-start | bytes 1540
  57.1 3.3 %collective-permute-start.21 = (f32[2,8,128]{2,1,0:T(8,128)S(1)}, f32[2,8,128]{2,1,0:T(8,128)S(1)}, u32[]{:S(2)}, u32[]{:S(2)}) collective-permute-start(f32[2,8,128]{2,1,0:T(8,128)S(1)} %get-tuple-element.41), channel_id=1, source_target_pairs={{0,1},{1,0},{2,3},{3,2},{4,5},{5,4},{6,7},{7,6},{8,9},{9,8},{10,11... | collective-permute-start | bytes 24584 | tf_op jit(solution)/shard_map/ppermute | solution.py:404
  57.2 8.9 %collective-permute-start.16 = (bf16[4,256,128]{2,1,0:T(8,128)(2,1)S(1)}, bf16[4,256,128]{2,1,0:T(8,128)(2,1)S(1)}, u32[]{:S(2)}, u32[]{:S(2)}) collective-permute-start(bf16[4,256,128]{2,1,0:T(8,128)(2,1)S(1)} %get-tuple-element.37.refs_0_.refs_4_.refs_3_), channel_id=1, source_target_pairs={{0,4},{2,6},{4,8},{6,10},{8,12},{10,14},{1,5},{3,7},{5,9},{7,11},{... | collective-permute-start | bytes 786440 | tf_op jit(solution)/shard_map/ppermute | solution.py:398
  58.6 7.6 %collective-permute-start.23 = (bf16[2,2,256,128]{3,2,1,0:T(8,128)(2,1)S(1)}, bf16[2,2,256,128]{3,2,1,0:T(8,128)(2,1)S(1)}, u32[]{:S(2)}, u32[]{:S(2)}) collective-permute-start(bf16[2,2,256,128]{3,2,1,0:T(8,128)(2,1)S(1)} %get-tuple-element.42), channel_id=1, source_target_pairs={{0,1},{1,0},{2,3},{3,2},{4,5},{5,4},{6,7},{7,6},{8,9},{9,8},{10,11... | collective-permute-start | bytes 786440 | tf_op jit(solution)/shard_map/ppermute | solution.py:404
  59.1 18.7 %collective-permute-start.19 = (bf16[5,256,128]{2,1,0:T(8,128)(2,1)S(1)}, bf16[5,256,128]{2,1,0:T(8,128)(2,1)S(1)}, u32[]{:S(2)}, u32[]{:S(2)}) collective-permute-start(bf16[5,256,128]{2,1,0:T(8,128)(2,1)S(1)} %get-tuple-element.40.refs_3_), channel_id=1, source_target_pairs={{0,4},{2,6},{4,8},{6,10},{8,12},{10,14},{1,5},{3,7},{5,9},{7,11},{... | collective-permute-start | bytes 983048 | tf_op jit(solution)/shard_map/ppermute | solution.py:398
  60.5 22.9 %collective-permute-start.17 = (bf16[4,256,128]{2,1,0:T(8,128)(2,1)S(1)}, bf16[4,256,128]{2,1,0:T(8,128)(2,1)S(1)}, u32[]{:S(2)}, u32[]{:S(2)}) collective-permute-start(bf16[4,256,128]{2,1,0:T(8,128)(2,1)S(1)} %get-tuple-element.38.refs_1_.refs_5_.refs_4_), channel_id=1, source_target_pairs={{0,4},{2,6},{4,8},{6,10},{8,12},{10,14},{1,5},{3,7},{5,9},{7,11},{... | collective-permute-start | bytes 786440 | tf_op jit(solution)/shard_map/ppermute | solution.py:398
  64.0 13.8 %collective-permute-start.22 = (f32[2,8,128]{2,1,0:T(8,128)S(1)}, f32[2,8,128]{2,1,0:T(8,128)S(1)}, u32[]{:S(2)}, u32[]{:S(2)}) collective-permute-start(f32[2,8,128]{2,1,0:T(8,128)S(1)} %add.12.refs_5_.refs_7_), channel_id=1, source_target_pairs={{0,4},{2,6},{4,8},{6,10},{8,12},{10,14},{1,5},{3,7},{5,9},{7,11},{... | collective-permute-start | bytes 24584 | tf_op jit(solution)/shard_map/ppermute | solution.py:398
  66.1 11.7 %collective-permute-start.20 = (bf16[1,2,256,128]{3,2,1,0:T(8,128)(2,1)S(1)}, bf16[1,2,256,128]{3,2,1,0:T(8,128)(2,1)S(1)}, u32[]{:S(2)}, u32[]{:S(2)}) collective-permute-start(bf16[1,2,256,128]{3,2,1,0:T(8,128)(2,1)S(1)} %slice_bitcast_fusion.1), channel_id=1, source_target_pairs={{0,1},{1,0},{2,3},{3,2},{4,5},{5,4},{6,7},{7,6},{8,9},{9,8},{10,11... | collective-permute-start | bytes 393224 | tf_op jit(solution)/shard_map/ppermute | solution.py:404
  66.2 15.6 %collective-permute-start.24 = (bf16[1,2,256,128]{3,2,1,0:T(8,128)(2,1)S(1)}, bf16[1,2,256,128]{3,2,1,0:T(8,128)(2,1)S(1)}, u32[]{:S(2)}, u32[]{:S(2)}) collective-permute-start(bf16[1,2,256,128]{3,2,1,0:T(8,128)(2,1)S(1)} %slice_bitcast_fusion), channel_id=1, source_target_pairs={{0,1},{1,0},{2,3},{3,2},{4,5},{5,4},{6,7},{7,6},{8,9},{9,8},{10,11... | collective-permute-start | bytes 393224 | tf_op jit(solution)/shard_map/ppermute | solution.py:404
  66.8 11.0 %copy-start.3 = (f32[128]{0:T(128)S(1)}, f32[128]{0:T(128)}, u32[]{:S(2)}) copy-start(f32[128]{0:T(128)} %param.21) | copy-start | bytes 1540
  66.8 11.0 %copy-start.7 = (f32[128]{0:T(128)S(1)}, f32[128]{0:T(128)}, u32[]{:S(2)}) copy-start(f32[128]{0:T(128)} %param.19) | copy-start | bytes 1540
  85.9 5.4 %collective-permute-start.25 = (bf16[4,128,128]{2,1,0:T(8,128)(2,1)S(1)}, bf16[4,128,128]{2,1,0:T(8,128)(2,1)S(1)}, u32[]{:S(2)}, u32[]{:S(2)}) collective-permute-start(bf16[4,128,128]{2,1,0:T(8,128)(2,1)S(1)} %get-tuple-element.48), channel_id=1, source_target_pairs={{0,2},{2,0},{4,6},{6,4},{8,10},{10,8},{12,14},{14,12},{1,3},{3,1},... | collective-permute-start | bytes 393224 | tf_op jit(solution)/shard_map/ppermute | solution.py:395
where the time goes:
time: 92.2 us; the launch traced here: 92 us
  waiting for transfers between devices  43.1 us (47%)
  Pallas kernels  24.1 us (26%)
  starting transfers between devices  22.2 us (24%)
  local copies, waits for them, and re-layouts  1.35 us (1%)
    ppermute x11, waiting for transfers between devices, later(): return lax.ppermute(v, 'tm', onward(name, 0))  27.9 us
    pallas_call x10, Pallas kernels, call(): pl.pallas_call(kernel, out_shape=out_shape, in_specs=[pl.BlockSpec(memory...  24.1 us
    ppermute x11, starting transfers between devices, later(): return lax.ppermute(v, 'tm', onward(name, 0))  14.2 us
    ppermute x5, waiting for transfers between devices, swapped(): return lax.ppermute(v, 'tm', swap)  8.53 us
    ppermute x1, waiting for transfers between devices, crossed(): return lax.ppermute(v, 'tm', onward(name, 1))  5.72 us
    ppermute x5, starting transfers between devices, swapped(): return lax.ppermute(v, 'tm', swap)  5.64 us
  transfers between devices with their start and end apart: 26, of which 10 were waited for; matrix products, arithmetic and copies ran while one was open for 0% of the time, Pallas kernels for 23%

commit v1 on v0

--- a/solution.py
+++ b/solution.py
@@ -50,16 +50,6 @@
     stack[r, :, 2 * channels :] = after.astype(BF16)
 
 
-def fill_frame(stack, values, params):
-    for r, value in enumerate(values):
-        fill_row(stack, r, value(), params)
-
-
-def close_stack(stack):
-    last = stack.shape[0] - 1
-    stack[last] = jnp.zeros(stack.shape[1:], BF16)
-
-
 def taps(stack, weights, start, count):
     rows = [
         jnp.concatenate([stack[r], stack[r + 1], stack[r + 2]], axis=1)
@@ -72,6 +62,28 @@
     total = last - first
     size = 3 if total % 3 == 0 else 2
     return [(r, min(size, last - r)) for r in range(first, last, size)]
+
+
+def sweep(frames, first, last, emit):
+    filled = 0
+
+    def fill(until):
+        nonlocal filled
+        for r in range(filled, until):
+            for stack, values, params, _ in frames:
+                if r < len(values):
+                    fill_row(stack, r, values[r](), params)
+                else:
+                    stack[r] = jnp.zeros(stack.shape[1:], BF16)
+        filled = max(filled, until)
+
+    groups = steps(first, last)
+    fill(sum(groups[0]) + 2)
+    for k, (start, count) in enumerate(groups):
+        part = sum(taps(stack, weights[...], start, count) for stack, _, _, weights in frames)
+        if k + 1 < len(groups):
+            fill(sum(groups[k + 1]) + 2)
+        emit(start, count, part)
 
 
 def reader(ref, r):
@@ -136,11 +148,11 @@
     height, width, _ = acc_ref.shape
     lay_weights(w_ref, k_ref, 2 + flags[0], flags[2])
     params = norm_params(t_ref[0], g_ref[...], c_ref[...], cells)
-    fill_frame(stack, rows_of(*own), params)
-    close_stack(stack)
-    for start, count in steps(0, height):
-        part = taps(stack, w_ref[...], start, count)
+
+    def emit(start, count, part):
         acc_ref[start : start + count] = part.reshape(count, width, -1)
+
+    sweep([(stack, rows_of(*own), params, w_ref)], 0, height, emit)
 
 
 def mates_kernel(cells, flags, own, mate, past, to_ref, tm_ref, tp_ref, tq_ref, g_ref, c_ref, k_ref, in_ref, acc_ref, last_ref, edge_ref, xm, xp, wm, wp):
@@ -150,37 +162,42 @@
     lay_weights(wm, k_ref, 3 - side, flags[2])
     lay_weights(wp, k_ref, side, flags[2])
     params = norm_params(tm_ref[1], g_ref[...], c_ref[...], cells)
-    fill_frame(xm, rows_of(*mate), params)
-    close_stack(xm)
+    frames = [(xm, rows_of(*mate), params, wm)]
     start_totals = jnp.where(even, to_ref[0], tm_ref[1])
     totals = jnp.where(first, start_totals, tp_ref[0])
     params = norm_params(totals, g_ref[...], c_ref[...], cells)
-    fill_frame(xp, chosen(flags, rows_of(*past), rows_of(*own), rows_of(*mate)), params)
-    close_stack(xp)
-    for start, count in steps(0, height):
-        part = taps(xm, wm[...], start, count) + taps(xp, wp[...], start, count)
+    values = chosen(flags, rows_of(*past), rows_of(*own), rows_of(*mate))
+    frames.append((xp, values, params, wp))
+
+    def emit(start, count, part):
         acc_ref[start : start + count] = in_ref[start : start + count] + part.reshape(count, width, -1)
+
+    sweep(frames, 0, height, emit)
     totals = jnp.where(first, start_totals, tq_ref[1])
     keep_params(last_ref, norm_params(totals, g_ref[...], c_ref[...], cells))
     edge_ref[0] = own[0][0]
     edge_ref[1] = mate[0][0]
 
 
-def hidden_rows(stack, w_ref, in_ref, bias_ref, first, a_ref, b_ref, sum_ref):
+def hidden_rows(stack, values, params, w_ref, in_ref, bias_ref, first, a_ref, b_ref, sum_ref):
     rows, width, channels = a_ref.shape
     both = 2 * channels
     bias = jnp.concatenate([bias_ref[...], bias_ref[...]], axis=1)
     total = jnp.zeros((8, both), F32)
     square = jnp.zeros((8, both), F32)
-    for start, count in steps(0, rows):
-        part = taps(stack, w_ref[...], start, count).reshape(count, width, both)
+
+    def emit(start, count, part):
+        nonlocal total, square
         begin = first + start
+        part = part.reshape(count, width, both)
         hidden = (in_ref[begin : begin + count] + part + bias).astype(BF16)
         a_ref[start : start + count] = hidden[:, :, :channels]
         b_ref[start : start + count] = hidden[:, :, channels:]
         wide = hidden.astype(F32).reshape(count * width // 8, 8, both)
         total += jnp.sum(wide, axis=0)
         square += jnp.sum(wide * wide, axis=0)
+
+    sweep([(stack, values, params, w_ref)], 0, rows, emit)
     total = jnp.sum(total, axis=0, keepdims=True)
     square = jnp.sum(square, axis=0, keepdims=True)
     for k in range(2):
@@ -194,8 +211,8 @@
     edges = own[0]
     owns = [reader(edges, 0)] + rows_of(*own[1:])
     mates = [reader(edges, 1)] + rows_of(*mate)
-    fill_frame(stack, chosen(flags, rows_of(*past), owns, mates), kept_params(n_ref))
-    hidden_rows(stack, w_ref, in_ref, bias_ref, 0, a_ref, b_ref, sum_ref)
+    values = chosen(flags, rows_of(*past), owns, mates)
+    hidden_rows(stack, values, kept_params(n_ref), w_ref, in_ref, bias_ref, 0, a_ref, b_ref, sum_ref)
     edge_ref[0] = a_ref[0:2]
     edge_ref[1] = b_ref[0:2]
 
@@ -205,9 +222,8 @@
     height = in_ref.shape[0]
     rows, early = b_ref.shape[0], near_ref.shape[0]
     values = chosen(flags, rows_of(*past), rows_of(*own), rows_of(*mate))
-    fill_frame(stack, values[height - rows - 1 :], kept_params(n_ref))
-    close_stack(stack)
-    hidden_rows(stack, w_ref, in_ref, bias_ref, height - rows, held, b_ref, sum_ref)
+    first = height - rows
+    hidden_rows(stack, values[first - 1 :], kept_params(n_ref), w_ref, in_ref, bias_ref, first, held, b_ref, sum_ref)
     sum_ref[...] += part_ref[...]
     whole = a_ref.shape[0]
     a_ref[0:early] = near_ref[...]
@@ -223,13 +239,15 @@
     out_rows, width, _ = acc_ref.shape
     lay_weights(wa, k_ref, 2, flags[2])
     lay_weights(wb, k_ref, 3, flags[2])
-    for k, (stack, near, far) in enumerate(((xa, a1, a2), (xb, b1, b2))):
+    frames = []
+    for k, (stack, near, far, weights) in enumerate(((xa, a1, a2, wa), (xb, b1, b2, wb))):
         params = norm_params(t_ref[k], g_ref[...], c_ref[...], cells)
-        fill_frame(stack, halves(e_ref, k, near, far), params)
-        close_stack(stack)
-    for start, count in steps(0, out_rows):
-        part = taps(xa, wa[...], start, count) + taps(xb, wb[...], start, count)
+        frames.append((stack, halves(e_ref, k, near, far), params, weights))
+
+    def emit(start, count, part):
         acc_ref[start : start + count] = part.reshape(count, width, -1)
+
+    sweep(frames, 0, out_rows, emit)
 
 
 def either(flags, first, other):
@@ -273,18 +291,19 @@
     values = [
         either(flags, f, o) for f, o in zip(halves(e_ref, 0, a1, a2), halves(eb_ref, 0, b1, b2))
     ]
-    fill_frame(stack, values, params)
-    close_stack(stack)
     raw = raw_rows(flags[0] == 0, rows_of(*mate), rows_of(*own))
     bias = jnp.concatenate([bias_ref[...], bias_ref[...]], axis=1)
     res[:, width:, :] = jnp.zeros((res.shape[0], res.shape[1] - width, channels), F32)
     res[out_rows] = jnp.zeros(res.shape[1:], F32)
-    for start, count in steps(0, out_rows):
-        part = taps(stack, w_ref[...], start, count).reshape(count, width, 2 * channels)
+
+    def emit(start, count, part):
+        part = part.reshape(count, width, 2 * channels)
         branch = in_ref[start : start + count] + part + bias
         acc_ref[start : start + count] = branch[:, :, :channels]
         for k in range(count):
             put_row(res, start + k, residual_row(raw[start + k](), branch[k, :, channels:]))
+
+    sweep([(stack, values, params, w_ref)], 0, out_rows, emit)
     out_ref[...] = down_rows(flags, res, wd_ref, bd_ref, 0, height // 2)
     params = norm_params(jnp.where(flags[1] == 1, t_ref[0], tp_ref[0]), g_ref[...], c_ref[...], cells)
     keep_params(last_ref, params)
@@ -294,13 +313,15 @@
     rows, width, channels = out_ref.shape
     firsts = [lambda: e_ref[0, 1], lambda: e_ref[0, 0]] + rows_of(a1)
     others = [lambda: ep_ref[0, 1], lambda: ep_ref[0, 0]] + rows_of(p1)
-    fill_frame(stack, [either(flags, f, o) for f, o in zip(firsts, others)], kept_params(n_ref))
+    values = [either(flags, f, o) for f, o in zip(firsts, others)]
     raw = raw_rows(flags[0] == 0, rows_of(*own), rows_of(*mate))
-    for start, count in steps(0, rows):
-        part = taps(stack, w_ref[...], start, count).reshape(count, width, channels)
-        branch = in_ref[start : start + count] + part
+
+    def emit(start, count, part):
+        branch = in_ref[start : start + count] + part.reshape(count, width, channels)
         for k in range(count):
             out_ref[start + k] = residual_row(raw[start + k](), branch[k])
+
+    sweep([(stack, values, kept_params(n_ref), w_ref)], 0, rows, emit)
 
 
 def first_far_kernel(cells, flags, p1, p2, n_ref, a1, a2, w_ref, in_ref, near_ref, other_ref, own, mate, wd_ref, bd_ref, send_ref, keep_ref, stack, res):
@@ -309,19 +330,19 @@
     done = near_ref.shape[0]
     even = flags[0] == 0
     values = [either(flags, f, o) for f, o in zip(rows_of(a1, a2), rows_of(p1, p2))]
-    fill_frame(stack, values[done - 2 :], kept_params(n_ref))
-    close_stack(stack)
     raw = raw_rows(even, rows_of(*own), rows_of(*mate))
     res[:, width:, :] = jnp.zeros((res.shape[0], res.shape[1] - width, channels), F32)
     res[out_rows] = jnp.zeros(res.shape[1:], F32)
     for r in range(done):
         put_row(res, r, near_ref[r])
-    for start, count in steps(0, out_rows - done):
-        part = taps(stack, w_ref[...], start, count).reshape(count, width, channels)
-        branch = in_ref[done + start : done + start + count] + part
+
+    def emit(start, count, part):
+        begin = done + start
+        branch = in_ref[begin : begin + count] + part.reshape(count, width, channels)
         for k in range(count):
-            r = done + start + k
-            put_row(res, r, residual_row(raw[r - 1](), branch[k]))
+            put_row(res, begin + k, residual_row(raw[begin + k - 1](), branch[k]))
+
+    sweep([(stack, values[done - 2 :], kept_params(n_ref), w_ref)], 0, out_rows - done, emit)
     out = down_rows(flags, res, wd_ref, bd_ref, 0, height // 2)
     rows = height // 2
     for i in range(rows):
@@ -599,7 +620,7 @@
     return result[:, None]
 
 
-OPEN = ('b_on1', 'b_on2', 'a_on1', 'a_on2', 'hsums_on')
+OPEN = ('b_on2','a_on1','a_on2')
 TAIL = 2
 
 

time: 92.2 us -> 92.2 us (level)
  starting transfers between devices: 22.2 us -> 19.8 us
  waiting for transfers between devices: 43.1 us -> 45.5 us
    ppermute x11, waiting for transfers between devices: 27.9 us -> 30.3 us  [later(): return lax.ppermute(v, 'tm', onward(name, 0))]
    ppermute x11, starting transfers between devices: 14.2 us -> 11.9 us  [later(): return lax.ppermute(v, 'tm', onward(name, 0))]
  transfers between devices with their start and end apart: 26 -> 26, of which waited for: 10 -> 11; matrix products, arithmetic and copies ran while one was open for 0% -> 0% of each run, Pallas kernels for 23% -> 23%
where the time goes in v1:
time: 92.2 us; the launch traced here: 92 us
  waiting for transfers between devices  45.5 us (49%)
  Pallas kernels  24.1 us (26%)
  starting transfers between devices  19.8 us (21%)
  local copies, waits for them, and re-layouts  1.35 us (1%)
    ppermute x11, waiting for transfers between devices, later(): return lax.ppermute(v, 'tm', onward(name, 0))  30.3 us
    pallas_call x10, Pallas kernels, call(): pl.pallas_call(kernel, out_shape=out_shape, in_specs=[pl.BlockSpec(memory...  24.1 us
    ppermute x11, starting transfers between devices, later(): return lax.ppermute(v, 'tm', onward(name, 0))  11.9 us
    ppermute x5, waiting for transfers between devices, swapped(): return lax.ppermute(v, 'tm', swap)  8.53 us
    ppermute x1, waiting for transfers between devices, crossed(): return lax.ppermute(v, 'tm', onward(name, 1))  5.72 us
    ppermute x5, starting transfers between devices, swapped(): return lax.ppermute(v, 'tm', swap)  5.64 us
  transfers between devices with their start and end apart: 26, of which 11 were waited for; matrix products, arithmetic and copies ran while one was open for 0% of the time, Pallas kernels for 23%

profile of v1, /device:TPU:0, one launch (start us, length us, event | category | flops | bytes accessed | tf_op | source)
XLA Modules:
  0.0 92.0 jit_solution(7871786478189121540)
XLA Ops:
  0.0 0.1 pad_add_fusion.flags_ref
  0.1 1.3 %copy-done.1 = bf16[2,1,8,256,128]{4,3,2,1,0:T(8,128)(2,1)S(1)} copy-done((bf16[2,1,8,256,128]{4,3,2,1,0:T(8,128)(2,1)S(1)}, bf16[2,1,8,256,128]{4,3,2,1,0:T(8,128)(2,1)}, u32[]{:S(2)}) %copy-start.1) | copy-done | bytes 1048600
  1.4 0.6 shard_map.109
  2.0 3.1 %collective-permute-start.10 = (bf16[7,256,128]{2,1,0:T(8,128)(2,1)S(1)}, bf16[7,256,128]{2,1,0:T(8,128)(2,1)S(1)}, u32[]{:S(2)}, u32[]{:S(2)}) collective-permute-start(bf16[7,256,128]{2,1,0:T(8,128)(2,1)S(1)} %get-tuple-element.28.refs_1_.refs_2_.refs_15_.refs_9_.refs_10_), channel_id=1, source_target_pairs={{0,4},{2,6},{4,8},{6,10},{8,12},{10,14},{12,0},{14,2},{1,5},{3,7},... | collective-permute-start | bytes 1376264 | tf_op jit(solution)/shard_map/ppermute | solution.py:419
  5.1 1.5 %collective-permute-start.2 = (bf16[4,256,128]{2,1,0:T(8,128)(2,1)S(1)}, bf16[4,256,128]{2,1,0:T(8,128)(2,1)S(1)}, u32[]{:S(2)}, u32[]{:S(2)}) collective-permute-start(bf16[4,256,128]{2,1,0:T(8,128)(2,1)S(1)} %get-tuple-element.31.refs_4_), channel_id=1, source_target_pairs={{0,2},{2,0},{4,6},{6,4},{8,10},{10,8},{12,14},{14,12},{1,3},{3,1},... | collective-permute-start | bytes 786440 | tf_op jit(solution)/shard_map/ppermute | solution.py:416
  6.6 0.0 collective-permute-start.6
  6.6 0.5 collective-permute-start
  7.1 0.8 shard_map.110
  8.0 0.3 collective-permute-start.11
  8.3 0.9 %collective-permute-done.11 = f32[2,8,128]{2,1,0:T(8,128)S(1)} collective-permute-done((f32[2,8,128]{2,1,0:T(8,128)S(1)}, f32[2,8,128]{2,1,0:T(8,128)S(1)}, u32[]{:S(2)}, u32[]{:S(2)}) %collective-permute-start.11) | collective-permute-done | bytes 8224 | tf_op jit(solution)/shard_map/ppermute | solution.py:425
  9.2 1.5 %collective-permute-start.12 = (f32[2,8,128]{2,1,0:T(8,128)S(1)}, f32[2,8,128]{2,1,0:T(8,128)S(1)}, u32[]{:S(2)}, u32[]{:S(2)}) collective-permute-start(f32[2,8,128]{2,1,0:T(8,128)S(1)} %add.11.refs_3_.refs_10_), channel_id=1, source_target_pairs={{0,2},{2,0},{4,6},{6,4},{8,10},{10,8},{12,14},{14,12},{1,3},{3,1},... | collective-permute-start | bytes 24584 | tf_op jit(solution)/shard_map/ppermute | solution.py:416
  10.7 3.7 %collective-permute-done.12.refs_11_ = f32[2,8,128]{2,1,0:T(8,128)S(1)} collective-permute-done((f32[2,8,128]{2,1,0:T(8,128)S(1)}, f32[2,8,128]{2,1,0:T(8,128)S(1)}, u32[]{:S(2)}, u32[]{:S(2)}) %collective-permute-start.12) | collective-permute-done | bytes 8224 | tf_op jit(solution)/shard_map/ppermute | solution.py:416
  14.4 1.6 %collective-permute-start.13 = (f32[2,8,128]{2,1,0:T(8,128)S(1)}, f32[2,8,128]{2,1,0:T(8,128)S(1)}, u32[]{:S(2)}, u32[]{:S(2)}) collective-permute-start(f32[2,8,128]{2,1,0:T(8,128)S(1)} %add.11.refs_3_.refs_10_), channel_id=1, source_target_pairs={{0,4},{2,6},{4,8},{6,10},{8,12},{10,14},{12,0},{14,2},{1,5},{3,7},... | collective-permute-start | bytes 24584 | tf_op jit(solution)/shard_map/ppermute | solution.py:419
  16.0 3.9 %collective-permute-done.13.refs_12_ = f32[2,8,128]{2,1,0:T(8,128)S(1)} collective-permute-done((f32[2,8,128]{2,1,0:T(8,128)S(1)}, f32[2,8,128]{2,1,0:T(8,128)S(1)}, u32[]{:S(2)}, u32[]{:S(2)}) %collective-permute-start.13) | collective-permute-done | bytes 8224 | tf_op jit(solution)/shard_map/ppermute | solution.py:419
  19.9 0.7 collective-permute-start.14
  20.6 5.7 %collective-permute-done.14.refs_13_ = f32[2,8,128]{2,1,0:T(8,128)S(1)} collective-permute-done((f32[2,8,128]{2,1,0:T(8,128)S(1)}, f32[2,8,128]{2,1,0:T(8,128)S(1)}, u32[]{:S(2)}, u32[]{:S(2)}) %collective-permute-start.14) | collective-permute-done | bytes 8224 | tf_op jit(solution)/shard_map/ppermute | solution.py:422
  26.4 1.5 %collective-permute-start.1 = (bf16[3,256,128]{2,1,0:T(8,128)(2,1)S(1)}, bf16[3,256,128]{2,1,0:T(8,128)(2,1)S(1)}, u32[]{:S(2)}, u32[]{:S(2)}) collective-permute-start(bf16[3,256,128]{2,1,0:T(8,128)(2,1)S(1)} %get-tuple-element.30.refs_3_), channel_id=1, source_target_pairs={{0,2},{2,0},{4,6},{6,4},{8,10},{10,8},{12,14},{14,12},{1,3},{3,1},... | collective-permute-start | bytes 589832 | tf_op jit(solution)/shard_map/ppermute | solution.py:416
  27.9 0.0 collective-permute-done.6.refs_0_.refs_13_.refs_7_
  27.9 0.0 collective-permute-start.8
  27.9 0.0 collective-permute-done.refs_4_.refs_3_.refs_2_.refs_17_.refs_11_
  27.9 0.1 collective-permute-start.7
  28.0 6.3 %collective-permute-done.8.refs_8_ = bf16[1,256,128]{2,1,0:T(8,128)(2,1)S(1)} collective-permute-done((bf16[1,256,128]{2,1,0:T(8,128)(2,1)S(1)}, bf16[1,256,128]{2,1,0:T(8,128)(2,1)S(1)}, u32[]{:S(2)}, u32[]{:S(2)}) %collective-permute-start.8) | collective-permute-done | bytes 65568 | tf_op jit(solution)/shard_map/ppermute | solution.py:419
  34.3 0.0 collective-permute-start.3
  34.3 0.0 collective-permute-done.7.refs_3_.refs_16_.refs_10_
  34.3 0.0 collective-permute-start.9
  34.3 2.6 %shard_map.111.refs_17_ = f32[8,256,256]{2,1,0:T(8,128)S(1)} custom-call(s32[3]{0:T(128)S(1)} %pad_add_fusion.flags_ref, bf16[1,256,128]{2,1,0:T(8,128)(2,1)S(1)} %collective-permute-done.6.refs_0_.refs_13_.refs_7_, bf16[1,256,128]{2,1,0:T(8,128)(2,1)S(1)} %get-tuple-element.27.refs_0_.refs_1_.refs_14_.refs_8_.refs_9_, ...), custom_call_target="tpu_custom_call" | custom-call | flops 1207959552 | bytes 1483776 | tf_op jit(solution)/shard_map/pallas_call | solution.py:367
  36.9 0.0 copy-start.4
  37.0 3.4 %collective-permute-done.3.refs_6_.refs_5_ = bf16[1,256,128]{2,1,0:T(8,128)(2,1)S(1)} collective-permute-done((bf16[1,256,128]{2,1,0:T(8,128)(2,1)S(1)}, bf16[1,256,128]{2,1,0:T(8,128)(2,1)S(1)}, u32[]{:S(2)}, u32[]{:S(2)}) %collective-permute-start.3) | collective-permute-done | bytes 65568 | tf_op jit(solution)/shard_map/ppermute | solution.py:419
  40.4 0.0 collective-permute-start.15
  40.4 0.0 collective-permute-done.1.refs_5_.refs_4_.refs_3_.refs_18_.refs_12_
  40.4 0.0 collective-permute-start.4
  40.4 0.0 collective-permute-done.2.refs_6_.refs_4_.refs_19_.refs_13_
  40.4 0.1 collective-permute-start.5
  40.5 0.0 collective-permute-done.9.refs_7_
  40.5 0.0 collective-permute-done.10.refs_9_
  40.5 4.2 %shard_map.112 = (f32[8,256,256]{2,1,0:T(8,128)S(1)}, f32[8,128]{1,0:T(8,128)S(1)}, bf16[2,256,128]{2,1,0:T(8,128)(2,1)S(1)}) custom-call(s32[3]{0:T(128)S(1)} %pad_add_fusion.flags_ref, bf16[1,256,128]{2,1,0:T(8,128)(2,1)S(1)} %collective-permute-done.6.refs_0_.refs_13_.refs_7_, ...), custom_call_target="tpu_custom_call" | custom-call | flops 2415919104 | bytes 4785152 | tf_op jit(solution)/shard_map/pallas_call | solution.py:367
  44.7 5.3 %collective-permute-done.4.refs_7_.refs_6_ = bf16[3,256,128]{2,1,0:T(8,128)(2,1)S(1)} collective-permute-done((bf16[3,256,128]{2,1,0:T(8,128)(2,1)S(1)}, bf16[3,256,128]{2,1,0:T(8,128)(2,1)S(1)}, u32[]{:S(2)}, u32[]{:S(2)}) %collective-permute-start.4) | collective-permute-done | bytes 196640 | tf_op jit(solution)/shard_map/ppermute | solution.py:419
  49.9 1.5 %shard_map.113 = (bf16[3,256,128]{2,1,0:T(8,128)(2,1)S(1)}, bf16[3,256,128]{2,1,0:T(8,128)(2,1)S(1)}, bf16[2,2,256,128]{3,2,1,0:T(8,128)(2,1)S(1)}, f32[2,8,128]{2,1,0:T(8,128)S(1)}) custom-call(s32[3]{0:T(128)S(1)} %pad_add_fusion.flags_ref, bf16[2,256,128]{2,1,0:T(8,128)(2,1)S(1)} %get-tuple-element.34.refs_0_, ...), custom_call_target="tpu_custom_call" | custom-call | flops 452984832 | bytes 4231680 | tf_op jit(solution)/shard_map/pallas_call | solution.py:367
  51.5 0.1 collective-permute-start.18
  51.5 3.6 %collective-permute-done.5.refs_7_ = bf16[4,256,128]{2,1,0:T(8,128)(2,1)S(1)} collective-permute-done((bf16[4,256,128]{2,1,0:T(8,128)(2,1)S(1)}, bf16[4,256,128]{2,1,0:T(8,128)(2,1)S(1)}, u32[]{:S(2)}, u32[]{:S(2)}) %collective-permute-start.5) | collective-permute-done | bytes 262176 | tf_op jit(solution)/shard_map/ppermute | solution.py:419
  55.1 2.0 %shard_map.114 = (bf16[4,256,128]{2,1,0:T(8,128)(2,1)S(1)}, bf16[5,256,128]{2,1,0:T(8,128)(2,1)S(1)}, bf16[4,256,128]{2,1,0:T(8,128)(2,1)S(1)}, f32[2,8,128]{2,1,0:T(8,128)S(1)}) custom-call(s32[3]{0:T(128)S(1)} %pad_add_fusion.flags_ref, bf16[1,256,128]{2,1,0:T(8,128)(2,1)S(1)} %get-tuple-element.27.refs_0_.refs_1_.refs_14_.refs_8_.refs_9_, ...), custom_call_target="tpu_custom_call" | custom-call | flops 754974720 | bytes 4764160 | tf_op jit(solution)/shard_map/pallas_call | solution.py:367
  57.1 0.1 collective-permute-start.21
  57.2 1.3 %collective-permute-start.16 = (bf16[4,256,128]{2,1,0:T(8,128)(2,1)S(1)}, bf16[4,256,128]{2,1,0:T(8,128)(2,1)S(1)}, u32[]{:S(2)}, u32[]{:S(2)}) collective-permute-start(bf16[4,256,128]{2,1,0:T(8,128)(2,1)S(1)} %get-tuple-element.37.refs_0_.refs_4_.refs_3_), channel_id=1, source_target_pairs={{0,4},{2,6},{4,8},{6,10},{8,12},{10,14},{1,5},{3,7},{5,9},{7,11},{... | collective-permute-start | bytes 786440 | tf_op jit(solution)/shard_map/ppermute | solution.py:419
  58.5 0.1 reverse_select_fusion
  58.6 0.6 collective-permute-start.23
  59.1 1.3 %collective-permute-start.19 = (bf16[5,256,128]{2,1,0:T(8,128)(2,1)S(1)}, bf16[5,256,128]{2,1,0:T(8,128)(2,1)S(1)}, u32[]{:S(2)}, u32[]{:S(2)}) collective-permute-start(bf16[5,256,128]{2,1,0:T(8,128)(2,1)S(1)} %get-tuple-element.40.refs_3_), channel_id=1, source_target_pairs={{0,4},{2,6},{4,8},{6,10},{8,12},{10,14},{1,5},{3,7},{5,9},{7,11},{... | collective-permute-start | bytes 983048 | tf_op jit(solution)/shard_map/ppermute | solution.py:419
  60.5 0.0 collective-permute-done.21
  60.5 4.2 %collective-permute-start.17 = (bf16[4,256,128]{2,1,0:T(8,128)(2,1)S(1)}, bf16[4,256,128]{2,1,0:T(8,128)(2,1)S(1)}, u32[]{:S(2)}, u32[]{:S(2)}) collective-permute-start(bf16[4,256,128]{2,1,0:T(8,128)(2,1)S(1)} %get-tuple-element.38.refs_1_.refs_5_.refs_4_), channel_id=1, source_target_pairs={{0,4},{2,6},{4,8},{6,10},{8,12},{10,14},{1,5},{3,7},{5,9},{7,11},{... | collective-permute-start | bytes 786440 | tf_op jit(solution)/shard_map/ppermute | solution.py:419
  64.7 0.0 collective-permute-done.18.refs_0_
  64.7 0.2 collective-permute-start.22
  65.0 0.2 collective-permute-done.16.refs_0_
  65.2 0.0 collective-permute-done.23.refs_4_.refs_6_
  65.2 0.6 collective-permute-start.24
  65.8 0.0 copy-start.7
  65.8 4.3 %shard_map.115.refs_11_ = f32[9,256,256]{2,1,0:T(8,128)S(1)} custom-call(s32[3]{0:T(128)S(1)} %pad_add_fusion.flags_ref, bf16[4,256,128]{2,1,0:T(8,128)(2,1)S(1)} %get-tuple-element.37.refs_0_.refs_4_.refs_3_, bf16[4,256,128]{2,1,0:T(8,128)(2,1)S(1)} %get-tuple-element.38.refs_1_.refs_5_.refs_4_, bf16[3,256,128]{2,1,0:T(8,128)(2,1)S(1)} %get-tuple-element.39.refs_2_, ...), custom_call_target="tpu_custom_call" | custom-call | flops 2717908992 | bytes 2204672 | tf_op jit(solution)/shard_map/pallas_call | solution.py:367
  70.2 7.6 %collective-permute-done.22.refs_3_ = f32[2,8,128]{2,1,0:T(8,128)S(1)} collective-permute-done((f32[2,8,128]{2,1,0:T(8,128)S(1)}, f32[2,8,128]{2,1,0:T(8,128)S(1)}, u32[]{:S(2)}, u32[]{:S(2)}) %collective-permute-start.22) | collective-permute-done | bytes 8224 | tf_op jit(solution)/shard_map/ppermute | solution.py:419
  77.8 0.0 collective-permute-done.20.refs_2_
  77.8 4.0 %shard_map.116 = (f32[9,256,128]{2,1,0:T(8,128)S(1)}, bf16[4,128,128]{2,1,0:T(8,128)(2,1)S(1)}, f32[8,128]{1,0:T(8,128)S(1)}, bf16[1152,128]{1,0:T(8,128)(2,1)S(1)}) custom-call(s32[3]{0:T(128)S(1)} %pad_add_fusion.flags_ref, bf16[3,256,128]{2,1,0:T(8,128)(2,1)S(1)} %collective-permute-done.18.refs_0_, ...), custom_call_target="tpu_custom_call" | custom-call | flops 1358954496 | bytes 6178816 | tf_op jit(solution)/shard_map/pallas_call | solution.py:367
  81.8 0.0 collective-permute-done.24.refs_1_
  81.8 1.5 %shard_map.117.refs_7_ = bf16[4,256,128]{2,1,0:T(8,128)(2,1)S(1)} custom-call(s32[3]{0:T(128)S(1)} %pad_add_fusion.flags_ref, bf16[4,256,128]{2,1,0:T(8,128)(2,1)S(1)} %collective-permute-done.16.refs_0_, bf16[1,2,256,128]{3,2,1,0:T(8,128)(2,1)S(1)} %collective-permute-done.24.refs_1_, f32[8,128]{1,0:T(8,128)S(1)} %get-tuple-element.43.refs_2_, ...), custom_call_target="tpu_custom_call" | custom-call | flops 603979776 | bytes 3313664 | tf_op jit(solution)/shard_map/pallas_call | solution.py:367
  83.4 2.5 %shard_map.118 = (bf16[4,128,128]{2,1,0:T(8,128)(2,1)S(1)}, bf16[4,128,128]{2,1,0:T(8,128)(2,1)S(1)}) custom-call(s32[3]{0:T(128)S(1)} %pad_add_fusion.flags_ref, bf16[4,256,128]{2,1,0:T(8,128)(2,1)S(1)} %collective-permute-done.16.refs_0_, bf16[4,256,128]{2,1,0:T(8,128)(2,1)S(1)} %collective-permute-done.17.refs_1_, ...), custom_call_target="tpu_custom_call" | custom-call | flops 754974720 | bytes 4264448 | tf_op jit(solution)/shard_map/pallas_call | solution.py:367
  85.9 0.6 collective-permute-start.25
  86.5 4.8 %collective-permute-done.25 = bf16[4,128,128]{2,1,0:T(8,128)(2,1)S(1)} collective-permute-done((bf16[4,128,128]{2,1,0:T(8,128)(2,1)S(1)}, bf16[4,128,128]{2,1,0:T(8,128)(2,1)S(1)}, u32[]{:S(2)}, u32[]{:S(2)}) %collective-permute-start.25) | collective-permute-done | bytes 131104 | tf_op jit(solution)/shard_map/ppermute | solution.py:416
  91.3 0.7 maximum_select_fusion
  (27 shorter events, 0.1 us)
Async XLA Ops:
  0.0 34.3 %copy-start = (bf16[3,3,3,128,128]{4,3,2,1,0:T(8,128)(2,1)S(1)}, bf16[3,3,3,128,128]{4,3,2,1,0:T(8,128)(2,1)}, u32[]{:S(2)}) copy-start(bf16[3,3,3,128,128]{4,3,2,1,0:T(8,128)(2,1)} %refs_9_.3) | copy-start | bytes 2654212
  0.1 1.3 %copy-start.1 = (bf16[2,1,8,256,128]{4,3,2,1,0:T(8,128)(2,1)S(1)}, bf16[2,1,8,256,128]{4,3,2,1,0:T(8,128)(2,1)}, u32[]{:S(2)}) copy-start(bf16[2,1,8,256,128]{4,3,2,1,0:T(8,128)(2,1)} %param.11) | copy-start | bytes 3145732
  1.4 33.0 %copy-start.8 = (f32[128]{0:T(128)S(1)}, f32[128]{0:T(128)}, u32[]{:S(2)}) copy-start(f32[128]{0:T(128)} %param.12) | copy-start | bytes 1540
  1.4 33.0 %copy-start.9 = (f32[128]{0:T(128)S(1)}, f32[128]{0:T(128)}, u32[]{:S(2)}) copy-start(f32[128]{0:T(128)} %param.13) | copy-start | bytes 1540
  2.0 38.5 %collective-permute-start.10 = (bf16[7,256,128]{2,1,0:T(8,128)(2,1)S(1)}, bf16[7,256,128]{2,1,0:T(8,128)(2,1)S(1)}, u32[]{:S(2)}, u32[]{:S(2)}) collective-permute-start(bf16[7,256,128]{2,1,0:T(8,128)(2,1)S(1)} %get-tuple-element.28.refs_1_.refs_2_.refs_15_.refs_9_.refs_10_), channel_id=1, source_target_pairs={{0,4},{2,6},{4,8},{6,10},{8,12},{10,14},{12,0},{14,2},{1,5},{3,7},... | collective-permute-start | bytes 1376264 | tf_op jit(solution)/shard_map/ppermute | solution.py:419
  5.1 35.3 %collective-permute-start.2 = (bf16[4,256,128]{2,1,0:T(8,128)(2,1)S(1)}, bf16[4,256,128]{2,1,0:T(8,128)(2,1)S(1)}, u32[]{:S(2)}, u32[]{:S(2)}) collective-permute-start(bf16[4,256,128]{2,1,0:T(8,128)(2,1)S(1)} %get-tuple-element.31.refs_4_), channel_id=1, source_target_pairs={{0,2},{2,0},{4,6},{6,4},{8,10},{10,8},{12,14},{14,12},{1,3},{3,1},... | collective-permute-start | bytes 786440 | tf_op jit(solution)/shard_map/ppermute | solution.py:416
  6.6 21.3 %collective-permute-start.6 = (bf16[1,256,128]{2,1,0:T(8,128)(2,1)S(1)}, bf16[1,256,128]{2,1,0:T(8,128)(2,1)S(1)}, u32[]{:S(2)}, u32[]{:S(2)}) collective-permute-start(bf16[1,256,128]{2,1,0:T(8,128)(2,1)S(1)} %get-tuple-element.27.refs_0_.refs_1_.refs_14_.refs_8_.refs_9_), channel_id=1, source_target_pairs={{0,1},{1,0},{2,3},{3,2},{4,5},{5,4},{6,7},{7,6},{8,9},{9,8},{10,11... | collective-permute-start | bytes 196616 | tf_op jit(solution)/shard_map/ppermute | solution.py:425
  6.6 21.3 %collective-permute-start = (bf16[1,256,128]{2,1,0:T(8,128)(2,1)S(1)}, bf16[1,256,128]{2,1,0:T(8,128)(2,1)S(1)}, u32[]{:S(2)}, u32[]{:S(2)}) collective-permute-start(bf16[1,256,128]{2,1,0:T(8,128)(2,1)S(1)} %get-tuple-element.29.refs_2_), channel_id=1, source_target_pairs={{0,2},{2,0},{4,6},{6,4},{8,10},{10,8},{12,14},{14,12},{1,3},{3,1},... | collective-permute-start | bytes 196616 | tf_op jit(solution)/shard_map/ppermute | solution.py:416
  8.0 1.2 %collective-permute-start.11 = (f32[2,8,128]{2,1,0:T(8,128)S(1)}, f32[2,8,128]{2,1,0:T(8,128)S(1)}, u32[]{:S(2)}, u32[]{:S(2)}) collective-permute-start(f32[2,8,128]{2,1,0:T(8,128)S(1)} %shard_map.110), channel_id=1, source_target_pairs={{0,1},{1,0},{2,3},{3,2},{4,5},{5,4},{6,7},{7,6},{8,9},{9,8},{10,11... | collective-permute-start | bytes 24584 | tf_op jit(solution)/shard_map/ppermute | solution.py:425
  9.2 5.2 %collective-permute-start.12 = (f32[2,8,128]{2,1,0:T(8,128)S(1)}, f32[2,8,128]{2,1,0:T(8,128)S(1)}, u32[]{:S(2)}, u32[]{:S(2)}) collective-permute-start(f32[2,8,128]{2,1,0:T(8,128)S(1)} %add.11.refs_3_.refs_10_), channel_id=1, source_target_pairs={{0,2},{2,0},{4,6},{6,4},{8,10},{10,8},{12,14},{14,12},{1,3},{3,1},... | collective-permute-start | bytes 24584 | tf_op jit(solution)/shard_map/ppermute | solution.py:416
  14.4 5.4 %collective-permute-start.13 = (f32[2,8,128]{2,1,0:T(8,128)S(1)}, f32[2,8,128]{2,1,0:T(8,128)S(1)}, u32[]{:S(2)}, u32[]{:S(2)}) collective-permute-start(f32[2,8,128]{2,1,0:T(8,128)S(1)} %add.11.refs_3_.refs_10_), channel_id=1, source_target_pairs={{0,4},{2,6},{4,8},{6,10},{8,12},{10,14},{12,0},{14,2},{1,5},{3,7},... | collective-permute-start | bytes 24584 | tf_op jit(solution)/shard_map/ppermute | solution.py:419
  19.9 6.5 %collective-permute-start.14 = (f32[2,8,128]{2,1,0:T(8,128)S(1)}, f32[2,8,128]{2,1,0:T(8,128)S(1)}, u32[]{:S(2)}, u32[]{:S(2)}) collective-permute-start(f32[2,8,128]{2,1,0:T(8,128)S(1)} %add.11.refs_3_.refs_10_), channel_id=1, source_target_pairs={{0,6},{2,4},{4,10},{6,8},{8,14},{10,12},{12,2},{14,0},{1,7},{3,5},... | collective-permute-start | bytes 24584 | tf_op jit(solution)/shard_map/ppermute | solution.py:422
  26.4 14.0 %collective-permute-start.1 = (bf16[3,256,128]{2,1,0:T(8,128)(2,1)S(1)}, bf16[3,256,128]{2,1,0:T(8,128)(2,1)S(1)}, u32[]{:S(2)}, u32[]{:S(2)}) collective-permute-start(bf16[3,256,128]{2,1,0:T(8,128)(2,1)S(1)} %get-tuple-element.30.refs_3_), channel_id=1, source_target_pairs={{0,2},{2,0},{4,6},{6,4},{8,10},{10,8},{12,14},{14,12},{1,3},{3,1},... | collective-permute-start | bytes 589832 | tf_op jit(solution)/shard_map/ppermute | solution.py:416
  27.9 6.4 %collective-permute-start.8 = (bf16[1,256,128]{2,1,0:T(8,128)(2,1)S(1)}, bf16[1,256,128]{2,1,0:T(8,128)(2,1)S(1)}, u32[]{:S(2)}, u32[]{:S(2)}) collective-permute-start(bf16[1,256,128]{2,1,0:T(8,128)(2,1)S(1)} %get-tuple-element.27.refs_0_.refs_1_.refs_14_.refs_8_.refs_9_), channel_id=1, source_target_pairs={{0,4},{2,6},{4,8},{6,10},{8,12},{10,14},{12,0},{14,2},{1,5},{3,7},... | collective-permute-start | bytes 196616 | tf_op jit(solution)/shard_map/ppermute | solution.py:419
  27.9 6.4 %collective-permute-start.7 = (bf16[1,256,128]{2,1,0:T(8,128)(2,1)S(1)}, bf16[1,256,128]{2,1,0:T(8,128)(2,1)S(1)}, u32[]{:S(2)}, u32[]{:S(2)}) collective-permute-start(bf16[1,256,128]{2,1,0:T(8,128)(2,1)S(1)} %collective-permute-done.refs_4_.refs_3_.refs_2_.refs_17_.refs_11_), channel_id=1, source_target_pairs={{0,1},{1,0},{2,3},{3,2},{4,5},{5,4},{6,7},{7,6},{8,9},{9,8},{10,11... | collective-permute-start | bytes 196616 | tf_op jit(solution)/shard_map/ppermute | solution.py:425
  34.3 6.1 %collective-permute-start.3 = (bf16[1,256,128]{2,1,0:T(8,128)(2,1)S(1)}, bf16[1,256,128]{2,1,0:T(8,128)(2,1)S(1)}, u32[]{:S(2)}, u32[]{:S(2)}) collective-permute-start(bf16[1,256,128]{2,1,0:T(8,128)(2,1)S(1)} %collective-permute-done.refs_4_.refs_3_.refs_2_.refs_17_.refs_11_), channel_id=1, source_target_pairs={{0,4},{2,6},{4,8},{6,10},{8,12},{10,14},{12,0},{14,2},{1,5},{3,7},... | collective-permute-start | bytes 196616 | tf_op jit(solution)/shard_map/ppermute | solution.py:419
  34.3 6.2 %collective-permute-start.9 = (bf16[1,256,128]{2,1,0:T(8,128)(2,1)S(1)}, bf16[1,256,128]{2,1,0:T(8,128)(2,1)S(1)}, u32[]{:S(2)}, u32[]{:S(2)}) collective-permute-start(bf16[1,256,128]{2,1,0:T(8,128)(2,1)S(1)} %collective-permute-done.8.refs_8_), channel_id=1, source_target_pairs={{0,1},{1,0},{2,3},{3,2},{4,5},{5,4},{6,7},{7,6},{8,9},{9,8},{10,11... | collective-permute-start | bytes 196616 | tf_op jit(solution)/shard_map/ppermute | solution.py:425
  36.9 13.0 %copy-start.4 = (f32[128]{0:T(128)S(1)}, f32[128]{0:T(128)}, u32[]{:S(2)}) copy-start(f32[128]{0:T(128)} %param.15) | copy-start | bytes 1540
  40.4 4.3 %collective-permute-start.15 = (bf16[1,256,128]{2,1,0:T(8,128)(2,1)S(1)}, bf16[1,256,128]{2,1,0:T(8,128)(2,1)S(1)}, u32[]{:S(2)}, u32[]{:S(2)}) collective-permute-start(bf16[1,256,128]{2,1,0:T(8,128)(2,1)S(1)} %collective-permute-done.3.refs_6_.refs_5_), channel_id=1, source_target_pairs={{0,1},{1,0},{2,3},{3,2},{4,5},{5,4},{6,7},{7,6},{8,9},{9,8},{10,11... | collective-permute-start | bytes 196616 | tf_op jit(solution)/shard_map/ppermute | solution.py:425
  40.4 9.6 %collective-permute-start.4 = (bf16[3,256,128]{2,1,0:T(8,128)(2,1)S(1)}, bf16[3,256,128]{2,1,0:T(8,128)(2,1)S(1)}, u32[]{:S(2)}, u32[]{:S(2)}) collective-permute-start(bf16[3,256,128]{2,1,0:T(8,128)(2,1)S(1)} %collective-permute-done.1.refs_5_.refs_4_.refs_3_.refs_18_.refs_12_), channel_id=1, source_target_pairs={{0,4},{2,6},{4,8},{6,10},{8,12},{10,14},{12,0},{14,2},{1,5},{3,7},... | collective-permute-start | bytes 589832 | tf_op jit(solution)/shard_map/ppermute | solution.py:419
  40.4 14.7 %collective-permute-start.5 = (bf16[4,256,128]{2,1,0:T(8,128)(2,1)S(1)}, bf16[4,256,128]{2,1,0:T(8,128)(2,1)S(1)}, u32[]{:S(2)}, u32[]{:S(2)}) collective-permute-start(bf16[4,256,128]{2,1,0:T(8,128)(2,1)S(1)} %collective-permute-done.2.refs_6_.refs_4_.refs_19_.refs_13_), channel_id=1, source_target_pairs={{0,4},{2,6},{4,8},{6,10},{8,12},{10,14},{12,0},{14,2},{1,5},{3,7},... | collective-permute-start | bytes 786440 | tf_op jit(solution)/shard_map/ppermute | solution.py:419
  51.5 13.2 %collective-permute-start.18 = (bf16[3,256,128]{2,1,0:T(8,128)(2,1)S(1)}, bf16[3,256,128]{2,1,0:T(8,128)(2,1)S(1)}, u32[]{:S(2)}, u32[]{:S(2)}) collective-permute-start(bf16[3,256,128]{2,1,0:T(8,128)(2,1)S(1)} %get-tuple-element.39.refs_2_), channel_id=1, source_target_pairs={{0,4},{2,6},{4,8},{6,10},{8,12},{10,14},{12,0},{14,2},{1,5},{3,7},... | collective-permute-start | bytes 589832 | tf_op jit(solution)/shard_map/ppermute | solution.py:419
  55.1 3.4 %copy-start.10 = (bf16[3,3,128,128]{3,2,1,0:T(8,128)(2,1)S(1)}, bf16[3,3,128,128]{3,2,1,0:T(8,128)(2,1)}, u32[]{:S(2)}) copy-start(bf16[3,3,128,128]{3,2,1,0:T(8,128)(2,1)} %param.20) | copy-start | bytes 884740
  55.1 10.7 %copy-start.2 = (bf16[3,3,3,128,128]{4,3,2,1,0:T(8,128)(2,1)S(1)}, bf16[3,3,3,128,128]{4,3,2,1,0:T(8,128)(2,1)}, u32[]{:S(2)}) copy-start(bf16[3,3,3,128,128]{4,3,2,1,0:T(8,128)(2,1)} %refs_10_.1) | copy-start | bytes 2654212
  55.1 10.7 %copy-start.5 = (f32[128]{0:T(128)S(1)}, f32[128]{0:T(128)}, u32[]{:S(2)}) copy-start(f32[128]{0:T(128)} %param.16) | copy-start | bytes 1540
  55.1 10.7 %copy-start.6 = (f32[128]{0:T(128)S(1)}, f32[128]{0:T(128)}, u32[]{:S(2)}) copy-start(f32[128]{0:T(128)} %param.17) | copy-start | bytes 1540
  57.1 3.3 %collective-permute-start.21 = (f32[2,8,128]{2,1,0:T(8,128)S(1)}, f32[2,8,128]{2,1,0:T(8,128)S(1)}, u32[]{:S(2)}, u32[]{:S(2)}) collective-permute-start(f32[2,8,128]{2,1,0:T(8,128)S(1)} %get-tuple-element.41), channel_id=1, source_target_pairs={{0,1},{1,0},{2,3},{3,2},{4,5},{5,4},{6,7},{7,6},{8,9},{9,8},{10,11... | collective-permute-start | bytes 24584 | tf_op jit(solution)/shard_map/ppermute | solution.py:425
  57.2 8.0 %collective-permute-start.16 = (bf16[4,256,128]{2,1,0:T(8,128)(2,1)S(1)}, bf16[4,256,128]{2,1,0:T(8,128)(2,1)S(1)}, u32[]{:S(2)}, u32[]{:S(2)}) collective-permute-start(bf16[4,256,128]{2,1,0:T(8,128)(2,1)S(1)} %get-tuple-element.37.refs_0_.refs_4_.refs_3_), channel_id=1, source_target_pairs={{0,4},{2,6},{4,8},{6,10},{8,12},{10,14},{1,5},{3,7},{5,9},{7,11},{... | collective-permute-start | bytes 786440 | tf_op jit(solution)/shard_map/ppermute | solution.py:419
  58.6 6.6 %collective-permute-start.23 = (bf16[2,2,256,128]{3,2,1,0:T(8,128)(2,1)S(1)}, bf16[2,2,256,128]{3,2,1,0:T(8,128)(2,1)S(1)}, u32[]{:S(2)}, u32[]{:S(2)}) collective-permute-start(bf16[2,2,256,128]{3,2,1,0:T(8,128)(2,1)S(1)} %get-tuple-element.42), channel_id=1, source_target_pairs={{0,1},{1,0},{2,3},{3,2},{4,5},{5,4},{6,7},{7,6},{8,9},{9,8},{10,11... | collective-permute-start | bytes 786440 | tf_op jit(solution)/shard_map/ppermute | solution.py:425
  59.1 18.7 %collective-permute-start.19 = (bf16[5,256,128]{2,1,0:T(8,128)(2,1)S(1)}, bf16[5,256,128]{2,1,0:T(8,128)(2,1)S(1)}, u32[]{:S(2)}, u32[]{:S(2)}) collective-permute-start(bf16[5,256,128]{2,1,0:T(8,128)(2,1)S(1)} %get-tuple-element.40.refs_3_), channel_id=1, source_target_pairs={{0,4},{2,6},{4,8},{6,10},{8,12},{10,14},{1,5},{3,7},{5,9},{7,11},{... | collective-permute-start | bytes 983048 | tf_op jit(solution)/shard_map/ppermute | solution.py:419
  60.5 22.9 %collective-permute-start.17 = (bf16[4,256,128]{2,1,0:T(8,128)(2,1)S(1)}, bf16[4,256,128]{2,1,0:T(8,128)(2,1)S(1)}, u32[]{:S(2)}, u32[]{:S(2)}) collective-permute-start(bf16[4,256,128]{2,1,0:T(8,128)(2,1)S(1)} %get-tuple-element.38.refs_1_.refs_5_.refs_4_), channel_id=1, source_target_pairs={{0,4},{2,6},{4,8},{6,10},{8,12},{10,14},{1,5},{3,7},{5,9},{7,11},{... | collective-permute-start | bytes 786440 | tf_op jit(solution)/shard_map/ppermute | solution.py:419
  64.7 13.1 %collective-permute-start.22 = (f32[2,8,128]{2,1,0:T(8,128)S(1)}, f32[2,8,128]{2,1,0:T(8,128)S(1)}, u32[]{:S(2)}, u32[]{:S(2)}) collective-permute-start(f32[2,8,128]{2,1,0:T(8,128)S(1)} %add.12.refs_5_.refs_7_), channel_id=1, source_target_pairs={{0,4},{2,6},{4,8},{6,10},{8,12},{10,14},{12,0},{14,2},{1,5},{3,7},... | collective-permute-start | bytes 24584 | tf_op jit(solution)/shard_map/ppermute | solution.py:419
  65.2 12.6 %collective-permute-start.20 = (bf16[1,2,256,128]{3,2,1,0:T(8,128)(2,1)S(1)}, bf16[1,2,256,128]{3,2,1,0:T(8,128)(2,1)S(1)}, u32[]{:S(2)}, u32[]{:S(2)}) collective-permute-start(bf16[1,2,256,128]{3,2,1,0:T(8,128)(2,1)S(1)} %slice_bitcast_fusion.1), channel_id=1, source_target_pairs={{0,1},{1,0},{2,3},{3,2},{4,5},{5,4},{6,7},{7,6},{8,9},{9,8},{10,11... | collective-permute-start | bytes 393224 | tf_op jit(solution)/shard_map/ppermute | solution.py:425
  65.2 16.6 %collective-permute-start.24 = (bf16[1,2,256,128]{3,2,1,0:T(8,128)(2,1)S(1)}, bf16[1,2,256,128]{3,2,1,0:T(8,128)(2,1)S(1)}, u32[]{:S(2)}, u32[]{:S(2)}) collective-permute-start(bf16[1,2,256,128]{3,2,1,0:T(8,128)(2,1)S(1)} %slice_bitcast_fusion), channel_id=1, source_target_pairs={{0,1},{1,0},{2,3},{3,2},{4,5},{5,4},{6,7},{7,6},{8,9},{9,8},{10,11... | collective-permute-start | bytes 393224 | tf_op jit(solution)/shard_map/ppermute | solution.py:425
  65.8 12.0 %copy-start.3 = (f32[128]{0:T(128)S(1)}, f32[128]{0:T(128)}, u32[]{:S(2)}) copy-start(f32[128]{0:T(128)} %param.21) | copy-start | bytes 1540
  65.8 12.0 %copy-start.7 = (f32[128]{0:T(128)S(1)}, f32[128]{0:T(128)}, u32[]{:S(2)}) copy-start(f32[128]{0:T(128)} %param.19) | copy-start | bytes 1540
  85.9 5.4 %collective-permute-start.25 = (bf16[4,128,128]{2,1,0:T(8,128)(2,1)S(1)}, bf16[4,128,128]{2,1,0:T(8,128)(2,1)S(1)}, u32[]{:S(2)}, u32[]{:S(2)}) collective-permute-start(bf16[4,128,128]{2,1,0:T(8,128)(2,1)S(1)} %get-tuple-element.48), channel_id=1, source_target_pairs={{0,2},{2,0},{4,6},{6,4},{8,10},{10,8},{12,14},{14,12},{1,3},{3,1},... | collective-permute-start | bytes 393224 | tf_op jit(solution)/shard_map/ppermute | solution.py:416

commit v2 on v1

--- a/solution.py
+++ b/solution.py
@@ -443,7 +443,7 @@
         return call(functools.partial(body, cells), *rest, **options)
 
     split = near + 1
-    sizes = (1, height - 1, 1, split - 1, height - split)
+    sizes = (1, height - 1, split, height - split)
     parts = call(place_kernel, [shape(n, width, channels) for n in sizes], [], flags, x)
     own, other = tuple(parts[:2]), tuple(parts[2:])
     past = later(own[0], "own_on0"), later(own[1], "own_on1")
@@ -453,9 +453,11 @@
     own_on_total = later(totals, "own_sums")
     cross_total = crossed(totals, "cross_sums")
     mate_total = swapped(totals)
+    mate_on = tuple(
+        later(v, f"mate_on{k}") for k, v in enumerate((mate[0][:1], mate[0][1:], mate[1]))
+    )
     own = (beside(own[0]), *own)
-    mate_on = tuple(later(v, f"mate_on{k}") for k, v in enumerate(mate))
-    mate = (beside(mate[0]), *mate)
+    mate = (beside(mate[0][:1]), *mate)
     past = (beside(past[0]), *past)
 
     norm_one = (row(gain_one), row(norm_bias_one))
@@ -501,7 +503,7 @@
         stack(near + 2) + laid(2),
         flags,
         (fall_edges, *own[1:]),
-        mate[1:3],
+        mate[1:2],
         (cross_edge, *mate_on[:2]),
         cross_params,
         kernel_one,
@@ -591,7 +593,7 @@
         w_a_on,
         acc,
         own,
-        mate[:3],
+        mate[:2],
         flops=flops(ready, 1),
     )
     sent, kept = kernel(

time: 92.2 us -> 81.2 us (0.88)
  waiting for transfers between devices: 45.5 us -> 28.1 us
  starting transfers between devices: 19.8 us -> 26.2 us
    ppermute x11, waiting for transfers between devices: 30.3 us -> 14.8 us  [later(): return lax.ppermute(v, 'tm', onward(name, 0))]
    ppermute x11, starting transfers between devices: 11.9 us -> 17.2 us  [later(): return lax.ppermute(v, 'tm', onward(name, 0))]
    ppermute x1, waiting for transfers between devices: 5.72 us -> 1.92 us  [crossed(): return lax.ppermute(v, 'tm', onward(name, 1))]
    ppermute x1, starting transfers between devices: 0.73 us -> 2.58 us  [crossed(): return lax.ppermute(v, 'tm', onward(name, 1))]
    ppermute x5 -> x4, waiting for transfers between devices: 8.53 us -> 10.2 us  [swapped(): return lax.ppermute(v, 'tm', swap)]
    ppermute x5 -> x4, starting transfers between devices: 5.64 us -> 5.13 us  [swapped(): return lax.ppermute(v, 'tm', swap)]
  transfers between devices with their start and end apart: 26 -> 25, of which waited for: 11 -> 9; matrix products, arithmetic and copies ran while one was open for 0% -> 0% of each run, Pallas kernels for 23% -> 26%
where the time goes in v2:
time: 81.2 us; the launch traced here: 81 us
  waiting for transfers between devices  28.1 us (35%)
  starting transfers between devices  26.2 us (32%)
  Pallas kernels  24.2 us (30%)
  local copies, waits for them, and re-layouts  1.37 us (2%)
  other arithmetic  0.86 us (1%)
    pallas_call x10, Pallas kernels, call(): pl.pallas_call(kernel, out_shape=out_shape, in_specs=[pl.BlockSpec(memory...  24.2 us
    ppermute x11, starting transfers between devices, later(): return lax.ppermute(v, 'tm', onward(name, 0))  17.2 us
    ppermute x11, waiting for transfers between devices, later(): return lax.ppermute(v, 'tm', onward(name, 0))  14.8 us
    ppermute x4, waiting for transfers between devices, swapped(): return lax.ppermute(v, 'tm', swap)  10.2 us
    ppermute x4, starting transfers between devices, swapped(): return lax.ppermute(v, 'tm', swap)  5.13 us
    ppermute x1, starting transfers between devices, crossed(): return lax.ppermute(v, 'tm', onward(name, 1))  2.58 us
    ppermute x1, waiting for transfers between devices, crossed(): return lax.ppermute(v, 'tm', onward(name, 1))  1.92 us
  transfers between devices with their start and end apart: 25, of which 9 were waited for; matrix products, arithmetic and copies ran while one was open for 0% of the time, Pallas kernels for 26%

profile of v2, /device:TPU:0, one launch (start us, length us, event | category | flops | bytes accessed | tf_op | source)
XLA Modules:
  0.0 81.0 jit_solution(16783355342514749274)
XLA Ops:
  0.0 0.1 pad_add_fusion.flags_ref
  0.1 1.3 %copy-done.1 = bf16[2,1,8,256,128]{4,3,2,1,0:T(8,128)(2,1)S(1)} copy-done((bf16[2,1,8,256,128]{4,3,2,1,0:T(8,128)(2,1)S(1)}, bf16[2,1,8,256,128]{4,3,2,1,0:T(8,128)(2,1)}, u32[]{:S(2)}) %copy-start.1) | copy-done | bytes 1048600
  1.4 0.6 shard_map.109
  2.0 3.1 %collective-permute-start.9 = (bf16[7,256,128]{2,1,0:T(8,128)(2,1)S(1)}, bf16[7,256,128]{2,1,0:T(8,128)(2,1)S(1)}, u32[]{:S(2)}, u32[]{:S(2)}) collective-permute-start(bf16[7,256,128]{2,1,0:T(8,128)(2,1)S(1)} %get-tuple-element.27.refs_1_.refs_2_.refs_15_.refs_9_.refs_10_), channel_id=1, source_target_pairs={{0,4},{2,6},{4,8},{6,10},{8,12},{10,14},{12,0},{14,2},{1,5},{3,7},... | collective-permute-start | bytes 1376264 | tf_op jit(solution)/shard_map/ppermute | solution.py:419
  5.1 1.5 %collective-permute-start = (bf16[4,256,128]{2,1,0:T(8,128)(2,1)S(1)}, bf16[4,256,128]{2,1,0:T(8,128)(2,1)S(1)}, u32[]{:S(2)}, u32[]{:S(2)}) collective-permute-start(bf16[4,256,128]{2,1,0:T(8,128)(2,1)S(1)} %get-tuple-element.28.refs_2_), channel_id=1, source_target_pairs={{0,2},{2,0},{4,6},{6,4},{8,10},{10,8},{12,14},{14,12},{1,3},{3,1},... | collective-permute-start | bytes 786440 | tf_op jit(solution)/shard_map/ppermute | solution.py:416
  6.6 0.5 collective-permute-start.1
  7.1 0.8 %shard_map.110 = f32[2,8,128]{2,1,0:T(8,128)S(1)} custom-call(s32[3]{0:T(128)S(1)} %pad_add_fusion.flags_ref, bf16[1,256,128]{2,1,0:T(8,128)(2,1)S(1)} %get-tuple-element.26.refs_0_.refs_1_.refs_14_.refs_8_.refs_9_, bf16[7,256,128]{2,1,0:T(8,128)(2,1)S(1)} %get-tuple-element.27.refs_1_.refs_2_.refs_15_.refs_9_.refs_10_, ...), custom_call_target="tpu_custom_call" | custom-call | bytes 1048576 | tf_op jit(solution)/shard_map/pallas_call | solution.py:367
  8.0 0.1 collective-permute-start.10
  8.0 1.2 %collective-permute-done.10 = f32[2,8,128]{2,1,0:T(8,128)S(1)} collective-permute-done((f32[2,8,128]{2,1,0:T(8,128)S(1)}, f32[2,8,128]{2,1,0:T(8,128)S(1)}, u32[]{:S(2)}, u32[]{:S(2)}) %collective-permute-start.10) | collective-permute-done | bytes 8224 | tf_op jit(solution)/shard_map/ppermute | solution.py:425
  9.2 1.5 %collective-permute-start.11 = (f32[2,8,128]{2,1,0:T(8,128)S(1)}, f32[2,8,128]{2,1,0:T(8,128)S(1)}, u32[]{:S(2)}, u32[]{:S(2)}) collective-permute-start(f32[2,8,128]{2,1,0:T(8,128)S(1)} %add.11.refs_3_.refs_9_), channel_id=1, source_target_pairs={{0,2},{2,0},{4,6},{6,4},{8,10},{10,8},{12,14},{14,12},{1,3},{3,1},... | collective-permute-start | bytes 24584 | tf_op jit(solution)/shard_map/ppermute | solution.py:416
  10.7 1.6 %collective-permute-start.12 = (f32[2,8,128]{2,1,0:T(8,128)S(1)}, f32[2,8,128]{2,1,0:T(8,128)S(1)}, u32[]{:S(2)}, u32[]{:S(2)}) collective-permute-start(f32[2,8,128]{2,1,0:T(8,128)S(1)} %add.11.refs_3_.refs_9_), channel_id=1, source_target_pairs={{0,4},{2,6},{4,8},{6,10},{8,12},{10,14},{12,0},{14,2},{1,5},{3,7},... | collective-permute-start | bytes 24584 | tf_op jit(solution)/shard_map/ppermute | solution.py:419
  12.3 6.4 %collective-permute-done.11.refs_10_ = f32[2,8,128]{2,1,0:T(8,128)S(1)} collective-permute-done((f32[2,8,128]{2,1,0:T(8,128)S(1)}, f32[2,8,128]{2,1,0:T(8,128)S(1)}, u32[]{:S(2)}, u32[]{:S(2)}) %collective-permute-start.11) | collective-permute-done | bytes 8224 | tf_op jit(solution)/shard_map/ppermute | solution.py:416
  18.7 1.6 %collective-permute-start.7 = (bf16[1,256,128]{2,1,0:T(8,128)(2,1)S(1)}, bf16[1,256,128]{2,1,0:T(8,128)(2,1)S(1)}, u32[]{:S(2)}, u32[]{:S(2)}) collective-permute-start(bf16[1,256,128]{2,1,0:T(8,128)(2,1)S(1)} %get-tuple-element.26.refs_0_.refs_1_.refs_14_.refs_8_.refs_9_), channel_id=1, source_target_pairs={{0,4},{2,6},{4,8},{6,10},{8,12},{10,14},{12,0},{14,2},{1,5},{3,7},... | collective-permute-start | bytes 196616 | tf_op jit(solution)/shard_map/ppermute | solution.py:419
  20.2 0.0 collective-permute-done.12.refs_11_
  20.2 0.0 collective-permute-start.5
  20.2 0.0 collective-permute-done.refs_4_.refs_3_.refs_2_.refs_17_.refs_11_
  20.3 2.6 %collective-permute-start.13 = (f32[2,8,128]{2,1,0:T(8,128)S(1)}, f32[2,8,128]{2,1,0:T(8,128)S(1)}, u32[]{:S(2)}, u32[]{:S(2)}) collective-permute-start(f32[2,8,128]{2,1,0:T(8,128)S(1)} %add.11.refs_3_.refs_9_), channel_id=1, source_target_pairs={{0,6},{2,4},{4,10},{6,8},{8,14},{10,12},{12,2},{14,0},{1,7},{3,5},... | collective-permute-start | bytes 24584 | tf_op jit(solution)/shard_map/ppermute | solution.py:422
  22.8 1.9 %collective-permute-done.7.refs_7_ = bf16[1,256,128]{2,1,0:T(8,128)(2,1)S(1)} collective-permute-done((bf16[1,256,128]{2,1,0:T(8,128)(2,1)S(1)}, bf16[1,256,128]{2,1,0:T(8,128)(2,1)S(1)}, u32[]{:S(2)}, u32[]{:S(2)}) %collective-permute-start.7) | collective-permute-done | bytes 65568 | tf_op jit(solution)/shard_map/ppermute | solution.py:419
  24.7 0.0 collective-permute-start.8
  24.7 1.9 %collective-permute-done.13.refs_12_ = f32[2,8,128]{2,1,0:T(8,128)S(1)} collective-permute-done((f32[2,8,128]{2,1,0:T(8,128)S(1)}, f32[2,8,128]{2,1,0:T(8,128)S(1)}, u32[]{:S(2)}, u32[]{:S(2)}) %collective-permute-start.13) | collective-permute-done | bytes 8224 | tf_op jit(solution)/shard_map/ppermute | solution.py:422
  26.7 0.0 collective-permute-start.6
  26.7 0.0 collective-permute-done.5.refs_0_.refs_13_.refs_7_
  26.7 0.0 collective-permute-start.2
  26.7 2.6 %shard_map.111.refs_16_ = f32[8,256,256]{2,1,0:T(8,128)S(1)} custom-call(s32[3]{0:T(128)S(1)} %pad_add_fusion.flags_ref, bf16[1,256,128]{2,1,0:T(8,128)(2,1)S(1)} %collective-permute-done.5.refs_0_.refs_13_.refs_7_, bf16[1,256,128]{2,1,0:T(8,128)(2,1)S(1)} %get-tuple-element.26.refs_0_.refs_1_.refs_14_.refs_8_.refs_9_, ...), custom_call_target="tpu_custom_call" | custom-call | flops 1207959552 | bytes 1483776 | tf_op jit(solution)/shard_map/pallas_call | solution.py:367
  29.3 0.0 copy-start.4
  29.3 0.0 collective-permute-done.8.refs_6_
  29.3 0.5 collective-permute-start.3
  29.8 0.0 collective-permute-done.1.refs_5_.refs_3_.refs_18_.refs_12_
  29.8 1.1 %collective-permute-start.4 = (bf16[4,256,128]{2,1,0:T(8,128)(2,1)S(1)}, bf16[4,256,128]{2,1,0:T(8,128)(2,1)S(1)}, u32[]{:S(2)}, u32[]{:S(2)}) collective-permute-start(bf16[4,256,128]{2,1,0:T(8,128)(2,1)S(1)} %collective-permute-done.1.refs_5_.refs_3_.refs_18_.refs_12_), channel_id=1, source_target_pairs={{0,4},{2,6},{4,8},{6,10},{8,12},{10,14},{12,0},{14,2},{1,5},{3,7},... | collective-permute-start | bytes 786440 | tf_op jit(solution)/shard_map/ppermute | solution.py:419
  30.9 2.0 %collective-permute-done.2.refs_5_.refs_4_ = bf16[1,256,128]{2,1,0:T(8,128)(2,1)S(1)} collective-permute-done((bf16[1,256,128]{2,1,0:T(8,128)(2,1)S(1)}, bf16[1,256,128]{2,1,0:T(8,128)(2,1)S(1)}, u32[]{:S(2)}, u32[]{:S(2)}) %collective-permute-start.2) | collective-permute-done | bytes 65568 | tf_op jit(solution)/shard_map/ppermute | solution.py:419
  33.0 0.0 collective-permute-start.14
  33.0 0.0 collective-permute-done.6.refs_3_.refs_16_.refs_10_
  33.0 0.0 collective-permute-done.9.refs_8_
  33.0 4.2 %shard_map.112 = (f32[8,256,256]{2,1,0:T(8,128)S(1)}, f32[8,128]{1,0:T(8,128)S(1)}, bf16[2,256,128]{2,1,0:T(8,128)(2,1)S(1)}) custom-call(s32[3]{0:T(128)S(1)} %pad_add_fusion.flags_ref, bf16[1,256,128]{2,1,0:T(8,128)(2,1)S(1)} %collective-permute-done.5.refs_0_.refs_13_.refs_7_, ...), custom_call_target="tpu_custom_call" | custom-call | flops 2415919104 | bytes 4785152 | tf_op jit(solution)/shard_map/pallas_call | solution.py:367
  37.1 0.0 collective-permute-done.14.refs_4_
  37.2 1.8 %collective-permute-done.3.refs_6_.refs_5_ = bf16[3,256,128]{2,1,0:T(8,128)(2,1)S(1)} collective-permute-done((bf16[3,256,128]{2,1,0:T(8,128)(2,1)S(1)}, bf16[3,256,128]{2,1,0:T(8,128)(2,1)S(1)}, u32[]{:S(2)}, u32[]{:S(2)}) %collective-permute-start.3) | collective-permute-done | bytes 196640 | tf_op jit(solution)/shard_map/ppermute | solution.py:419
  39.0 1.5 %shard_map.113 = (bf16[3,256,128]{2,1,0:T(8,128)(2,1)S(1)}, bf16[3,256,128]{2,1,0:T(8,128)(2,1)S(1)}, bf16[2,2,256,128]{3,2,1,0:T(8,128)(2,1)S(1)}, f32[2,8,128]{2,1,0:T(8,128)S(1)}) custom-call(s32[3]{0:T(128)S(1)} %pad_add_fusion.flags_ref, bf16[2,256,128]{2,1,0:T(8,128)(2,1)S(1)} %get-tuple-element.32.refs_0_, ...), custom_call_target="tpu_custom_call" | custom-call | flops 452984832 | bytes 4231680 | tf_op jit(solution)/shard_map/pallas_call | solution.py:367
  40.5 0.1 collective-permute-start.17
  40.6 3.6 %collective-permute-done.4.refs_6_ = bf16[4,256,128]{2,1,0:T(8,128)(2,1)S(1)} collective-permute-done((bf16[4,256,128]{2,1,0:T(8,128)(2,1)S(1)}, bf16[4,256,128]{2,1,0:T(8,128)(2,1)S(1)}, u32[]{:S(2)}, u32[]{:S(2)}) %collective-permute-start.4) | collective-permute-done | bytes 262176 | tf_op jit(solution)/shard_map/ppermute | solution.py:419
  44.1 2.0 %shard_map.114 = (bf16[4,256,128]{2,1,0:T(8,128)(2,1)S(1)}, bf16[5,256,128]{2,1,0:T(8,128)(2,1)S(1)}, bf16[4,256,128]{2,1,0:T(8,128)(2,1)S(1)}, f32[2,8,128]{2,1,0:T(8,128)S(1)}) custom-call(s32[3]{0:T(128)S(1)} %pad_add_fusion.flags_ref, bf16[1,256,128]{2,1,0:T(8,128)(2,1)S(1)} %get-tuple-element.26.refs_0_.refs_1_.refs_14_.refs_8_.refs_9_, ...), custom_call_target="tpu_custom_call" | custom-call | flops 754974720 | bytes 4764160 | tf_op jit(solution)/shard_map/pallas_call | solution.py:367
  46.2 0.1 collective-permute-start.20
  46.2 1.3 %collective-permute-start.15 = (bf16[4,256,128]{2,1,0:T(8,128)(2,1)S(1)}, bf16[4,256,128]{2,1,0:T(8,128)(2,1)S(1)}, u32[]{:S(2)}, u32[]{:S(2)}) collective-permute-start(bf16[4,256,128]{2,1,0:T(8,128)(2,1)S(1)} %get-tuple-element.35.refs_0_.refs_4_.refs_3_), channel_id=1, source_target_pairs={{0,4},{2,6},{4,8},{6,10},{8,12},{10,14},{1,5},{3,7},{5,9},{7,11},{... | collective-permute-start | bytes 786440 | tf_op jit(solution)/shard_map/ppermute | solution.py:419
  47.6 0.1 reverse_select_fusion
  47.6 0.6 collective-permute-start.22
  48.2 3.3 %collective-permute-start.18 = (bf16[5,256,128]{2,1,0:T(8,128)(2,1)S(1)}, bf16[5,256,128]{2,1,0:T(8,128)(2,1)S(1)}, u32[]{:S(2)}, u32[]{:S(2)}) collective-permute-start(bf16[5,256,128]{2,1,0:T(8,128)(2,1)S(1)} %get-tuple-element.38.refs_3_), channel_id=1, source_target_pairs={{0,4},{2,6},{4,8},{6,10},{8,12},{10,14},{1,5},{3,7},{5,9},{7,11},{... | collective-permute-start | bytes 983048 | tf_op jit(solution)/shard_map/ppermute | solution.py:419
  51.5 0.0 collective-permute-done.20
  51.5 4.4 %collective-permute-start.16 = (bf16[4,256,128]{2,1,0:T(8,128)(2,1)S(1)}, bf16[4,256,128]{2,1,0:T(8,128)(2,1)S(1)}, u32[]{:S(2)}, u32[]{:S(2)}) collective-permute-start(bf16[4,256,128]{2,1,0:T(8,128)(2,1)S(1)} %get-tuple-element.36.refs_1_.refs_5_.refs_4_), channel_id=1, source_target_pairs={{0,4},{2,6},{4,8},{6,10},{8,12},{10,14},{1,5},{3,7},{5,9},{7,11},{... | collective-permute-start | bytes 786440 | tf_op jit(solution)/shard_map/ppermute | solution.py:419
  55.9 0.0 collective-permute-done.17.refs_0_
  55.9 0.2 collective-permute-start.21
  56.2 0.0 collective-permute-done.15.refs_0_
  56.2 0.1 collective-permute-start.19
  56.3 0.0 collective-permute-done.22.refs_4_.refs_6_
  56.3 0.6 collective-permute-start.23
  56.9 0.0 copy-start.7
  56.9 4.4 %shard_map.115.refs_11_ = f32[9,256,256]{2,1,0:T(8,128)S(1)} custom-call(s32[3]{0:T(128)S(1)} %pad_add_fusion.flags_ref, bf16[4,256,128]{2,1,0:T(8,128)(2,1)S(1)} %get-tuple-element.35.refs_0_.refs_4_.refs_3_, bf16[4,256,128]{2,1,0:T(8,128)(2,1)S(1)} %get-tuple-element.36.refs_1_.refs_5_.refs_4_, bf16[3,256,128]{2,1,0:T(8,128)(2,1)S(1)} %get-tuple-element.37.refs_2_, ...), custom_call_target="tpu_custom_call" | custom-call | flops 2717908992 | bytes 2204672 | tf_op jit(solution)/shard_map/pallas_call | solution.py:367
  61.3 5.6 %collective-permute-done.21.refs_3_ = f32[2,8,128]{2,1,0:T(8,128)S(1)} collective-permute-done((f32[2,8,128]{2,1,0:T(8,128)S(1)}, f32[2,8,128]{2,1,0:T(8,128)S(1)}, u32[]{:S(2)}, u32[]{:S(2)}) %collective-permute-start.21) | collective-permute-done | bytes 8224 | tf_op jit(solution)/shard_map/ppermute | solution.py:419
  66.8 0.0 collective-permute-done.19.refs_2_
  66.8 0.0 collective-permute-done.18.refs_1_
  66.8 4.0 %shard_map.116 = (f32[9,256,128]{2,1,0:T(8,128)S(1)}, bf16[4,128,128]{2,1,0:T(8,128)(2,1)S(1)}, f32[8,128]{1,0:T(8,128)S(1)}, bf16[1152,128]{1,0:T(8,128)(2,1)S(1)}) custom-call(s32[3]{0:T(128)S(1)} %pad_add_fusion.flags_ref, bf16[3,256,128]{2,1,0:T(8,128)(2,1)S(1)} %collective-permute-done.17.refs_0_, ...), custom_call_target="tpu_custom_call" | custom-call | flops 1358954496 | bytes 6178816 | tf_op jit(solution)/shard_map/pallas_call | solution.py:367
  70.8 1.5 %shard_map.117.refs_7_ = bf16[4,256,128]{2,1,0:T(8,128)(2,1)S(1)} custom-call(s32[3]{0:T(128)S(1)} %pad_add_fusion.flags_ref, bf16[4,256,128]{2,1,0:T(8,128)(2,1)S(1)} %collective-permute-done.15.refs_0_, bf16[1,2,256,128]{3,2,1,0:T(8,128)(2,1)S(1)} %collective-permute-done.23.refs_1_, f32[8,128]{1,0:T(8,128)S(1)} %get-tuple-element.41.refs_2_, ...), custom_call_target="tpu_custom_call" | custom-call | flops 603979776 | bytes 3313664 | tf_op jit(solution)/shard_map/pallas_call | solution.py:367
  72.4 2.6 %shard_map.118 = (bf16[4,128,128]{2,1,0:T(8,128)(2,1)S(1)}, bf16[4,128,128]{2,1,0:T(8,128)(2,1)S(1)}) custom-call(s32[3]{0:T(128)S(1)} %pad_add_fusion.flags_ref, bf16[4,256,128]{2,1,0:T(8,128)(2,1)S(1)} %collective-permute-done.15.refs_0_, bf16[4,256,128]{2,1,0:T(8,128)(2,1)S(1)} %collective-permute-done.16.refs_1_, ...), custom_call_target="tpu_custom_call" | custom-call | flops 754974720 | bytes 4264448 | tf_op jit(solution)/shard_map/pallas_call | solution.py:367
  74.9 1.6 %collective-permute-start.24 = (bf16[4,128,128]{2,1,0:T(8,128)(2,1)S(1)}, bf16[4,128,128]{2,1,0:T(8,128)(2,1)S(1)}, u32[]{:S(2)}, u32[]{:S(2)}) collective-permute-start(bf16[4,128,128]{2,1,0:T(8,128)(2,1)S(1)} %get-tuple-element.46), channel_id=1, source_target_pairs={{0,2},{2,0},{4,6},{6,4},{8,10},{10,8},{12,14},{14,12},{1,3},{3,1},... | collective-permute-start | bytes 393224 | tf_op jit(solution)/shard_map/ppermute | solution.py:416
  76.5 3.8 %collective-permute-done.24 = bf16[4,128,128]{2,1,0:T(8,128)(2,1)S(1)} collective-permute-done((bf16[4,128,128]{2,1,0:T(8,128)(2,1)S(1)}, bf16[4,128,128]{2,1,0:T(8,128)(2,1)S(1)}, u32[]{:S(2)}, u32[]{:S(2)}) %collective-permute-start.24) | collective-permute-done | bytes 131104 | tf_op jit(solution)/shard_map/ppermute | solution.py:416
  80.3 0.7 maximum_select_fusion
  (27 shorter events, 0.1 us)
Async XLA Ops:
  0.0 26.7 %copy-start = (bf16[3,3,3,128,128]{4,3,2,1,0:T(8,128)(2,1)S(1)}, bf16[3,3,3,128,128]{4,3,2,1,0:T(8,128)(2,1)}, u32[]{:S(2)}) copy-start(bf16[3,3,3,128,128]{4,3,2,1,0:T(8,128)(2,1)} %refs_8_.4) | copy-start | bytes 2654212
  0.1 1.3 %copy-start.1 = (bf16[2,1,8,256,128]{4,3,2,1,0:T(8,128)(2,1)S(1)}, bf16[2,1,8,256,128]{4,3,2,1,0:T(8,128)(2,1)}, u32[]{:S(2)}) copy-start(bf16[2,1,8,256,128]{4,3,2,1,0:T(8,128)(2,1)} %param.11) | copy-start | bytes 3145732
  1.4 25.3 %copy-start.8 = (f32[128]{0:T(128)S(1)}, f32[128]{0:T(128)}, u32[]{:S(2)}) copy-start(f32[128]{0:T(128)} %param.12) | copy-start | bytes 1540
  1.4 25.3 %copy-start.9 = (f32[128]{0:T(128)S(1)}, f32[128]{0:T(128)}, u32[]{:S(2)}) copy-start(f32[128]{0:T(128)} %param.13) | copy-start | bytes 1540
  2.0 31.0 %collective-permute-start.9 = (bf16[7,256,128]{2,1,0:T(8,128)(2,1)S(1)}, bf16[7,256,128]{2,1,0:T(8,128)(2,1)S(1)}, u32[]{:S(2)}, u32[]{:S(2)}) collective-permute-start(bf16[7,256,128]{2,1,0:T(8,128)(2,1)S(1)} %get-tuple-element.27.refs_1_.refs_2_.refs_15_.refs_9_.refs_10_), channel_id=1, source_target_pairs={{0,4},{2,6},{4,8},{6,10},{8,12},{10,14},{12,0},{14,2},{1,5},{3,7},... | collective-permute-start | bytes 1376264 | tf_op jit(solution)/shard_map/ppermute | solution.py:419
  5.1 15.1 %collective-permute-start = (bf16[4,256,128]{2,1,0:T(8,128)(2,1)S(1)}, bf16[4,256,128]{2,1,0:T(8,128)(2,1)S(1)}, u32[]{:S(2)}, u32[]{:S(2)}) collective-permute-start(bf16[4,256,128]{2,1,0:T(8,128)(2,1)S(1)} %get-tuple-element.28.refs_2_), channel_id=1, source_target_pairs={{0,2},{2,0},{4,6},{6,4},{8,10},{10,8},{12,14},{14,12},{1,3},{3,1},... | collective-permute-start | bytes 786440 | tf_op jit(solution)/shard_map/ppermute | solution.py:416
  6.6 23.2 %collective-permute-start.1 = (bf16[4,256,128]{2,1,0:T(8,128)(2,1)S(1)}, bf16[4,256,128]{2,1,0:T(8,128)(2,1)S(1)}, u32[]{:S(2)}, u32[]{:S(2)}) collective-permute-start(bf16[4,256,128]{2,1,0:T(8,128)(2,1)S(1)} %get-tuple-element.29.refs_3_), channel_id=1, source_target_pairs={{0,2},{2,0},{4,6},{6,4},{8,10},{10,8},{12,14},{14,12},{1,3},{3,1},... | collective-permute-start | bytes 786440 | tf_op jit(solution)/shard_map/ppermute | solution.py:416
  8.0 1.2 %collective-permute-start.10 = (f32[2,8,128]{2,1,0:T(8,128)S(1)}, f32[2,8,128]{2,1,0:T(8,128)S(1)}, u32[]{:S(2)}, u32[]{:S(2)}) collective-permute-start(f32[2,8,128]{2,1,0:T(8,128)S(1)} %shard_map.110), channel_id=1, source_target_pairs={{0,1},{1,0},{2,3},{3,2},{4,5},{5,4},{6,7},{7,6},{8,9},{9,8},{10,11... | collective-permute-start | bytes 24584 | tf_op jit(solution)/shard_map/ppermute | solution.py:425
  9.2 9.5 %collective-permute-start.11 = (f32[2,8,128]{2,1,0:T(8,128)S(1)}, f32[2,8,128]{2,1,0:T(8,128)S(1)}, u32[]{:S(2)}, u32[]{:S(2)}) collective-permute-start(f32[2,8,128]{2,1,0:T(8,128)S(1)} %add.11.refs_3_.refs_9_), channel_id=1, source_target_pairs={{0,2},{2,0},{4,6},{6,4},{8,10},{10,8},{12,14},{14,12},{1,3},{3,1},... | collective-permute-start | bytes 24584 | tf_op jit(solution)/shard_map/ppermute | solution.py:416
  10.7 9.5 %collective-permute-start.12 = (f32[2,8,128]{2,1,0:T(8,128)S(1)}, f32[2,8,128]{2,1,0:T(8,128)S(1)}, u32[]{:S(2)}, u32[]{:S(2)}) collective-permute-start(f32[2,8,128]{2,1,0:T(8,128)S(1)} %add.11.refs_3_.refs_9_), channel_id=1, source_target_pairs={{0,4},{2,6},{4,8},{6,10},{8,12},{10,14},{12,0},{14,2},{1,5},{3,7},... | collective-permute-start | bytes 24584 | tf_op jit(solution)/shard_map/ppermute | solution.py:419
  18.7 6.1 %collective-permute-start.7 = (bf16[1,256,128]{2,1,0:T(8,128)(2,1)S(1)}, bf16[1,256,128]{2,1,0:T(8,128)(2,1)S(1)}, u32[]{:S(2)}, u32[]{:S(2)}) collective-permute-start(bf16[1,256,128]{2,1,0:T(8,128)(2,1)S(1)} %get-tuple-element.26.refs_0_.refs_1_.refs_14_.refs_8_.refs_9_), channel_id=1, source_target_pairs={{0,4},{2,6},{4,8},{6,10},{8,12},{10,14},{12,0},{14,2},{1,5},{3,7},... | collective-permute-start | bytes 196616 | tf_op jit(solution)/shard_map/ppermute | solution.py:419
  20.2 6.4 %collective-permute-start.5 = (bf16[1,256,128]{2,1,0:T(8,128)(2,1)S(1)}, bf16[1,256,128]{2,1,0:T(8,128)(2,1)S(1)}, u32[]{:S(2)}, u32[]{:S(2)}) collective-permute-start(bf16[1,256,128]{2,1,0:T(8,128)(2,1)S(1)} %get-tuple-element.26.refs_0_.refs_1_.refs_14_.refs_8_.refs_9_), channel_id=1, source_target_pairs={{0,1},{1,0},{2,3},{3,2},{4,5},{5,4},{6,7},{7,6},{8,9},{9,8},{10,11... | collective-permute-start | bytes 196616 | tf_op jit(solution)/shard_map/ppermute | solution.py:425
  20.3 6.4 %collective-permute-start.13 = (f32[2,8,128]{2,1,0:T(8,128)S(1)}, f32[2,8,128]{2,1,0:T(8,128)S(1)}, u32[]{:S(2)}, u32[]{:S(2)}) collective-permute-start(f32[2,8,128]{2,1,0:T(8,128)S(1)} %add.11.refs_3_.refs_9_), channel_id=1, source_target_pairs={{0,6},{2,4},{4,10},{6,8},{8,14},{10,12},{12,2},{14,0},{1,7},{3,5},... | collective-permute-start | bytes 24584 | tf_op jit(solution)/shard_map/ppermute | solution.py:422
  24.7 4.6 %collective-permute-start.8 = (bf16[1,256,128]{2,1,0:T(8,128)(2,1)S(1)}, bf16[1,256,128]{2,1,0:T(8,128)(2,1)S(1)}, u32[]{:S(2)}, u32[]{:S(2)}) collective-permute-start(bf16[1,256,128]{2,1,0:T(8,128)(2,1)S(1)} %collective-permute-done.7.refs_7_), channel_id=1, source_target_pairs={{0,1},{1,0},{2,3},{3,2},{4,5},{5,4},{6,7},{7,6},{8,9},{9,8},{10,11... | collective-permute-start | bytes 196616 | tf_op jit(solution)/shard_map/ppermute | solution.py:425
  26.7 6.3 %collective-permute-start.6 = (bf16[1,256,128]{2,1,0:T(8,128)(2,1)S(1)}, bf16[1,256,128]{2,1,0:T(8,128)(2,1)S(1)}, u32[]{:S(2)}, u32[]{:S(2)}) collective-permute-start(bf16[1,256,128]{2,1,0:T(8,128)(2,1)S(1)} %slice.17), channel_id=1, source_target_pairs={{0,1},{1,0},{2,3},{3,2},{4,5},{5,4},{6,7},{7,6},{8,9},{9,8},{10,11... | collective-permute-start | bytes 196616 | tf_op jit(solution)/shard_map/ppermute | solution.py:425
  26.7 6.3 %collective-permute-start.2 = (bf16[1,256,128]{2,1,0:T(8,128)(2,1)S(1)}, bf16[1,256,128]{2,1,0:T(8,128)(2,1)S(1)}, u32[]{:S(2)}, u32[]{:S(2)}) collective-permute-start(bf16[1,256,128]{2,1,0:T(8,128)(2,1)S(1)} %slice.17), channel_id=1, source_target_pairs={{0,4},{2,6},{4,8},{6,10},{8,12},{10,14},{12,0},{14,2},{1,5},{3,7},... | collective-permute-start | bytes 196616 | tf_op jit(solution)/shard_map/ppermute | solution.py:419
  29.3 9.7 %copy-start.4 = (f32[128]{0:T(128)S(1)}, f32[128]{0:T(128)}, u32[]{:S(2)}) copy-start(f32[128]{0:T(128)} %param.15) | copy-start | bytes 1540
  29.3 9.6 %collective-permute-start.3 = (bf16[3,256,128]{2,1,0:T(8,128)(2,1)S(1)}, bf16[3,256,128]{2,1,0:T(8,128)(2,1)S(1)}, u32[]{:S(2)}, u32[]{:S(2)}) collective-permute-start(bf16[3,256,128]{2,1,0:T(8,128)(2,1)S(1)} %slice.18), channel_id=1, source_target_pairs={{0,4},{2,6},{4,8},{6,10},{8,12},{10,14},{12,0},{14,2},{1,5},{3,7},... | collective-permute-start | bytes 589832 | tf_op jit(solution)/shard_map/ppermute | solution.py:419
  29.8 14.3 %collective-permute-start.4 = (bf16[4,256,128]{2,1,0:T(8,128)(2,1)S(1)}, bf16[4,256,128]{2,1,0:T(8,128)(2,1)S(1)}, u32[]{:S(2)}, u32[]{:S(2)}) collective-permute-start(bf16[4,256,128]{2,1,0:T(8,128)(2,1)S(1)} %collective-permute-done.1.refs_5_.refs_3_.refs_18_.refs_12_), channel_id=1, source_target_pairs={{0,4},{2,6},{4,8},{6,10},{8,12},{10,14},{12,0},{14,2},{1,5},{3,7},... | collective-permute-start | bytes 786440 | tf_op jit(solution)/shard_map/ppermute | solution.py:419
  33.0 4.2 %collective-permute-start.14 = (bf16[1,256,128]{2,1,0:T(8,128)(2,1)S(1)}, bf16[1,256,128]{2,1,0:T(8,128)(2,1)S(1)}, u32[]{:S(2)}, u32[]{:S(2)}) collective-permute-start(bf16[1,256,128]{2,1,0:T(8,128)(2,1)S(1)} %collective-permute-done.2.refs_5_.refs_4_), channel_id=1, source_target_pairs={{0,1},{1,0},{2,3},{3,2},{4,5},{5,4},{6,7},{7,6},{8,9},{9,8},{10,11... | collective-permute-start | bytes 196616 | tf_op jit(solution)/shard_map/ppermute | solution.py:425
  40.5 15.4 %collective-permute-start.17 = (bf16[3,256,128]{2,1,0:T(8,128)(2,1)S(1)}, bf16[3,256,128]{2,1,0:T(8,128)(2,1)S(1)}, u32[]{:S(2)}, u32[]{:S(2)}) collective-permute-start(bf16[3,256,128]{2,1,0:T(8,128)(2,1)S(1)} %get-tuple-element.37.refs_2_), channel_id=1, source_target_pairs={{0,4},{2,6},{4,8},{6,10},{8,12},{10,14},{12,0},{14,2},{1,5},{3,7},... | collective-permute-start | bytes 589832 | tf_op jit(solution)/shard_map/ppermute | solution.py:419
  44.1 3.4 %copy-start.10 = (bf16[3,3,128,128]{3,2,1,0:T(8,128)(2,1)S(1)}, bf16[3,3,128,128]{3,2,1,0:T(8,128)(2,1)}, u32[]{:S(2)}) copy-start(bf16[3,3,128,128]{3,2,1,0:T(8,128)(2,1)} %param.20) | copy-start | bytes 884740
  44.1 12.8 %copy-start.2 = (bf16[3,3,3,128,128]{4,3,2,1,0:T(8,128)(2,1)S(1)}, bf16[3,3,3,128,128]{4,3,2,1,0:T(8,128)(2,1)}, u32[]{:S(2)}) copy-start(bf16[3,3,3,128,128]{4,3,2,1,0:T(8,128)(2,1)} %refs_10_.1) | copy-start | bytes 2654212
  44.1 12.8 %copy-start.5 = (f32[128]{0:T(128)S(1)}, f32[128]{0:T(128)}, u32[]{:S(2)}) copy-start(f32[128]{0:T(128)} %param.16) | copy-start | bytes 1540
  44.1 12.8 %copy-start.6 = (f32[128]{0:T(128)S(1)}, f32[128]{0:T(128)}, u32[]{:S(2)}) copy-start(f32[128]{0:T(128)} %param.17) | copy-start | bytes 1540
  46.2 5.4 %collective-permute-start.20 = (f32[2,8,128]{2,1,0:T(8,128)S(1)}, f32[2,8,128]{2,1,0:T(8,128)S(1)}, u32[]{:S(2)}, u32[]{:S(2)}) collective-permute-start(f32[2,8,128]{2,1,0:T(8,128)S(1)} %get-tuple-element.39), channel_id=1, source_target_pairs={{0,1},{1,0},{2,3},{3,2},{4,5},{5,4},{6,7},{7,6},{8,9},{9,8},{10,11... | collective-permute-start | bytes 24584 | tf_op jit(solution)/shard_map/ppermute | solution.py:425
  46.2 10.0 %collective-permute-start.15 = (bf16[4,256,128]{2,1,0:T(8,128)(2,1)S(1)}, bf16[4,256,128]{2,1,0:T(8,128)(2,1)S(1)}, u32[]{:S(2)}, u32[]{:S(2)}) collective-permute-start(bf16[4,256,128]{2,1,0:T(8,128)(2,1)S(1)} %get-tuple-element.35.refs_0_.refs_4_.refs_3_), channel_id=1, source_target_pairs={{0,4},{2,6},{4,8},{6,10},{8,12},{10,14},{1,5},{3,7},{5,9},{7,11},{... | collective-permute-start | bytes 786440 | tf_op jit(solution)/shard_map/ppermute | solution.py:419
  47.6 8.7 %collective-permute-start.22 = (bf16[2,2,256,128]{3,2,1,0:T(8,128)(2,1)S(1)}, bf16[2,2,256,128]{3,2,1,0:T(8,128)(2,1)S(1)}, u32[]{:S(2)}, u32[]{:S(2)}) collective-permute-start(bf16[2,2,256,128]{3,2,1,0:T(8,128)(2,1)S(1)} %get-tuple-element.40), channel_id=1, source_target_pairs={{0,1},{1,0},{2,3},{3,2},{4,5},{5,4},{6,7},{7,6},{8,9},{9,8},{10,11... | collective-permute-start | bytes 786440 | tf_op jit(solution)/shard_map/ppermute | solution.py:425
  48.2 18.7 %collective-permute-start.18 = (bf16[5,256,128]{2,1,0:T(8,128)(2,1)S(1)}, bf16[5,256,128]{2,1,0:T(8,128)(2,1)S(1)}, u32[]{:S(2)}, u32[]{:S(2)}) collective-permute-start(bf16[5,256,128]{2,1,0:T(8,128)(2,1)S(1)} %get-tuple-element.38.refs_3_), channel_id=1, source_target_pairs={{0,4},{2,6},{4,8},{6,10},{8,12},{10,14},{1,5},{3,7},{5,9},{7,11},{... | collective-permute-start | bytes 983048 | tf_op jit(solution)/shard_map/ppermute | solution.py:419
  51.5 20.9 %collective-permute-start.16 = (bf16[4,256,128]{2,1,0:T(8,128)(2,1)S(1)}, bf16[4,256,128]{2,1,0:T(8,128)(2,1)S(1)}, u32[]{:S(2)}, u32[]{:S(2)}) collective-permute-start(bf16[4,256,128]{2,1,0:T(8,128)(2,1)S(1)} %get-tuple-element.36.refs_1_.refs_5_.refs_4_), channel_id=1, source_target_pairs={{0,4},{2,6},{4,8},{6,10},{8,12},{10,14},{1,5},{3,7},{5,9},{7,11},{... | collective-permute-start | bytes 786440 | tf_op jit(solution)/shard_map/ppermute | solution.py:419
  55.9 10.9 %collective-permute-start.21 = (f32[2,8,128]{2,1,0:T(8,128)S(1)}, f32[2,8,128]{2,1,0:T(8,128)S(1)}, u32[]{:S(2)}, u32[]{:S(2)}) collective-permute-start(f32[2,8,128]{2,1,0:T(8,128)S(1)} %add.12.refs_5_.refs_7_), channel_id=1, source_target_pairs={{0,4},{2,6},{4,8},{6,10},{8,12},{10,14},{12,0},{14,2},{1,5},{3,7},... | collective-permute-start | bytes 24584 | tf_op jit(solution)/shard_map/ppermute | solution.py:419
  56.2 10.6 %collective-permute-start.19 = (bf16[1,2,256,128]{3,2,1,0:T(8,128)(2,1)S(1)}, bf16[1,2,256,128]{3,2,1,0:T(8,128)(2,1)S(1)}, u32[]{:S(2)}, u32[]{:S(2)}) collective-permute-start(bf16[1,2,256,128]{3,2,1,0:T(8,128)(2,1)S(1)} %slice_bitcast_fusion.1), channel_id=1, source_target_pairs={{0,1},{1,0},{2,3},{3,2},{4,5},{5,4},{6,7},{7,6},{8,9},{9,8},{10,11... | collective-permute-start | bytes 393224 | tf_op jit(solution)/shard_map/ppermute | solution.py:425
  56.3 14.5 %collective-permute-start.23 = (bf16[1,2,256,128]{3,2,1,0:T(8,128)(2,1)S(1)}, bf16[1,2,256,128]{3,2,1,0:T(8,128)(2,1)S(1)}, u32[]{:S(2)}, u32[]{:S(2)}) collective-permute-start(bf16[1,2,256,128]{3,2,1,0:T(8,128)(2,1)S(1)} %slice_bitcast_fusion), channel_id=1, source_target_pairs={{0,1},{1,0},{2,3},{3,2},{4,5},{5,4},{6,7},{7,6},{8,9},{9,8},{10,11... | collective-permute-start | bytes 393224 | tf_op jit(solution)/shard_map/ppermute | solution.py:425
  56.9 9.9 %copy-start.3 = (f32[128]{0:T(128)S(1)}, f32[128]{0:T(128)}, u32[]{:S(2)}) copy-start(f32[128]{0:T(128)} %param.21) | copy-start | bytes 1540
  56.9 9.9 %copy-start.7 = (f32[128]{0:T(128)S(1)}, f32[128]{0:T(128)}, u32[]{:S(2)}) copy-start(f32[128]{0:T(128)} %param.19) | copy-start | bytes 1540
  74.9 5.4 %collective-permute-start.24 = (bf16[4,128,128]{2,1,0:T(8,128)(2,1)S(1)}, bf16[4,128,128]{2,1,0:T(8,128)(2,1)S(1)}, u32[]{:S(2)}, u32[]{:S(2)}) collective-permute-start(bf16[4,128,128]{2,1,0:T(8,128)(2,1)S(1)} %get-tuple-element.46), channel_id=1, source_target_pairs={{0,2},{2,0},{4,6},{6,4},{8,10},{10,8},{12,14},{14,12},{1,3},{3,1},... | collective-permute-start | bytes 393224 | tf_op jit(solution)/shard_map/ppermute | solution.py:416

commit v3 on v2

--- a/solution.py
+++ b/solution.py
@@ -24,7 +24,7 @@
     grouped = jnp.dot(totals, same, precision=lax.Precision.HIGHEST, preferred_element_type=F32)
     grouped = grouped / (cells * size)
     mean = grouped[0:1]
-    inverse = lax.rsqrt(grouped[1:2] - mean * mean + EPSILON)
+    inverse = lax.rsqrt(jnp.maximum(grouped[1:2] - mean * mean, 0.0) + EPSILON)
     return mean, inverse * gain, bias
 
 
@@ -60,7 +60,7 @@
 
 def steps(first, last):
     total = last - first
-    size = 3 if total % 3 == 0 else 2
+    size = -(-total // 2) if total > 5 else total
     return [(r, min(size, last - r)) for r in range(first, last, size)]
 
 
@@ -399,7 +399,7 @@
     assert clips == 2 and bands == 2 and count % 2 == 0 and height % 8 == 0
     cells = height * bands * width
     near = 3 * height // 8
-    tail = height // TAIL
+    tail = 3 * height // 8
     position = lax.axis_index("tm")
     band = lax.axis_index("rows")
     side = position % 2
@@ -622,8 +622,7 @@
     return result[:, None]
 
 
-OPEN = ('b_on2','a_on1','a_on2')
-TAIL = 2
+OPEN = ('b_on2', 'a_on2')
 
 
 def solution(mesh):

time: 81.2 us -> 79.8 us (0.983)
  transfers between devices with their start and end apart: 25 -> 25, of which waited for: 9 -> 10; matrix products, arithmetic and copies ran while one was open for 0% -> 0% of each run, Pallas kernels for 26% -> 27%
where the time goes in v3:
time: 79.8 us; the launch traced here: 79.7 us
  waiting for transfers between devices  27.3 us (34%)
  starting transfers between devices  25.6 us (32%)
  Pallas kernels  24.2 us (30%)
  local copies, waits for them, and re-layouts  1.37 us (2%)
  other arithmetic  0.86 us (1%)
    pallas_call x10, Pallas kernels, call(): pl.pallas_call(kernel, out_shape=out_shape, in_specs=[pl.BlockSpec(memory...  24.2 us
    ppermute x11, starting transfers between devices, later(): return lax.ppermute(v, 'tm', onward(name, 0))  16.7 us
    ppermute x11, waiting for transfers between devices, later(): return lax.ppermute(v, 'tm', onward(name, 0))  14.1 us
    ppermute x4, waiting for transfers between devices, swapped(): return lax.ppermute(v, 'tm', swap)  10.1 us
    ppermute x4, starting transfers between devices, swapped(): return lax.ppermute(v, 'tm', swap)  5.13 us
    ppermute x1, starting transfers between devices, crossed(): return lax.ppermute(v, 'tm', onward(name, 1))  2.58 us
    ppermute x1, waiting for transfers between devices, crossed(): return lax.ppermute(v, 'tm', onward(name, 1))  1.92 us
  transfers between devices with their start and end apart: 25, of which 10 were waited for; matrix products, arithmetic and copies ran while one was open for 0% of the time, Pallas kernels for 27%

profile of v3, /device:TPU:0, one launch (start us, length us, event | category | flops | bytes accessed | tf_op | source)
XLA Modules:
  0.0 79.7 jit_solution(9907996915477957528)
XLA Ops:
  0.0 0.1 pad_add_fusion.flags_ref
  0.1 1.3 %copy-done.1 = bf16[2,1,8,256,128]{4,3,2,1,0:T(8,128)(2,1)S(1)} copy-done((bf16[2,1,8,256,128]{4,3,2,1,0:T(8,128)(2,1)S(1)}, bf16[2,1,8,256,128]{4,3,2,1,0:T(8,128)(2,1)}, u32[]{:S(2)}) %copy-start.1) | copy-done | bytes 1048600
  1.4 0.6 shard_map.109
  2.0 3.1 %collective-permute-start.9 = (bf16[7,256,128]{2,1,0:T(8,128)(2,1)S(1)}, bf16[7,256,128]{2,1,0:T(8,128)(2,1)S(1)}, u32[]{:S(2)}, u32[]{:S(2)}) collective-permute-start(bf16[7,256,128]{2,1,0:T(8,128)(2,1)S(1)} %get-tuple-element.27.refs_1_.refs_2_.refs_15_.refs_9_.refs_10_), channel_id=1, source_target_pairs={{0,4},{2,6},{4,8},{6,10},{8,12},{10,14},{12,0},{14,2},{1,5},{3,7},... | collective-permute-start | bytes 1376264 | tf_op jit(solution)/shard_map/ppermute | solution.py:419
  5.1 1.5 %collective-permute-start = (bf16[4,256,128]{2,1,0:T(8,128)(2,1)S(1)}, bf16[4,256,128]{2,1,0:T(8,128)(2,1)S(1)}, u32[]{:S(2)}, u32[]{:S(2)}) collective-permute-start(bf16[4,256,128]{2,1,0:T(8,128)(2,1)S(1)} %get-tuple-element.28.refs_2_), channel_id=1, source_target_pairs={{0,2},{2,0},{4,6},{6,4},{8,10},{10,8},{12,14},{14,12},{1,3},{3,1},... | collective-permute-start | bytes 786440 | tf_op jit(solution)/shard_map/ppermute | solution.py:416
  6.6 0.5 collective-permute-start.1
  7.1 0.8 %shard_map.110 = f32[2,8,128]{2,1,0:T(8,128)S(1)} custom-call(s32[3]{0:T(128)S(1)} %pad_add_fusion.flags_ref, bf16[1,256,128]{2,1,0:T(8,128)(2,1)S(1)} %get-tuple-element.26.refs_0_.refs_1_.refs_14_.refs_8_.refs_9_, bf16[7,256,128]{2,1,0:T(8,128)(2,1)S(1)} %get-tuple-element.27.refs_1_.refs_2_.refs_15_.refs_9_.refs_10_, ...), custom_call_target="tpu_custom_call" | custom-call | bytes 1048576 | tf_op jit(solution)/shard_map/pallas_call | solution.py:367
  8.0 0.1 collective-permute-start.10
  8.0 1.2 %collective-permute-done.10 = f32[2,8,128]{2,1,0:T(8,128)S(1)} collective-permute-done((f32[2,8,128]{2,1,0:T(8,128)S(1)}, f32[2,8,128]{2,1,0:T(8,128)S(1)}, u32[]{:S(2)}, u32[]{:S(2)}) %collective-permute-start.10) | collective-permute-done | bytes 8224 | tf_op jit(solution)/shard_map/ppermute | solution.py:425
  9.2 1.5 %collective-permute-start.11 = (f32[2,8,128]{2,1,0:T(8,128)S(1)}, f32[2,8,128]{2,1,0:T(8,128)S(1)}, u32[]{:S(2)}, u32[]{:S(2)}) collective-permute-start(f32[2,8,128]{2,1,0:T(8,128)S(1)} %add.11.refs_3_.refs_9_), channel_id=1, source_target_pairs={{0,2},{2,0},{4,6},{6,4},{8,10},{10,8},{12,14},{14,12},{1,3},{3,1},... | collective-permute-start | bytes 24584 | tf_op jit(solution)/shard_map/ppermute | solution.py:416
  10.7 1.6 %collective-permute-start.12 = (f32[2,8,128]{2,1,0:T(8,128)S(1)}, f32[2,8,128]{2,1,0:T(8,128)S(1)}, u32[]{:S(2)}, u32[]{:S(2)}) collective-permute-start(f32[2,8,128]{2,1,0:T(8,128)S(1)} %add.11.refs_3_.refs_9_), channel_id=1, source_target_pairs={{0,4},{2,6},{4,8},{6,10},{8,12},{10,14},{12,0},{14,2},{1,5},{3,7},... | collective-permute-start | bytes 24584 | tf_op jit(solution)/shard_map/ppermute | solution.py:419
  12.3 6.4 %collective-permute-done.11.refs_10_ = f32[2,8,128]{2,1,0:T(8,128)S(1)} collective-permute-done((f32[2,8,128]{2,1,0:T(8,128)S(1)}, f32[2,8,128]{2,1,0:T(8,128)S(1)}, u32[]{:S(2)}, u32[]{:S(2)}) %collective-permute-start.11) | collective-permute-done | bytes 8224 | tf_op jit(solution)/shard_map/ppermute | solution.py:416
  18.7 1.6 %collective-permute-start.7 = (bf16[1,256,128]{2,1,0:T(8,128)(2,1)S(1)}, bf16[1,256,128]{2,1,0:T(8,128)(2,1)S(1)}, u32[]{:S(2)}, u32[]{:S(2)}) collective-permute-start(bf16[1,256,128]{2,1,0:T(8,128)(2,1)S(1)} %get-tuple-element.26.refs_0_.refs_1_.refs_14_.refs_8_.refs_9_), channel_id=1, source_target_pairs={{0,4},{2,6},{4,8},{6,10},{8,12},{10,14},{12,0},{14,2},{1,5},{3,7},... | collective-permute-start | bytes 196616 | tf_op jit(solution)/shard_map/ppermute | solution.py:419
  20.2 0.0 collective-permute-done.12.refs_11_
  20.2 0.0 collective-permute-start.5
  20.2 0.0 collective-permute-done.refs_4_.refs_3_.refs_2_.refs_17_.refs_11_
  20.3 2.6 %collective-permute-start.13 = (f32[2,8,128]{2,1,0:T(8,128)S(1)}, f32[2,8,128]{2,1,0:T(8,128)S(1)}, u32[]{:S(2)}, u32[]{:S(2)}) collective-permute-start(f32[2,8,128]{2,1,0:T(8,128)S(1)} %add.11.refs_3_.refs_9_), channel_id=1, source_target_pairs={{0,6},{2,4},{4,10},{6,8},{8,14},{10,12},{12,2},{14,0},{1,7},{3,5},... | collective-permute-start | bytes 24584 | tf_op jit(solution)/shard_map/ppermute | solution.py:422
  22.8 1.9 %collective-permute-done.7.refs_7_ = bf16[1,256,128]{2,1,0:T(8,128)(2,1)S(1)} collective-permute-done((bf16[1,256,128]{2,1,0:T(8,128)(2,1)S(1)}, bf16[1,256,128]{2,1,0:T(8,128)(2,1)S(1)}, u32[]{:S(2)}, u32[]{:S(2)}) %collective-permute-start.7) | collective-permute-done | bytes 65568 | tf_op jit(solution)/shard_map/ppermute | solution.py:419
  24.7 0.0 collective-permute-start.8
  24.7 1.9 %collective-permute-done.13.refs_12_ = f32[2,8,128]{2,1,0:T(8,128)S(1)} collective-permute-done((f32[2,8,128]{2,1,0:T(8,128)S(1)}, f32[2,8,128]{2,1,0:T(8,128)S(1)}, u32[]{:S(2)}, u32[]{:S(2)}) %collective-permute-start.13) | collective-permute-done | bytes 8224 | tf_op jit(solution)/shard_map/ppermute | solution.py:422
  26.7 0.0 collective-permute-start.6
  26.7 0.0 collective-permute-done.5.refs_0_.refs_13_.refs_7_
  26.7 0.0 collective-permute-start.2
  26.7 2.7 %shard_map.111.refs_16_ = f32[8,256,256]{2,1,0:T(8,128)S(1)} custom-call(s32[3]{0:T(128)S(1)} %pad_add_fusion.flags_ref, bf16[1,256,128]{2,1,0:T(8,128)(2,1)S(1)} %collective-permute-done.5.refs_0_.refs_13_.refs_7_, bf16[1,256,128]{2,1,0:T(8,128)(2,1)S(1)} %get-tuple-element.26.refs_0_.refs_1_.refs_14_.refs_8_.refs_9_, ...), custom_call_target="tpu_custom_call" | custom-call | flops 1207959552 | bytes 1483776 | tf_op jit(solution)/shard_map/pallas_call | solution.py:367
  29.4 0.0 copy-start.4
  29.4 0.0 collective-permute-done.8.refs_6_
  29.4 0.5 collective-permute-start.3
  29.9 0.0 collective-permute-done.1.refs_5_.refs_3_.refs_18_.refs_12_
  29.9 1.1 %collective-permute-start.4 = (bf16[4,256,128]{2,1,0:T(8,128)(2,1)S(1)}, bf16[4,256,128]{2,1,0:T(8,128)(2,1)S(1)}, u32[]{:S(2)}, u32[]{:S(2)}) collective-permute-start(bf16[4,256,128]{2,1,0:T(8,128)(2,1)S(1)} %collective-permute-done.1.refs_5_.refs_3_.refs_18_.refs_12_), channel_id=1, source_target_pairs={{0,4},{2,6},{4,8},{6,10},{8,12},{10,14},{12,0},{14,2},{1,5},{3,7},... | collective-permute-start | bytes 786440 | tf_op jit(solution)/shard_map/ppermute | solution.py:419
  31.0 1.9 %collective-permute-done.2.refs_5_.refs_4_ = bf16[1,256,128]{2,1,0:T(8,128)(2,1)S(1)} collective-permute-done((bf16[1,256,128]{2,1,0:T(8,128)(2,1)S(1)}, bf16[1,256,128]{2,1,0:T(8,128)(2,1)S(1)}, u32[]{:S(2)}, u32[]{:S(2)}) %collective-permute-start.2) | collective-permute-done | bytes 65568 | tf_op jit(solution)/shard_map/ppermute | solution.py:419
  33.0 0.0 collective-permute-start.14
  33.0 0.0 collective-permute-done.6.refs_3_.refs_16_.refs_10_
  33.0 0.0 collective-permute-done.9.refs_8_
  33.0 4.3 %shard_map.112 = (f32[8,256,256]{2,1,0:T(8,128)S(1)}, f32[8,128]{1,0:T(8,128)S(1)}, bf16[2,256,128]{2,1,0:T(8,128)(2,1)S(1)}) custom-call(s32[3]{0:T(128)S(1)} %pad_add_fusion.flags_ref, bf16[1,256,128]{2,1,0:T(8,128)(2,1)S(1)} %collective-permute-done.5.refs_0_.refs_13_.refs_7_, ...), custom_call_target="tpu_custom_call" | custom-call | flops 2415919104 | bytes 4785152 | tf_op jit(solution)/shard_map/pallas_call | solution.py:367
  37.3 0.0 collective-permute-done.14.refs_4_
  37.3 1.7 %collective-permute-done.3.refs_6_.refs_5_ = bf16[3,256,128]{2,1,0:T(8,128)(2,1)S(1)} collective-permute-done((bf16[3,256,128]{2,1,0:T(8,128)(2,1)S(1)}, bf16[3,256,128]{2,1,0:T(8,128)(2,1)S(1)}, u32[]{:S(2)}, u32[]{:S(2)}) %collective-permute-start.3) | collective-permute-done | bytes 196640 | tf_op jit(solution)/shard_map/ppermute | solution.py:419
  39.0 1.5 %shard_map.113 = (bf16[3,256,128]{2,1,0:T(8,128)(2,1)S(1)}, bf16[3,256,128]{2,1,0:T(8,128)(2,1)S(1)}, bf16[2,2,256,128]{3,2,1,0:T(8,128)(2,1)S(1)}, f32[2,8,128]{2,1,0:T(8,128)S(1)}) custom-call(s32[3]{0:T(128)S(1)} %pad_add_fusion.flags_ref, bf16[2,256,128]{2,1,0:T(8,128)(2,1)S(1)} %get-tuple-element.32.refs_0_, ...), custom_call_target="tpu_custom_call" | custom-call | flops 452984832 | bytes 4231680 | tf_op jit(solution)/shard_map/pallas_call | solution.py:367
  40.6 0.1 collective-permute-start.17
  40.6 3.6 %collective-permute-done.4.refs_6_ = bf16[4,256,128]{2,1,0:T(8,128)(2,1)S(1)} collective-permute-done((bf16[4,256,128]{2,1,0:T(8,128)(2,1)S(1)}, bf16[4,256,128]{2,1,0:T(8,128)(2,1)S(1)}, u32[]{:S(2)}, u32[]{:S(2)}) %collective-permute-start.4) | collective-permute-done | bytes 262176 | tf_op jit(solution)/shard_map/ppermute | solution.py:419
  44.2 2.0 %shard_map.114 = (bf16[5,256,128]{2,1,0:T(8,128)(2,1)S(1)}, bf16[5,256,128]{2,1,0:T(8,128)(2,1)S(1)}, bf16[3,256,128]{2,1,0:T(8,128)(2,1)S(1)}, f32[2,8,128]{2,1,0:T(8,128)S(1)}) custom-call(s32[3]{0:T(128)S(1)} %pad_add_fusion.flags_ref, bf16[1,256,128]{2,1,0:T(8,128)(2,1)S(1)} %get-tuple-element.26.refs_0_.refs_1_.refs_14_.refs_8_.refs_9_, ...), custom_call_target="tpu_custom_call" | custom-call | flops 754974720 | bytes 4764160 | tf_op jit(solution)/shard_map/pallas_call | solution.py:367
  46.2 0.1 collective-permute-start.20
  46.3 0.1 collective-permute-start.15
  46.3 0.1 reverse_select_fusion
  46.4 0.5 collective-permute-start.22
  46.9 2.7 %collective-permute-start.18 = (bf16[5,256,128]{2,1,0:T(8,128)(2,1)S(1)}, bf16[5,256,128]{2,1,0:T(8,128)(2,1)S(1)}, u32[]{:S(2)}, u32[]{:S(2)}) collective-permute-start(bf16[5,256,128]{2,1,0:T(8,128)(2,1)S(1)} %get-tuple-element.38.refs_3_), channel_id=1, source_target_pairs={{0,4},{2,6},{4,8},{6,10},{8,12},{10,14},{1,5},{3,7},{5,9},{7,11},{... | collective-permute-start | bytes 983048 | tf_op jit(solution)/shard_map/ppermute | solution.py:419
  49.6 4.4 %collective-permute-start.16 = (bf16[3,256,128]{2,1,0:T(8,128)(2,1)S(1)}, bf16[3,256,128]{2,1,0:T(8,128)(2,1)S(1)}, u32[]{:S(2)}, u32[]{:S(2)}) collective-permute-start(bf16[3,256,128]{2,1,0:T(8,128)(2,1)S(1)} %get-tuple-element.36.refs_1_.refs_5_.refs_4_), channel_id=1, source_target_pairs={{0,4},{2,6},{4,8},{6,10},{8,12},{10,14},{1,5},{3,7},{5,9},{7,11},{... | collective-permute-start | bytes 589832 | tf_op jit(solution)/shard_map/ppermute | solution.py:419
  54.0 0.0 collective-permute-done.17.refs_0_
  54.1 1.6 %collective-permute-start.21 = (f32[2,8,128]{2,1,0:T(8,128)S(1)}, f32[2,8,128]{2,1,0:T(8,128)S(1)}, u32[]{:S(2)}, u32[]{:S(2)}) collective-permute-start(f32[2,8,128]{2,1,0:T(8,128)S(1)} %add.12.refs_5_.refs_7_), channel_id=1, source_target_pairs={{0,4},{2,6},{4,8},{6,10},{8,12},{10,14},{12,0},{14,2},{1,5},{3,7},... | collective-permute-start | bytes 24584 | tf_op jit(solution)/shard_map/ppermute | solution.py:419
  55.7 2.5 %collective-permute-done.15.refs_0_ = bf16[5,256,128]{2,1,0:T(8,128)(2,1)S(1)} collective-permute-done((bf16[5,256,128]{2,1,0:T(8,128)(2,1)S(1)}, bf16[5,256,128]{2,1,0:T(8,128)(2,1)S(1)}, u32[]{:S(2)}, u32[]{:S(2)}) %collective-permute-start.15) | collective-permute-done | bytes 327712 | tf_op jit(solution)/shard_map/ppermute | solution.py:419
  58.2 0.0 collective-permute-done.22.refs_4_.refs_6_
  58.2 0.6 collective-permute-start.23
  58.8 0.0 copy-start.7
  58.8 4.3 %shard_map.115.refs_11_ = f32[9,256,256]{2,1,0:T(8,128)S(1)} custom-call(s32[3]{0:T(128)S(1)} %pad_add_fusion.flags_ref, bf16[5,256,128]{2,1,0:T(8,128)(2,1)S(1)} %get-tuple-element.35.refs_0_.refs_4_.refs_3_, bf16[3,256,128]{2,1,0:T(8,128)(2,1)S(1)} %get-tuple-element.36.refs_1_.refs_5_.refs_4_, bf16[3,256,128]{2,1,0:T(8,128)(2,1)S(1)} %get-tuple-element.37.refs_2_, ...), custom_call_target="tpu_custom_call" | custom-call | flops 2717908992 | bytes 2204672 | tf_op jit(solution)/shard_map/pallas_call | solution.py:367
  63.2 2.4 %collective-permute-done.21.refs_3_ = f32[2,8,128]{2,1,0:T(8,128)S(1)} collective-permute-done((f32[2,8,128]{2,1,0:T(8,128)S(1)}, f32[2,8,128]{2,1,0:T(8,128)S(1)}, u32[]{:S(2)}, u32[]{:S(2)}) %collective-permute-start.21) | collective-permute-done | bytes 8224 | tf_op jit(solution)/shard_map/ppermute | solution.py:419
  65.6 0.0 collective-permute-done.19.refs_2_
  65.6 0.0 collective-permute-done.18.refs_1_
  65.6 3.9 %shard_map.116 = (f32[9,256,128]{2,1,0:T(8,128)S(1)}, bf16[4,128,128]{2,1,0:T(8,128)(2,1)S(1)}, f32[8,128]{1,0:T(8,128)S(1)}, bf16[1152,128]{1,0:T(8,128)(2,1)S(1)}) custom-call(s32[3]{0:T(128)S(1)} %pad_add_fusion.flags_ref, bf16[3,256,128]{2,1,0:T(8,128)(2,1)S(1)} %collective-permute-done.17.refs_0_, ...), custom_call_target="tpu_custom_call" | custom-call | flops 1358954496 | bytes 6178816 | tf_op jit(solution)/shard_map/pallas_call | solution.py:367
  69.5 0.0 collective-permute-done.23.refs_1_
  69.6 1.6 %shard_map.117.refs_7_ = bf16[5,256,128]{2,1,0:T(8,128)(2,1)S(1)} custom-call(s32[3]{0:T(128)S(1)} %pad_add_fusion.flags_ref, bf16[5,256,128]{2,1,0:T(8,128)(2,1)S(1)} %collective-permute-done.15.refs_0_, bf16[1,2,256,128]{3,2,1,0:T(8,128)(2,1)S(1)} %collective-permute-done.23.refs_1_, f32[8,128]{1,0:T(8,128)S(1)} %get-tuple-element.41.refs_2_, ...), custom_call_target="tpu_custom_call" | custom-call | flops 754974720 | bytes 3444736 | tf_op jit(solution)/shard_map/pallas_call | solution.py:367
  71.2 0.0 collective-permute-done.16.refs_1_
  71.2 2.4 %shard_map.118 = (bf16[4,128,128]{2,1,0:T(8,128)(2,1)S(1)}, bf16[4,128,128]{2,1,0:T(8,128)(2,1)S(1)}) custom-call(s32[3]{0:T(128)S(1)} %pad_add_fusion.flags_ref, bf16[5,256,128]{2,1,0:T(8,128)(2,1)S(1)} %collective-permute-done.15.refs_0_, bf16[3,256,128]{2,1,0:T(8,128)(2,1)S(1)} %collective-permute-done.16.refs_1_, ...), custom_call_target="tpu_custom_call" | custom-call | flops 603979776 | bytes 4329984 | tf_op jit(solution)/shard_map/pallas_call | solution.py:367
  73.6 1.6 %collective-permute-start.24 = (bf16[4,128,128]{2,1,0:T(8,128)(2,1)S(1)}, bf16[4,128,128]{2,1,0:T(8,128)(2,1)S(1)}, u32[]{:S(2)}, u32[]{:S(2)}) collective-permute-start(bf16[4,128,128]{2,1,0:T(8,128)(2,1)S(1)} %get-tuple-element.46), channel_id=1, source_target_pairs={{0,2},{2,0},{4,6},{6,4},{8,10},{10,8},{12,14},{14,12},{1,3},{3,1},... | collective-permute-start | bytes 393224 | tf_op jit(solution)/shard_map/ppermute | solution.py:416
  75.2 3.7 %collective-permute-done.24 = bf16[4,128,128]{2,1,0:T(8,128)(2,1)S(1)} collective-permute-done((bf16[4,128,128]{2,1,0:T(8,128)(2,1)S(1)}, bf16[4,128,128]{2,1,0:T(8,128)(2,1)S(1)}, u32[]{:S(2)}, u32[]{:S(2)}) %collective-permute-start.24) | collective-permute-done | bytes 131104 | tf_op jit(solution)/shard_map/ppermute | solution.py:416
  78.9 0.7 maximum_select_fusion
  (27 shorter events, 0.1 us)
Async XLA Ops:
  0.0 26.7 %copy-start = (bf16[3,3,3,128,128]{4,3,2,1,0:T(8,128)(2,1)S(1)}, bf16[3,3,3,128,128]{4,3,2,1,0:T(8,128)(2,1)}, u32[]{:S(2)}) copy-start(bf16[3,3,3,128,128]{4,3,2,1,0:T(8,128)(2,1)} %refs_8_.4) | copy-start | bytes 2654212
  0.1 1.3 %copy-start.1 = (bf16[2,1,8,256,128]{4,3,2,1,0:T(8,128)(2,1)S(1)}, bf16[2,1,8,256,128]{4,3,2,1,0:T(8,128)(2,1)}, u32[]{:S(2)}) copy-start(bf16[2,1,8,256,128]{4,3,2,1,0:T(8,128)(2,1)} %param.11) | copy-start | bytes 3145732
  1.4 25.3 %copy-start.8 = (f32[128]{0:T(128)S(1)}, f32[128]{0:T(128)}, u32[]{:S(2)}) copy-start(f32[128]{0:T(128)} %param.12) | copy-start | bytes 1540
  1.4 25.3 %copy-start.9 = (f32[128]{0:T(128)S(1)}, f32[128]{0:T(128)}, u32[]{:S(2)}) copy-start(f32[128]{0:T(128)} %param.13) | copy-start | bytes 1540
  2.0 31.0 %collective-permute-start.9 = (bf16[7,256,128]{2,1,0:T(8,128)(2,1)S(1)}, bf16[7,256,128]{2,1,0:T(8,128)(2,1)S(1)}, u32[]{:S(2)}, u32[]{:S(2)}) collective-permute-start(bf16[7,256,128]{2,1,0:T(8,128)(2,1)S(1)} %get-tuple-element.27.refs_1_.refs_2_.refs_15_.refs_9_.refs_10_), channel_id=1, source_target_pairs={{0,4},{2,6},{4,8},{6,10},{8,12},{10,14},{12,0},{14,2},{1,5},{3,7},... | collective-permute-start | bytes 1376264 | tf_op jit(solution)/shard_map/ppermute | solution.py:419
  5.1 15.1 %collective-permute-start = (bf16[4,256,128]{2,1,0:T(8,128)(2,1)S(1)}, bf16[4,256,128]{2,1,0:T(8,128)(2,1)S(1)}, u32[]{:S(2)}, u32[]{:S(2)}) collective-permute-start(bf16[4,256,128]{2,1,0:T(8,128)(2,1)S(1)} %get-tuple-element.28.refs_2_), channel_id=1, source_target_pairs={{0,2},{2,0},{4,6},{6,4},{8,10},{10,8},{12,14},{14,12},{1,3},{3,1},... | collective-permute-start | bytes 786440 | tf_op jit(solution)/shard_map/ppermute | solution.py:416
  6.6 23.3 %collective-permute-start.1 = (bf16[4,256,128]{2,1,0:T(8,128)(2,1)S(1)}, bf16[4,256,128]{2,1,0:T(8,128)(2,1)S(1)}, u32[]{:S(2)}, u32[]{:S(2)}) collective-permute-start(bf16[4,256,128]{2,1,0:T(8,128)(2,1)S(1)} %get-tuple-element.29.refs_3_), channel_id=1, source_target_pairs={{0,2},{2,0},{4,6},{6,4},{8,10},{10,8},{12,14},{14,12},{1,3},{3,1},... | collective-permute-start | bytes 786440 | tf_op jit(solution)/shard_map/ppermute | solution.py:416
  8.0 1.2 %collective-permute-start.10 = (f32[2,8,128]{2,1,0:T(8,128)S(1)}, f32[2,8,128]{2,1,0:T(8,128)S(1)}, u32[]{:S(2)}, u32[]{:S(2)}) collective-permute-start(f32[2,8,128]{2,1,0:T(8,128)S(1)} %shard_map.110), channel_id=1, source_target_pairs={{0,1},{1,0},{2,3},{3,2},{4,5},{5,4},{6,7},{7,6},{8,9},{9,8},{10,11... | collective-permute-start | bytes 24584 | tf_op jit(solution)/shard_map/ppermute | solution.py:425
  9.2 9.5 %collective-permute-start.11 = (f32[2,8,128]{2,1,0:T(8,128)S(1)}, f32[2,8,128]{2,1,0:T(8,128)S(1)}, u32[]{:S(2)}, u32[]{:S(2)}) collective-permute-start(f32[2,8,128]{2,1,0:T(8,128)S(1)} %add.11.refs_3_.refs_9_), channel_id=1, source_target_pairs={{0,2},{2,0},{4,6},{6,4},{8,10},{10,8},{12,14},{14,12},{1,3},{3,1},... | collective-permute-start | bytes 24584 | tf_op jit(solution)/shard_map/ppermute | solution.py:416
  10.7 9.5 %collective-permute-start.12 = (f32[2,8,128]{2,1,0:T(8,128)S(1)}, f32[2,8,128]{2,1,0:T(8,128)S(1)}, u32[]{:S(2)}, u32[]{:S(2)}) collective-permute-start(f32[2,8,128]{2,1,0:T(8,128)S(1)} %add.11.refs_3_.refs_9_), channel_id=1, source_target_pairs={{0,4},{2,6},{4,8},{6,10},{8,12},{10,14},{12,0},{14,2},{1,5},{3,7},... | collective-permute-start | bytes 24584 | tf_op jit(solution)/shard_map/ppermute | solution.py:419
  18.7 6.1 %collective-permute-start.7 = (bf16[1,256,128]{2,1,0:T(8,128)(2,1)S(1)}, bf16[1,256,128]{2,1,0:T(8,128)(2,1)S(1)}, u32[]{:S(2)}, u32[]{:S(2)}) collective-permute-start(bf16[1,256,128]{2,1,0:T(8,128)(2,1)S(1)} %get-tuple-element.26.refs_0_.refs_1_.refs_14_.refs_8_.refs_9_), channel_id=1, source_target_pairs={{0,4},{2,6},{4,8},{6,10},{8,12},{10,14},{12,0},{14,2},{1,5},{3,7},... | collective-permute-start | bytes 196616 | tf_op jit(solution)/shard_map/ppermute | solution.py:419
  20.2 6.4 %collective-permute-start.5 = (bf16[1,256,128]{2,1,0:T(8,128)(2,1)S(1)}, bf16[1,256,128]{2,1,0:T(8,128)(2,1)S(1)}, u32[]{:S(2)}, u32[]{:S(2)}) collective-permute-start(bf16[1,256,128]{2,1,0:T(8,128)(2,1)S(1)} %get-tuple-element.26.refs_0_.refs_1_.refs_14_.refs_8_.refs_9_), channel_id=1, source_target_pairs={{0,1},{1,0},{2,3},{3,2},{4,5},{5,4},{6,7},{7,6},{8,9},{9,8},{10,11... | collective-permute-start | bytes 196616 | tf_op jit(solution)/shard_map/ppermute | solution.py:425
  20.3 6.4 %collective-permute-start.13 = (f32[2,8,128]{2,1,0:T(8,128)S(1)}, f32[2,8,128]{2,1,0:T(8,128)S(1)}, u32[]{:S(2)}, u32[]{:S(2)}) collective-permute-start(f32[2,8,128]{2,1,0:T(8,128)S(1)} %add.11.refs_3_.refs_9_), channel_id=1, source_target_pairs={{0,6},{2,4},{4,10},{6,8},{8,14},{10,12},{12,2},{14,0},{1,7},{3,5},... | collective-permute-start | bytes 24584 | tf_op jit(solution)/shard_map/ppermute | solution.py:422
  24.7 4.7 %collective-permute-start.8 = (bf16[1,256,128]{2,1,0:T(8,128)(2,1)S(1)}, bf16[1,256,128]{2,1,0:T(8,128)(2,1)S(1)}, u32[]{:S(2)}, u32[]{:S(2)}) collective-permute-start(bf16[1,256,128]{2,1,0:T(8,128)(2,1)S(1)} %collective-permute-done.7.refs_7_), channel_id=1, source_target_pairs={{0,1},{1,0},{2,3},{3,2},{4,5},{5,4},{6,7},{7,6},{8,9},{9,8},{10,11... | collective-permute-start | bytes 196616 | tf_op jit(solution)/shard_map/ppermute | solution.py:425
  26.7 6.3 %collective-permute-start.6 = (bf16[1,256,128]{2,1,0:T(8,128)(2,1)S(1)}, bf16[1,256,128]{2,1,0:T(8,128)(2,1)S(1)}, u32[]{:S(2)}, u32[]{:S(2)}) collective-permute-start(bf16[1,256,128]{2,1,0:T(8,128)(2,1)S(1)} %slice.17), channel_id=1, source_target_pairs={{0,1},{1,0},{2,3},{3,2},{4,5},{5,4},{6,7},{7,6},{8,9},{9,8},{10,11... | collective-permute-start | bytes 196616 | tf_op jit(solution)/shard_map/ppermute | solution.py:425
  26.7 6.3 %collective-permute-start.2 = (bf16[1,256,128]{2,1,0:T(8,128)(2,1)S(1)}, bf16[1,256,128]{2,1,0:T(8,128)(2,1)S(1)}, u32[]{:S(2)}, u32[]{:S(2)}) collective-permute-start(bf16[1,256,128]{2,1,0:T(8,128)(2,1)S(1)} %slice.17), channel_id=1, source_target_pairs={{0,4},{2,6},{4,8},{6,10},{8,12},{10,14},{12,0},{14,2},{1,5},{3,7},... | collective-permute-start | bytes 196616 | tf_op jit(solution)/shard_map/ppermute | solution.py:419
  29.4 9.6 %copy-start.4 = (f32[128]{0:T(128)S(1)}, f32[128]{0:T(128)}, u32[]{:S(2)}) copy-start(f32[128]{0:T(128)} %param.15) | copy-start | bytes 1540
  29.4 9.6 %collective-permute-start.3 = (bf16[3,256,128]{2,1,0:T(8,128)(2,1)S(1)}, bf16[3,256,128]{2,1,0:T(8,128)(2,1)S(1)}, u32[]{:S(2)}, u32[]{:S(2)}) collective-permute-start(bf16[3,256,128]{2,1,0:T(8,128)(2,1)S(1)} %slice.18), channel_id=1, source_target_pairs={{0,4},{2,6},{4,8},{6,10},{8,12},{10,14},{12,0},{14,2},{1,5},{3,7},... | collective-permute-start | bytes 589832 | tf_op jit(solution)/shard_map/ppermute | solution.py:419
  29.9 14.3 %collective-permute-start.4 = (bf16[4,256,128]{2,1,0:T(8,128)(2,1)S(1)}, bf16[4,256,128]{2,1,0:T(8,128)(2,1)S(1)}, u32[]{:S(2)}, u32[]{:S(2)}) collective-permute-start(bf16[4,256,128]{2,1,0:T(8,128)(2,1)S(1)} %collective-permute-done.1.refs_5_.refs_3_.refs_18_.refs_12_), channel_id=1, source_target_pairs={{0,4},{2,6},{4,8},{6,10},{8,12},{10,14},{12,0},{14,2},{1,5},{3,7},... | collective-permute-start | bytes 786440 | tf_op jit(solution)/shard_map/ppermute | solution.py:419
  33.0 4.3 %collective-permute-start.14 = (bf16[1,256,128]{2,1,0:T(8,128)(2,1)S(1)}, bf16[1,256,128]{2,1,0:T(8,128)(2,1)S(1)}, u32[]{:S(2)}, u32[]{:S(2)}) collective-permute-start(bf16[1,256,128]{2,1,0:T(8,128)(2,1)S(1)} %collective-permute-done.2.refs_5_.refs_4_), channel_id=1, source_target_pairs={{0,1},{1,0},{2,3},{3,2},{4,5},{5,4},{6,7},{7,6},{8,9},{9,8},{10,11... | collective-permute-start | bytes 196616 | tf_op jit(solution)/shard_map/ppermute | solution.py:425
  40.6 13.5 %collective-permute-start.17 = (bf16[3,256,128]{2,1,0:T(8,128)(2,1)S(1)}, bf16[3,256,128]{2,1,0:T(8,128)(2,1)S(1)}, u32[]{:S(2)}, u32[]{:S(2)}) collective-permute-start(bf16[3,256,128]{2,1,0:T(8,128)(2,1)S(1)} %get-tuple-element.37.refs_2_), channel_id=1, source_target_pairs={{0,4},{2,6},{4,8},{6,10},{8,12},{10,14},{12,0},{14,2},{1,5},{3,7},... | collective-permute-start | bytes 589832 | tf_op jit(solution)/shard_map/ppermute | solution.py:419
  44.2 2.1 %copy-start.10 = (bf16[3,3,128,128]{3,2,1,0:T(8,128)(2,1)S(1)}, bf16[3,3,128,128]{3,2,1,0:T(8,128)(2,1)}, u32[]{:S(2)}) copy-start(bf16[3,3,128,128]{3,2,1,0:T(8,128)(2,1)} %param.20) | copy-start | bytes 884740
  44.2 14.6 %copy-start.2 = (bf16[3,3,3,128,128]{4,3,2,1,0:T(8,128)(2,1)S(1)}, bf16[3,3,3,128,128]{4,3,2,1,0:T(8,128)(2,1)}, u32[]{:S(2)}) copy-start(bf16[3,3,3,128,128]{4,3,2,1,0:T(8,128)(2,1)} %refs_10_.1) | copy-start | bytes 2654212
  44.2 14.6 %copy-start.5 = (f32[128]{0:T(128)S(1)}, f32[128]{0:T(128)}, u32[]{:S(2)}) copy-start(f32[128]{0:T(128)} %param.16) | copy-start | bytes 1540
  44.2 14.6 %copy-start.6 = (f32[128]{0:T(128)S(1)}, f32[128]{0:T(128)}, u32[]{:S(2)}) copy-start(f32[128]{0:T(128)} %param.17) | copy-start | bytes 1540
  46.2 3.4 %collective-permute-start.20 = (f32[2,8,128]{2,1,0:T(8,128)S(1)}, f32[2,8,128]{2,1,0:T(8,128)S(1)}, u32[]{:S(2)}, u32[]{:S(2)}) collective-permute-start(f32[2,8,128]{2,1,0:T(8,128)S(1)} %get-tuple-element.39), channel_id=1, source_target_pairs={{0,1},{1,0},{2,3},{3,2},{4,5},{5,4},{6,7},{7,6},{8,9},{9,8},{10,11... | collective-permute-start | bytes 24584 | tf_op jit(solution)/shard_map/ppermute | solution.py:425
  46.3 11.9 %collective-permute-start.15 = (bf16[5,256,128]{2,1,0:T(8,128)(2,1)S(1)}, bf16[5,256,128]{2,1,0:T(8,128)(2,1)S(1)}, u32[]{:S(2)}, u32[]{:S(2)}) collective-permute-start(bf16[5,256,128]{2,1,0:T(8,128)(2,1)S(1)} %get-tuple-element.35.refs_0_.refs_4_.refs_3_), channel_id=1, source_target_pairs={{0,4},{2,6},{4,8},{6,10},{8,12},{10,14},{12,0},{14,2},{1,5},{3,7},... | collective-permute-start | bytes 983048 | tf_op jit(solution)/shard_map/ppermute | solution.py:419
  46.4 11.8 %collective-permute-start.22 = (bf16[2,2,256,128]{3,2,1,0:T(8,128)(2,1)S(1)}, bf16[2,2,256,128]{3,2,1,0:T(8,128)(2,1)S(1)}, u32[]{:S(2)}, u32[]{:S(2)}) collective-permute-start(bf16[2,2,256,128]{3,2,1,0:T(8,128)(2,1)S(1)} %get-tuple-element.40), channel_id=1, source_target_pairs={{0,1},{1,0},{2,3},{3,2},{4,5},{5,4},{6,7},{7,6},{8,9},{9,8},{10,11... | collective-permute-start | bytes 786440 | tf_op jit(solution)/shard_map/ppermute | solution.py:425
  46.9 18.7 %collective-permute-start.18 = (bf16[5,256,128]{2,1,0:T(8,128)(2,1)S(1)}, bf16[5,256,128]{2,1,0:T(8,128)(2,1)S(1)}, u32[]{:S(2)}, u32[]{:S(2)}) collective-permute-start(bf16[5,256,128]{2,1,0:T(8,128)(2,1)S(1)} %get-tuple-element.38.refs_3_), channel_id=1, source_target_pairs={{0,4},{2,6},{4,8},{6,10},{8,12},{10,14},{1,5},{3,7},{5,9},{7,11},{... | collective-permute-start | bytes 983048 | tf_op jit(solution)/shard_map/ppermute | solution.py:419
  49.6 21.6 %collective-permute-start.16 = (bf16[3,256,128]{2,1,0:T(8,128)(2,1)S(1)}, bf16[3,256,128]{2,1,0:T(8,128)(2,1)S(1)}, u32[]{:S(2)}, u32[]{:S(2)}) collective-permute-start(bf16[3,256,128]{2,1,0:T(8,128)(2,1)S(1)} %get-tuple-element.36.refs_1_.refs_5_.refs_4_), channel_id=1, source_target_pairs={{0,4},{2,6},{4,8},{6,10},{8,12},{10,14},{1,5},{3,7},{5,9},{7,11},{... | collective-permute-start | bytes 589832 | tf_op jit(solution)/shard_map/ppermute | solution.py:419
  54.1 11.5 %collective-permute-start.21 = (f32[2,8,128]{2,1,0:T(8,128)S(1)}, f32[2,8,128]{2,1,0:T(8,128)S(1)}, u32[]{:S(2)}, u32[]{:S(2)}) collective-permute-start(f32[2,8,128]{2,1,0:T(8,128)S(1)} %add.12.refs_5_.refs_7_), channel_id=1, source_target_pairs={{0,4},{2,6},{4,8},{6,10},{8,12},{10,14},{12,0},{14,2},{1,5},{3,7},... | collective-permute-start | bytes 24584 | tf_op jit(solution)/shard_map/ppermute | solution.py:419
  58.2 7.4 %collective-permute-start.19 = (bf16[1,2,256,128]{3,2,1,0:T(8,128)(2,1)S(1)}, bf16[1,2,256,128]{3,2,1,0:T(8,128)(2,1)S(1)}, u32[]{:S(2)}, u32[]{:S(2)}) collective-permute-start(bf16[1,2,256,128]{3,2,1,0:T(8,128)(2,1)S(1)} %slice_bitcast_fusion.1), channel_id=1, source_target_pairs={{0,1},{1,0},{2,3},{3,2},{4,5},{5,4},{6,7},{7,6},{8,9},{9,8},{10,11... | collective-permute-start | bytes 393224 | tf_op jit(solution)/shard_map/ppermute | solution.py:425
  58.2 11.3 %collective-permute-start.23 = (bf16[1,2,256,128]{3,2,1,0:T(8,128)(2,1)S(1)}, bf16[1,2,256,128]{3,2,1,0:T(8,128)(2,1)S(1)}, u32[]{:S(2)}, u32[]{:S(2)}) collective-permute-start(bf16[1,2,256,128]{3,2,1,0:T(8,128)(2,1)S(1)} %slice_bitcast_fusion), channel_id=1, source_target_pairs={{0,1},{1,0},{2,3},{3,2},{4,5},{5,4},{6,7},{7,6},{8,9},{9,8},{10,11... | collective-permute-start | bytes 393224 | tf_op jit(solution)/shard_map/ppermute | solution.py:425
  58.8 6.8 %copy-start.3 = (f32[128]{0:T(128)S(1)}, f32[128]{0:T(128)}, u32[]{:S(2)}) copy-start(f32[128]{0:T(128)} %param.21) | copy-start | bytes 1540
  58.8 6.8 %copy-start.7 = (f32[128]{0:T(128)S(1)}, f32[128]{0:T(128)}, u32[]{:S(2)}) copy-start(f32[128]{0:T(128)} %param.19) | copy-start | bytes 1540
  73.6 5.3 %collective-permute-start.24 = (bf16[4,128,128]{2,1,0:T(8,128)(2,1)S(1)}, bf16[4,128,128]{2,1,0:T(8,128)(2,1)S(1)}, u32[]{:S(2)}, u32[]{:S(2)}) collective-permute-start(bf16[4,128,128]{2,1,0:T(8,128)(2,1)S(1)} %get-tuple-element.46), channel_id=1, source_target_pairs={{0,2},{2,0},{4,6},{6,4},{8,10},{10,8},{12,14},{14,12},{1,3},{3,1},... | collective-permute-start | bytes 393224 | tf_op jit(solution)/shard_map/ppermute | solution.py:416
